TPU v7x, 32 devices: a whole 2x2x4 slice. The times are simulated.
32 devices in a mesh: dp: 16 (over z, x, core), mp: 2 (over y).
Axes of the slice: x: 2, y: 2, z: 4, core: 2. Of those that a mesh axis runs over, the one named last changes fastest.
Arguments:
- activations: bfloat16 [256, 9216], P('mp', 'dp'), may hold values from -6 to 6
- block_values: bfloat16 [384, 20, 128, 128], P('dp'), may hold values from -0.125 to 0.125
- block_rows: int32 [384, 20], P('dp'), may hold values from 0 to 71, all different within a row
- cotangent: bfloat16 [256, 49152], P('mp', 'dp'), may hold values from -6 to 6
Outputs:
- gelu_out: bfloat16 [256, 49152], P('mp', 'dp')
- input_grad: bfloat16 [256, 9216], P('mp', 'dp')
- block_grad: float32 [384, 20, 128, 128], P('dp', 'mp')
Inputs may be any that keep to these rules, and one draw needn't show every extreme that they name: `block_rows`: the 20 entries of each column block are different block rows; every block row is named somewhere.
All inputs are finite; a program needn't handle non-finite values.
Results may differ from a plain program's by a relative error of at most 0.0049.
Values may be sent and summed in bfloat16 or wider, within the bound.
No kernel may reach another device: no remote copies, remote signals or barrier semaphores. Data moves between devices by JAX's collectives and lax.ppermute only.
A program may use at most 128 MiB of HBM per device.

v0:
```python
import jax
import jax.numpy as jnp
from jax import lax
from jax.sharding import PartitionSpec as P


def gelu_tanh(values):
    return jax.nn.gelu(values, approximate=True)


def body(activations, block_values, block_rows, cotangent):
    rows_here = activations.shape[0]
    col_blocks = block_values.shape[0]
    slot_count = block_values.shape[1]
    block_size = block_values.shape[2]
    total_slots = col_blocks * slot_count
    x_full = lax.all_gather(activations, "dp", axis=1, tiled=True)
    row_blocks = x_full.shape[1] // block_size
    rows_flat = block_rows.reshape(-1)
    picked_rows = jnp.take(x_full.reshape(rows_here, row_blocks, block_size), rows_flat, axis=1)
    picked_rows = picked_rows.reshape(rows_here, col_blocks, slot_count, block_size)
    pre_act = jnp.einsum(
        "tcki,ckij->tcj", picked_rows, block_values, preferred_element_type=jnp.float32
    )
    gelu_out = gelu_tanh(pre_act).astype(jnp.bfloat16).reshape(rows_here, col_blocks * block_size)
    unused, pull_back = jax.vjp(gelu_tanh, pre_act)
    cot_blocks = cotangent.reshape(rows_here, col_blocks, block_size).astype(jnp.float32)
    slopes = pull_back(cot_blocks)[0].astype(jnp.bfloat16)
    contrib = jnp.einsum("tcj,ckij->tcki", slopes, block_values, preferred_element_type=jnp.float32)
    contrib = contrib.reshape(rows_here, total_slots, block_size)
    one_hot = (rows_flat[:, None] == jnp.arange(row_blocks, dtype=jnp.int32)[None, :]).astype(
        jnp.float32
    )
    dx_term = jnp.einsum("tmi,mr->tri", contrib, one_hot, precision=lax.Precision.HIGHEST)
    dx_term = dx_term.reshape(rows_here, row_blocks * block_size)
    input_grad = lax.psum_scatter(dx_term, "dp", scatter_dimension=1, tiled=True).astype(
        jnp.bfloat16
    )
    mp_size = lax.axis_size("mp")
    per_peer = slot_count // mp_size
    outgoing = picked_rows.reshape(rows_here, col_blocks, mp_size, per_peer, block_size)
    outgoing = jnp.transpose(outgoing, (2, 0, 1, 3, 4)).reshape(
        mp_size, rows_here, col_blocks * per_peer * block_size
    )
    incoming = lax.all_to_all(outgoing, "mp", split_axis=0, concat_axis=0, tiled=True)
    own_cols = incoming.reshape(mp_size * rows_here, col_blocks, per_peer, block_size)
    slope_rows = lax.all_gather(
        slopes.reshape(rows_here, col_blocks * block_size), "mp", axis=0, tiled=True
    )
    slope_rows = slope_rows.reshape(mp_size * rows_here, col_blocks, block_size)
    block_grad = jnp.einsum(
        "tcki,tcj->ckij", own_cols, slope_rows, preferred_element_type=jnp.float32
    )
    return (gelu_out, input_grad, block_grad)


def solution(mesh):
    in_specs = (P("mp", "dp"), P("dp", None, None, None), P("dp", None), P("mp", "dp"))
    out_specs = (P("mp", "dp"), P("mp", "dp"), P("dp", "mp", None, None))
    return jax.shard_map(body, mesh=mesh, in_specs=in_specs, out_specs=out_specs, check_vma=False)
```

profile of v0, /device:TPU:0, one launch (start us, length us, event | category | flops | bytes accessed | tf_op | source)
XLA Modules:
  0.0 457.7 jit_solution(4548735737464194865)
XLA Ops:
  7.2 0.0 all-gather.3.cloned.1.call-start
  7.2 0.7 all-gather.3.cloned.1.call-update
  7.9 0.0 reduce-scatter.2.cloned.1.call-start
  7.9 0.8 reshape.82
  8.8 0.8 reshape.84
  9.6 0.8 copy.65
  10.4 0.1 copy.66
  10.5 2.5 copy.61
  13.0 0.7 compare_and_fusion.1
  13.8 41.6 %all-gather.3.cloned.1.call-done = bf16[128,9216]{0,1:T(8,128)(2,1)} async-done(((bf16[128,576]{0,1:T(8,128)(2,1)}), bf16[128,9216]{0,1:T(8,128)(2,1)}) %all-gather.3.cloned.1.call-update) | async-done | bytes 2359312 | tf_op jit(solution)/shard_map/all_gather | solution.py:17
  55.3 3.0 copy.59
  58.4 13.7 %gather_fusion = bf16[480,128,128]{2,1,0:T(8,128)(2,1)} fusion(bf16[128,72,128]{2,0,1:T(8,128)(2,1)S(1)} %copy.59, s32[1024]{0:T(1024)S(1)} %pad_clamp_fusion), kind=kCustom, calls=%fused_computation | custom fusion | bytes 31459200 | tf_op jit(solution)/shard_map/jit(_take)/gather | solution.py:20
  72.1 12.9 %fusion.15 = (bf16[128,24,128]{0,2,1:T(8,128)(2,1)S(1)}, bf16[128,24,128]{0,2,1:T(8,128)(2,1)S(1)}) fusion(f32[128,24,128]{0,2,1:T(8,128)} %bitcast.68, bf16[24,20,128,128]{3,2,1,0:T(8,128)(2,1)} %param.5, bf16[128,24,20,128]{3,0,2,1:T(8,128)(2,1)} %bitcast.61, pred[24,20]{1,0:T(8,128)(4,1)S(1)} %compare_and_fusion.1), kind=kOutput, calls=%fused_computation.17 | convolution fusion | flops 2029780992 | bytes 34603488 | tf_op jit(solution)/shard_map/tcki,ckij->tcj/dot_general | solution.py:22
  85.0 0.0 copy-start
  85.0 16.3 %fusion.19 = f32[24,128,20,128]{3,1,2,0:T(8,128)} fusion(bf16[24,20,128,128]{3,2,1,0:T(8,128)(2,1)} %param.5, bf16[128,24,128]{0,2,1:T(8,128)(2,1)S(1)} %get-tuple-element.21), kind=kOutput, calls=%fused_computation.23 | convolution fusion | flops 2013265920 | bytes 47972352 | tf_op jit(solution)/shard_map/tcj,ckij->tcki/dot_general | solution.py:29
  101.3 0.0 copy-done
  101.3 40.7 %fusion.6 = f32[128,72,128]{2,1,0:T(8,128)} fusion(f32[128,480,128]{2,0,1:T(8,128)} %bitcast.60, s32[480]{0:T(512)S(1)} %reshape.84), kind=kOutput, calls=%fused_computation.8 | convolution fusion | flops 6794807296 | bytes 36177792 | tf_op jit(solution)/shard_map/tmi,mr->tri/dot_general | solution.py:34
  142.0 6.1 %copy.77 = f32[128,72,128]{0,2,1:T(8,128)} copy(f32[128,72,128]{2,1,0:T(8,128)} %fusion.6) | data formatting | bytes 9437184 | tf_op jit(solution)/shard_map/reshape | solution.py:35
  148.1 0.0 reduce-scatter.2.cloned.1.call-update
  148.1 13.9 %select_bitcast_fusion = bf16[2,128,24,10,128]{4,1,3,0,2:T(8,128)(2,1)} fusion(bf16[128,24,2,10,128]{4,0,3,2,1:T(8,128)(2,1)} %bitcast.62, pred[24,2,10]{2,1,0:T(4,128)(4,1)S(1)} %copy.66), kind=kLoop, calls=%fused_computation.3 | loop fusion | flops 7864320 | bytes 31457760 | tf_op jit(solution)/shard_map/transpose | solution.py:42
  162.0 21.1 %copy.67 = bf16[2,128,24,10,128]{1,4,3,2,0:T(8,128)(2,1)} copy(bf16[2,128,24,10,128]{4,1,3,0,2:T(8,128)(2,1)} %select_bitcast_fusion) | data formatting | bytes 31457280 | tf_op jit(solution)/shard_map/transpose | solution.py:42
  183.1 9.4 %all-to-all-start = ((bf16[2,128,30720]{1,2,0:T(8,128)(2,1)}), bf16[2,128,30720]{1,2,0:T(8,128)(2,1)}, u32[]{:S(2)}, u32[]{:S(2)}) async-start(bf16[2,128,30720]{1,2,0:T(8,128)(2,1)} %bitcast.63), calls=%async_computation.1 | async-start | bytes 31457280 | tf_op jit(solution)/shard_map/all_to_all | solution.py:45
  192.5 0.0 all-gather.5.cloned.1.call-start
  192.5 0.7 all-gather.5.cloned.1.call-update
  193.2 1.2 copy.70
  194.4 28.2 %reduce-scatter.2.cloned.1.call-done = f32[128,576]{0,1:T(8,128)} async-done(((f32[128,9216]{0,1:T(8,128)}), f32[128,576]{0,1:T(8,128)}) %reduce-scatter.2.cloned.1.call-update) | async-done | bytes 294928 | tf_op jit(solution)/shard_map/reduce_scatter | solution.py:36
  222.6 1.6 convert_element_type.20
  224.2 156.6 %all-to-all-done = bf16[2,128,30720]{1,2,0:T(8,128)(2,1)} async-done(((bf16[2,128,30720]{1,2,0:T(8,128)(2,1)}), bf16[2,128,30720]{1,2,0:T(8,128)(2,1)}, u32[]{:S(2)}, u32[]{:S(2)}) %all-to-all-start) | async-done | bytes 15728672 | tf_op jit(solution)/shard_map/all_to_all | solution.py:45
  380.8 29.1 %copy.68 = bf16[2,128,30720]{1,0,2:T(2,128)(2,1)} copy(bf16[2,128,30720]{1,2,0:T(8,128)(2,1)} %all-to-all-done) | data formatting | bytes 31457280 | tf_op jit(solution)/shard_map/all_to_all | solution.py:45
  409.9 25.3 %reshape.89 = bf16[256,24,10,128]{0,3,2,1:T(8,128)(2,1)} reshape(bf16[2,128,30720]{1,0,2:T(2,128)(2,1)} %copy.68) | data formatting | bytes 31457280 | tf_op jit(solution)/shard_map/reshape | solution.py:46
  435.2 0.0 all-gather.5.cloned.1.call-done
  435.2 16.0 %fusion.25 = f32[24,10,128,128]{3,2,1,0:T(8,128)} fusion(bf16[256,24,10,128]{0,3,2,1:T(8,128)(2,1)} %reshape.89, bf16[256,24,128,1]{0,2,3,1:T(8,128)(2,1)} %bitcast.65), kind=kOutput, calls=%fused_computation.35 | convolution fusion | flops 2013265920 | bytes 33030144 | tf_op jit(solution)/shard_map/tcki,tcj->ckij/dot_general | solution.py:51
  (4 shorter events, 0.0 us)
Async XLA Ops:
  7.2 48.2 %all-gather.3.cloned.1.call-start = ((), (), s32[]{:S(2)}) async-start(), calls=%async_computation.2 | async-start | bytes 2506752 | tf_op jit(solution)/shard_map/all_gather | solution.py:17
  7.9 214.7 %reduce-scatter.2.cloned.1.call-start = ((), (), s32[]{:S(2)}) async-start(), calls=%async_computation.3 | async-start | bytes 5013504 | tf_op jit(solution)/shard_map/reduce_scatter | solution.py:36
  85.0 16.3 %copy-start = (bf16[128,24,128]{0,2,1:T(8,128)(2,1)}, bf16[128,24,128]{0,2,1:T(8,128)(2,1)S(1)}, u32[]{:S(2)}) copy-start(bf16[128,24,128]{0,2,1:T(8,128)(2,1)S(1)} %get-tuple-element.21) | copy-start | bytes 2359300
  183.1 197.7 %all-to-all-start = ((bf16[2,128,30720]{1,2,0:T(8,128)(2,1)}), bf16[2,128,30720]{1,2,0:T(8,128)(2,1)}, u32[]{:S(2)}, u32[]{:S(2)}) async-start(bf16[2,128,30720]{1,2,0:T(8,128)(2,1)} %bitcast.63), calls=%async_computation.1 | async-start | bytes 31457280 | tf_op jit(solution)/shard_map/all_to_all | solution.py:45
  192.5 242.7 %all-gather.5.cloned.1.call-start = ((), (), s32[]{:S(2)}) async-start(), calls=%async_computation.4 | async-start | bytes 2359296 | tf_op jit(solution)/shard_map/all_gather | solution.py:47
Sparse Core Ops, SparseCore 0:
  10.3 45.0 all-gather.2
  148.3 74.2 reduce-scatter.1
  224.1 43.3 all-gather.4
where the time goes:
time: 460 us; the launch traced here: 458 us
  waiting for transfers between devices  228 us (50%)
  local copies, waits for them, and re-layouts  105 us (23%)
  matrix products  85.8 us (19%)
  other arithmetic  16.3 us (4%)
  between operations  13.8 us (3%)
  starting transfers between devices  9.49 us (2%)
    all_to_all x1, waiting for transfers between devices, body(): lax.all_to_all(outgoing, 'mp', split_axis=0, concat_axis=0, tiled=True)  157 us
    all_gather x1, waiting for transfers between devices, body(): x_full = lax.all_gather(activations, 'dp', axis=1, tiled=True)  41.6 us
    dot_general x1, matrix products, body(): jnp.einsum('tmi,mr->tri', contrib, one_hot, precision=lax.Precision.HIGHEST)  40.7 us
    all_to_all x1, local copies, waits for them, and re-layouts, body(): lax.all_to_all(outgoing, 'mp', split_axis=0, concat_axis=0, tiled=True)  29.1 us
    reduce_scatter x1, waiting for transfers between devices, body(): lax.psum_scatter(dx_term, 'dp', scatter_dimension=1, tiled=True)  28.2 us
    reshape x1, local copies, waits for them, and re-layouts, body(): incoming.reshape(mp_size * rows_here, col_blocks, per_peer, block_size)  25.3 us
    transpose x1, local copies, waits for them, and re-layouts, body(): jnp.transpose(outgoing, (2, 0, 1, 3, 4))  21.1 us
    dot_general x1, matrix products, body(): jnp.einsum('tcj,ckij->tcki', slopes, block_values, preferred_element_type...  16.3 us
  transfers between devices with their start and end apart: 4, of which 3 were waited for; matrix products, arithmetic and copies ran while one was open for 21% of the time, Pallas kernels for 0%

commit v1 on v0

v1 whole, which is shorter than its diff:
```python
import functools

import jax
import jax.numpy as jnp
import numpy as np
from jax import lax
from jax.experimental import pallas as pl
from jax.experimental.pallas import tpu as pltpu
from jax.sharding import PartitionSpec as P

CORES = 2
SIDES = 2
MAX_LINE = 8


SQRT_2_PI = float(np.sqrt(2.0 / np.pi))
CUBIC = 0.044715


def forward_kernel(n_in, groups, sets, rows_s, offs_s, *refs):
    x_refs, refs = refs[:n_in], refs[n_in:]
    w_ref, cot_ref, gelu_ref, slope_ref = refs[:4]
    dx_refs, refs = refs[4 : 4 + len(groups)], refs[4 + len(groups) :]
    xt, xs, acc, w, cot, gelu, slopes, x_sem, w_sem, cot_sem, out_sem, dx_sem = refs
    cols, slots, side, _ = w.shape
    blocks = xs.shape[0]

    def shard(j):
        rows = x_refs[j].shape[0]
        target = xt.at[pl.ds(pl.multiple_of(offs_s[j], 16), rows), :]
        return pltpu.make_async_copy(x_refs[j], target, x_sem.at[j])

    def weights(c):
        return pltpu.make_async_copy(w_ref.at[c], w.at[c], w_sem.at[c])

    def outs(c):
        return (
            pltpu.make_async_copy(gelu.at[c], gelu_ref.at[:, column(c)], out_sem.at[0, c]),
            pltpu.make_async_copy(slopes.at[c], slope_ref.at[:, column(c)], out_sem.at[1, c]),
        )

    def column(c):
        return pl.ds(pl.multiple_of(c * side, side), side)

    def block(r):
        return pl.ds(pl.multiple_of(r * side, side), side)

    for j in range(n_in):
        shard(j).start()
    cotangent = pltpu.make_async_copy(cot_ref, cot, cot_sem)
    cotangent.start()

    def load(c, carry):
        weights(c).start()
        return carry

    def clear(r, carry):
        acc[r] = jnp.zeros(acc.shape[1:], acc.dtype)
        return carry

    lax.fori_loop(0, blocks, clear, 0)
    for j in range(n_in):
        shard(j).wait()
    lax.fori_loop(0, cols, load, 0)

    def turn(r, carry):
        xs[r] = xt[block(r), :].T
        return carry

    lax.fori_loop(0, blocks, turn, 0, unroll=4)
    cotangent.wait()

    def ahead(c):
        row = [rows_s[c, k] for k in range(slots)]
        v = 0.0
        for k in range(0, slots, 2):
            v = v + jnp.dot(
                jnp.concatenate([xs[r] for r in row[k : k + 2]], axis=1),
                w[c, k : k + 2].reshape(2 * side, side),
                preferred_element_type=jnp.float32,
            )
        v2 = v * v
        t = jnp.tanh(SQRT_2_PI * (v + CUBIC * (v * v2)))
        half = 0.5 * (1.0 + t)
        gelu[c] = (v * half).astype(gelu.dtype)
        slope = half + (0.5 * v) * (1.0 - t * t) * (SQRT_2_PI * (1.0 + (3.0 * CUBIC) * v2))
        slopes[c] = (cot[:, column(c)].astype(jnp.float32) * slope).astype(slopes.dtype)

    def back(c):
        turned = slopes[c].T
        step = 2 if slots % 2 == 0 else 1
        for k in range(0, slots, step):
            part = jnp.dot(
                w[c, k : k + step].reshape(step * side, side),
                turned,
                preferred_element_type=jnp.float32,
            )
            for i in range(step):
                acc[rows_s[c, k + i]] += part[i * side : (i + 1) * side, :]

    def send(c):
        for copy in outs(c):
            copy.start()

    def one(c, carry):
        weights(c + 1).wait()
        send(c)
        ahead(c + 1)
        back(c)
        return carry

    weights(0).wait()
    ahead(0)
    lax.fori_loop(0, cols - 1, one, 0)
    send(cols - 1)
    back(cols - 1)

    def results(members):
        for j in members:
            g = next(i for i, m in enumerate(groups) if j in m)
            rows = dx_refs[g].shape[0] // len(groups[g])
            i = groups[g].index(j)
            source = xt.at[pl.ds(pl.multiple_of(offs_s[j], 16), rows), :]
            yield pltpu.make_async_copy(
                source, dx_refs[g].at[i * rows : (i + 1) * rows, :], dx_sem.at[j]
            )

    per_set = blocks // len(sets)
    for members in sets:
        first = offs_s[members[0]]
        for j in members[1:]:
            first = jnp.minimum(first, offs_s[j])
        first = first // side

        def turn_back(i, carry):
            r = first + i
            xt[block(r), :] = acc[r].astype(xt.dtype)
            return carry

        lax.fori_loop(0, per_set, turn_back, 0, unroll=3)
        for copy in results(members):
            copy.start()

    def drain(c, carry):
        for copy in outs(c):
            copy.wait()
        return carry

    lax.fori_loop(0, cols, drain, 0)
    for members in sets:
        for copy in results(members):
            copy.wait()


def anywhere(count):
    return [pl.BlockSpec(memory_space=pl.ANY)] * count


def forward(shards, offs, weights, rows, cot, groups, sets):
    cols, slots, side, _ = weights.shape
    tokens = shards[0].shape[1]
    features = sum(s.shape[0] for s in shards)
    blocks = features // side
    part = shards[0].shape[0]
    flops = 4 * tokens * cols * slots * side * side
    dma = pltpu.SemaphoreType.DMA
    return pl.pallas_call(
        functools.partial(forward_kernel, len(shards), groups, sets),
        grid_spec=pltpu.PrefetchScalarGridSpec(
            num_scalar_prefetch=2,
            in_specs=anywhere(len(shards) + 2),
            out_specs=anywhere(2 + len(groups)),
            scratch_shapes=[
                pltpu.VMEM((features, tokens), jnp.bfloat16),
                pltpu.VMEM((blocks, tokens, side), jnp.bfloat16),
                pltpu.VMEM((blocks, tokens, side), jnp.float32),
                pltpu.VMEM(weights.shape, jnp.bfloat16),
                pltpu.VMEM((tokens, cols * side), jnp.bfloat16),
                pltpu.VMEM((cols, tokens, side), jnp.bfloat16),
                pltpu.VMEM((cols, tokens, side), jnp.bfloat16),
                dma((len(shards),)),
                dma((cols,)),
                dma,
                dma((2, cols)),
                dma((len(shards),)),
            ],
        ),
        out_shape=[jax.ShapeDtypeStruct((tokens, cols * side), jnp.bfloat16)] * 2
        + [jax.ShapeDtypeStruct((len(g) * part, tokens), jnp.bfloat16) for g in groups],
        compiler_params=pltpu.CompilerParams(vmem_limit_bytes=40 << 20),
        cost_estimate=pl.CostEstimate(
            flops=flops, bytes_accessed=2 * weights.size, transcendentals=tokens * cols * side
        ),
        name="forward",
    )(rows, offs, *shards, weights, cot)


def weight_kernel(n_planes, n_in, rows_s, offs_s, half_s, *refs):
    x_refs, refs = refs[: n_planes * n_in], refs[n_planes * n_in :]
    slope_refs, (out_ref, xt, slopes, out, x_sem, slope_sem, out_sem) = (
        refs[:n_planes],
        refs[n_planes:],
    )
    cols, slots, side, _ = out.shape
    tokens = slopes.shape[0] // n_planes

    def shard(p, j):
        ref = x_refs[p * n_in + j]
        rows = pl.ds(pl.multiple_of(offs_s[j], 16), ref.shape[0])
        target = xt.at[rows, p * tokens : (p + 1) * tokens]
        return pltpu.make_async_copy(ref, target, x_sem.at[p * n_in + j])

    def slope(p):
        target = slopes.at[p * tokens : (p + 1) * tokens, :]
        return pltpu.make_async_copy(slope_refs[p], target, slope_sem.at[p])

    def result(c):
        return pltpu.make_async_copy(out.at[c], out_ref.at[c], out_sem.at[c])

    copies = [shard(p, j) for p in range(n_planes) for j in range(n_in)]
    copies += [slope(p) for p in range(n_planes)]
    for copy in copies:
        copy.start()
    for copy in copies:
        copy.wait()

    def one(c, carry):
        right = slopes[:, pl.ds(pl.multiple_of(c * side, side), side)]
        for k in range(slots):
            r = rows_s[c, half_s[0] * slots + k]
            left = xt[pl.ds(pl.multiple_of(r * side, side), side), :]
            out[c, k] = jnp.dot(left, right, preferred_element_type=jnp.float32)
        result(c).start()
        return carry

    lax.fori_loop(0, cols, one, 0)

    def drain(c, carry):
        result(c).wait()
        return carry

    lax.fori_loop(0, cols, drain, 0)


def weight_grad(planes, offs, slopes, rows, half, slots, side):
    cols = rows.shape[0]
    tokens = slopes[0].shape[0]
    features = sum(s.shape[0] for s in planes[0])
    shards = [s for plane in planes for s in plane]
    dma = pltpu.SemaphoreType.DMA
    return pl.pallas_call(
        functools.partial(weight_kernel, len(planes), len(planes[0])),
        grid_spec=pltpu.PrefetchScalarGridSpec(
            num_scalar_prefetch=3,
            in_specs=anywhere(len(shards) + len(slopes)),
            out_specs=pl.BlockSpec(memory_space=pl.ANY),
            scratch_shapes=[
                pltpu.VMEM((features, len(planes) * tokens), jnp.bfloat16),
                pltpu.VMEM((len(planes) * tokens, cols * side), jnp.bfloat16),
                pltpu.VMEM((cols, slots, side, side), jnp.float32),
                dma((len(shards),)),
                dma((len(planes),)),
                dma((cols,)),
            ],
        ),
        out_shape=jax.ShapeDtypeStruct((cols, slots, side, side), jnp.float32),
        compiler_params=pltpu.CompilerParams(vmem_limit_bytes=40 << 20),
        cost_estimate=pl.CostEstimate(
            flops=2 * len(planes) * tokens * cols * slots * side * side,
            bytes_accessed=4 * cols * slots * side * side,
            transcendentals=0,
        ),
        name="weight_grad",
    )(rows, offs, half, *shards, *slopes)


def sum_kernel(sizes, *refs):
    refs = list(refs)
    ins, outs = refs[: sum(sizes)], refs[sum(sizes) :]
    for size, out in zip(sizes, outs):
        total = ins[0][...].astype(jnp.float32)
        for ref in ins[1:size]:
            total = total + ref[...].astype(jnp.float32)
        ins = ins[size:]
        out[...] = total.astype(out.dtype)


def add_parts(terms, part, tokens):
    flat = [t for group in terms for t in group]

    def spec(i):
        return pl.BlockSpec((part, tokens), lambda *_: (i, 0))

    return pl.pallas_call(
        functools.partial(sum_kernel, [len(g) for g in terms]),
        grid=(1,),
        in_specs=[spec(i) for _, i in flat],
        out_specs=[spec(0) for _ in terms],
        out_shape=[jax.ShapeDtypeStruct((part, tokens), jnp.bfloat16) for _ in terms],
        name="add_parts",
    )(*[a for a, _ in flat])


def body(activations, block_values, block_rows, cotangent):
    n, mp = lax.axis_size("dp"), lax.axis_size("mp")
    me, half = lax.axis_index("dp"), lax.axis_index("mp")
    side, slot_count = block_values.shape[2], block_values.shape[1]
    own = activations.T
    part, tokens = own.shape
    half = half.astype(jnp.int32).reshape(1)
    chip = CORES * SIDES
    line = n // chip
    if not direct(n, mp):
        offs = jnp.zeros((1,), jnp.int32)
        x_own = lax.all_gather(own, "dp", axis=0, tiled=True)
        x_all = lax.all_gather(x_own, "mp", axis=0)
        gelu_out, slopes, dx = forward(
            [x_own], offs, block_values, block_rows, cotangent, [(0,)], [(0,)]
        )
        slopes_all = lax.all_gather(slopes, "mp", axis=0)
        block_grad = weight_grad(
            [[x_all[p]] for p in range(mp)],
            offs,
            [slopes_all[p] for p in range(mp)],
            block_rows,
            half,
            slot_count // mp,
            side,
        )
        dx = dx.astype(jnp.float32)
        dx = lax.psum_scatter(dx, "dp", scatter_dimension=0, tiled=True)
        return gelu_out, dx.astype(jnp.bfloat16).T, block_grad

    def permute(a, k, s, q):
        def source(i):
            z, x, core = i // chip, i // CORES % SIDES, i % CORES
            return ((z + k) % line * SIDES + (x ^ s)) * CORES + (core ^ q)

        return lax.ppermute(a, "dp", [(source(i), i) for i in range(n)])

    def across(a):
        return lax.ppermute(a, "mp", [(i, i ^ 1) for i in range(mp)])

    rel = [(k, s, q) for q in range(CORES) for k in range(line) for s in range(SIDES)]
    ks, ss, qs = (np.array(v, np.int32) for v in zip(*rel))
    z, x, core = me // chip, me // CORES % SIDES, me % CORES
    offs = (((z + ks) % line * SIDES + (x ^ ss)) * CORES + (core ^ qs)) * part
    offs = offs.astype(jnp.int32)

    got = {(k, 0, 0): permute(own, k, 0, 0) if k else own for k in range(line)}
    for k in range(line):
        got[k, 1, 0] = permute(got[k, 0, 0], 0, 1, 0)
    far = {(k, s, q): across(a) for (k, s, q), a in got.items()}
    for k, s, q in rel:
        if q:
            got[k, s, 1] = permute(got[k, s, 0], 0, 0, 1)
            far[k, s, 1] = permute(far[k, s, 0], 0, 0, 1)
    x_own = [got[key] for key in rel]
    x_far = [far[key] for key in rel]

    per_core = len(rel) // CORES
    groups = [tuple(range(q * per_core, (q + 1) * per_core)) for q in range(CORES)]
    sets = [tuple(range(i, len(rel), per_core)) for i in range(per_core)]
    if CORES * part % side:
        sets = [tuple(range(len(rel)))]
    gelu_out, slopes, dx_own, dx_core = forward(
        x_own, offs, block_values, block_rows, cotangent, groups, sets
    )
    slopes_far = across(slopes)
    dx_in = permute(dx_core, 0, 0, 1)

    def at(k, s):
        return rel.index((k, s, 0))

    chips = add_parts(
        [[(dx_own, at(k, 1)), (dx_in, at(k, 1))] for k in range(line)], part, tokens
    )
    pairs = [permute(a, 0, 1, 0) for a in chips]
    last = [(dx_own, at(0, 0)), (dx_in, at(0, 0)), (pairs[0], 0)]
    for k in range(1, line):
        (mine,) = add_parts(
            [[(dx_own, at(k, 0)), (dx_in, at(k, 0)), (pairs[k], 0)]], part, tokens
        )
        last.append((permute(mine, line - k, 0, 0), 0))
    (dx,) = add_parts([last], part, tokens)
    block_grad = weight_grad(
        [x_own, x_far], offs, [slopes, slopes_far], block_rows, half, slot_count // mp, side
    )
    return gelu_out, dx.T, block_grad


def direct(n, mp):
    return n % (CORES * SIDES) == 0 and n // (CORES * SIDES) <= MAX_LINE and mp == 2


def solution(mesh):
    in_specs = (P("mp", "dp"), P("dp", None, None, None), P("dp", None), P("mp", "dp"))
    out_specs = (P("mp", "dp"), P("mp", "dp"), P("dp", "mp", None, None))
    return jax.shard_map(body, mesh=mesh, in_specs=in_specs, out_specs=out_specs, check_vma=False)
```

time: 460 us -> 147 us (0.32)
  waiting for transfers between devices: 228 us -> 48.4 us
  local copies, waits for them, and re-layouts: 105 us -> 14.8 us
  matrix products: 85.8 us -> 0 us
  Pallas kernels: 0 us -> 45.2 us
  starting transfers between devices: 9.49 us -> 36.3 us
  other arithmetic: 16.3 us -> 0.7 us
  between operations: 13.8 us -> 0.83 us
    all_to_all x1 -> x0, waiting for transfers between devices: 157 us -> none  [body(): lax.all_to_all(outgoing, 'mp', split_axis=0, concat_axis=0, tiled=True)]
    dot_general x4 -> x0, matrix products: 85.8 us -> none  [the longest x1 40.7 us: body(): jnp.einsum('tmi,mr->tri', contrib, one_hot, precision=lax.Precision.HIGHEST)]
    ppermute x0 -> x40, waiting for transfers between devices: none -> 48.4 us  [the longest x9 28.6 us: across(): return lax.ppermute(a, 'mp', [(i, i ^ 1) for i in range(mp)])]
    pallas_call x0 -> x7, Pallas kernels: none -> 45.2 us  [the longest x1 23.9 us: forward(): pl.pallas_call(functools.partial(forward_kernel, len(shards), groups, set...]
    all_gather x2 -> x0, waiting for transfers between devices: 41.6 us -> none  [the longest x1 41.6 us: body(): x_full = lax.all_gather(activations, 'dp', axis=1, tiled=True)]
    ppermute x0 -> x40, starting transfers between devices: none -> 36.3 us  [the longest x31 25.7 us: permute(): return lax.ppermute(a, 'dp', [(source(i), i) for i in range(n)])]
    reshape x6 -> x0, local copies, waits for them, and re-layouts: 36 us -> none  [the longest x1 25.3 us: body(): incoming.reshape(mp_size * rows_here, col_blocks, per_peer, block_size)]
    all_to_all x1 -> x0, local copies, waits for them, and re-layouts: 29.1 us -> none  [body(): lax.all_to_all(outgoing, 'mp', split_axis=0, concat_axis=0, tiled=True)]
  transfers between devices with their start and end apart: 4 -> 40, of which waited for: 3 -> 14; matrix products, arithmetic and copies ran while one was open for 21% -> 0% of each run, Pallas kernels for 0% -> 13%
where the time goes in v1:
time: 147 us; the launch traced here: 146 us
  waiting for transfers between devices  48.4 us (33%)
  Pallas kernels  45.2 us (31%)
  starting transfers between devices  36.3 us (25%)
  local copies, waits for them, and re-layouts  14.8 us (10%)
    ppermute x9, waiting for transfers between devices, across(): return lax.ppermute(a, 'mp', [(i, i ^ 1) for i in range(mp)])  28.6 us
    ppermute x31, starting transfers between devices, permute(): return lax.ppermute(a, 'dp', [(source(i), i) for i in range(n)])  25.7 us
    pallas_call x1, Pallas kernels, forward(): pl.pallas_call(functools.partial(forward_kernel, len(shards), groups, set...  23.9 us
    ppermute x31, waiting for transfers between devices, permute(): return lax.ppermute(a, 'dp', [(source(i), i) for i in range(n)])  19.8 us
    unnamed x48, local copies, waits for them, and re-layouts  14.8 us
    pallas_call x1, Pallas kernels, weight_grad(): pl.pallas_call(functools.partial(weight_kernel, len(planes), len(planes[0...  11.8 us
    ppermute x9, starting transfers between devices, across(): return lax.ppermute(a, 'mp', [(i, i ^ 1) for i in range(mp)])  10.7 us
    pallas_call x5, Pallas kernels, add_parts(): pl.pallas_call(functools.partial(sum_kernel, [len(g) for g in terms]), gr...  9.53 us
  transfers between devices with their start and end apart: 40, of which 14 were waited for; matrix products, arithmetic and copies ran while one was open for 0% of the time, Pallas kernels for 13%

profile of v1, /device:TPU:0, one launch (start us, length us, event | category | flops | bytes accessed | tf_op | source)
XLA Modules:
  0.0 146.3 jit_solution(2530067951580292862)
XLA Ops:
  0.6 3.1 %collective-permute-start.5 = (bf16[576,128]{1,0:T(8,128)(2,1)}, bf16[576,128]{1,0:T(8,128)(2,1)S(1)}, u32[]{:S(2)}, u32[]{:S(2)}) collective-permute-start(bf16[576,128]{1,0:T(8,128)(2,1)} %bitcast.3), channel_id=1, source_target_pairs={{24,0},{26,2},{28,4},{30,6},{0,8},{2,10},{4,12},{6,14},{8,16},{10,... | collective-permute-start | bytes 442376 | tf_op jit(solution)/shard_map/ppermute | solution.py:339
  3.7 2.6 %collective-permute-start.3 = (bf16[576,128]{1,0:T(8,128)(2,1)}, bf16[576,128]{1,0:T(8,128)(2,1)S(1)}, u32[]{:S(2)}, u32[]{:S(2)}) collective-permute-start(bf16[576,128]{1,0:T(8,128)(2,1)} %bitcast.5), channel_id=1, source_target_pairs={{16,0},{18,2},{20,4},{22,6},{24,8},{26,10},{28,12},{30,14},{0,16},... | collective-permute-start | bytes 442376 | tf_op jit(solution)/shard_map/ppermute | solution.py:339
  6.3 1.3 collective-permute-start.1
  7.7 1.5 %collective-permute-start = (bf16[576,128]{1,0:T(8,128)(2,1)}, bf16[576,128]{1,0:T(8,128)(2,1)S(1)}, u32[]{:S(2)}, u32[]{:S(2)}) collective-permute-start(bf16[576,128]{1,0:T(8,128)(2,1)} %bitcast.7), channel_id=1, source_target_pairs={{4,0},{6,2},{0,4},{2,6},{12,8},{14,10},{8,12},{10,14},{20,16},{22,... | collective-permute-start | bytes 442376 | tf_op jit(solution)/shard_map/ppermute | solution.py:339
  9.2 1.6 %collective-permute-done.5.refs_6_ = bf16[576,128]{1,0:T(8,128)(2,1)S(1)} collective-permute-done((bf16[576,128]{1,0:T(8,128)(2,1)}, bf16[576,128]{1,0:T(8,128)(2,1)S(1)}, u32[]{:S(2)}, u32[]{:S(2)}) %collective-permute-start.5) | collective-permute-done | bytes 147488 | tf_op jit(solution)/shard_map/ppermute | solution.py:339
  10.8 1.5 %collective-permute-start.6 = (bf16[576,128]{1,0:T(8,128)(2,1)S(1)}, bf16[576,128]{1,0:T(8,128)(2,1)S(1)}, u32[]{:S(2)}, u32[]{:S(2)}) collective-permute-start(bf16[576,128]{1,0:T(8,128)(2,1)S(1)} %collective-permute-done.5.refs_6_), channel_id=1, source_target_pairs={{4,0},{6,2},{0,4},{2,6},{12,8},{14,10},{8,12},{10,14},{20,16},{22,... | collective-permute-start | bytes 442376 | tf_op jit(solution)/shard_map/ppermute | solution.py:339
  12.3 4.0 %collective-permute-done.3.refs_4_ = bf16[576,128]{1,0:T(8,128)(2,1)S(1)} collective-permute-done((bf16[576,128]{1,0:T(8,128)(2,1)}, bf16[576,128]{1,0:T(8,128)(2,1)S(1)}, u32[]{:S(2)}, u32[]{:S(2)}) %collective-permute-start.3) | collective-permute-done | bytes 147488 | tf_op jit(solution)/shard_map/ppermute | solution.py:339
  16.3 1.5 %collective-permute-start.4 = (bf16[576,128]{1,0:T(8,128)(2,1)S(1)}, bf16[576,128]{1,0:T(8,128)(2,1)S(1)}, u32[]{:S(2)}, u32[]{:S(2)}) collective-permute-start(bf16[576,128]{1,0:T(8,128)(2,1)S(1)} %collective-permute-done.3.refs_4_), channel_id=1, source_target_pairs={{4,0},{6,2},{0,4},{2,6},{12,8},{14,10},{8,12},{10,14},{20,16},{22,... | collective-permute-start | bytes 442376 | tf_op jit(solution)/shard_map/ppermute | solution.py:339
  18.9 4.1 %collective-permute-done.4.refs_5_ = bf16[576,128]{1,0:T(8,128)(2,1)S(1)} collective-permute-done((bf16[576,128]{1,0:T(8,128)(2,1)S(1)}, bf16[576,128]{1,0:T(8,128)(2,1)S(1)}, u32[]{:S(2)}, u32[]{:S(2)}) %collective-permute-start.4) | collective-permute-done | bytes 147488 | tf_op jit(solution)/shard_map/ppermute | solution.py:339
  23.0 2.7 %collective-permute-done.2.refs_3_ = bf16[576,128]{1,0:T(8,128)(2,1)S(1)} collective-permute-done((bf16[576,128]{1,0:T(8,128)(2,1)S(1)}, bf16[576,128]{1,0:T(8,128)(2,1)S(1)}, u32[]{:S(2)}, u32[]{:S(2)}) %collective-permute-start.2) | collective-permute-done | bytes 147488 | tf_op jit(solution)/shard_map/ppermute | solution.py:339
  27.0 1.1 copy-done.1
  28.2 0.9 copy-done.2
  29.8 23.9 %forward.1 = (bf16[128,3072]{1,0:T(8,128)(2,1)}, bf16[128,3072]{1,0:T(8,128)(2,1)S(1)}, bf16[4608,128]{1,0:T(8,128)(2,1)S(1)}, bf16[4608,128]{1,0:T(8,128)(2,1)S(1)}) custom-call(s32[24,20]{1,0:T(8,128)S(1)} %copy-done.20, s32[16]{0:T(128)S(1)} %fusion.5.offs_s, bf16[576,128]{1,0:T(8,128)(2,1)S(1)} %bitcast.8, ...), custom_call_target="tpu_custom_call" | custom-call | flops 4026531840 | bytes 15728640 | tf_op jit(solution)/shard_map/forward/pallas_call | solution.py:167
  53.7 1.1 copy-done
  54.9 1.5 %collective-permute-start.23 = (bf16[576,128]{1,0:T(8,128)(2,1)S(1)}, bf16[576,128]{1,0:T(8,128)(2,1)S(1)}, u32[]{:S(2)}, u32[]{:S(2)}) collective-permute-start(bf16[576,128]{1,0:T(8,128)(2,1)S(1)} %bitcast.9), channel_id=1, source_target_pairs={{0,1},{1,0},{2,3},{3,2},{4,5},{5,4},{6,7},{7,6},{8,9},{9,8},{10,11... | collective-permute-start | bytes 442376 | tf_op jit(solution)/shard_map/ppermute | solution.py:342
  56.9 4.7 %collective-permute-done.23.refs_16_ = bf16[576,128]{1,0:T(8,128)(2,1)S(1)} collective-permute-done((bf16[576,128]{1,0:T(8,128)(2,1)S(1)}, bf16[576,128]{1,0:T(8,128)(2,1)S(1)}, u32[]{:S(2)}, u32[]{:S(2)}) %collective-permute-start.23) | collective-permute-done | bytes 147488 | tf_op jit(solution)/shard_map/ppermute | solution.py:342
  61.6 1.5 %collective-permute-start.29 = (bf16[576,128]{1,0:T(8,128)(2,1)S(1)}, bf16[576,128]{1,0:T(8,128)(2,1)S(1)}, u32[]{:S(2)}, u32[]{:S(2)}) collective-permute-start(bf16[576,128]{1,0:T(8,128)(2,1)S(1)} %collective-permute-done.5.refs_6_), channel_id=1, source_target_pairs={{0,1},{1,0},{2,3},{3,2},{4,5},{5,4},{6,7},{7,6},{8,9},{9,8},{10,11... | collective-permute-start | bytes 442376 | tf_op jit(solution)/shard_map/ppermute | solution.py:342
  64.3 1.5 %collective-permute-start.25 = (bf16[576,128]{1,0:T(8,128)(2,1)S(1)}, bf16[576,128]{1,0:T(8,128)(2,1)}, u32[]{:S(2)}, u32[]{:S(2)}) collective-permute-start(bf16[576,128]{1,0:T(8,128)(2,1)S(1)} %collective-permute-done.1.refs_2_), channel_id=1, source_target_pairs={{0,1},{1,0},{2,3},{3,2},{4,5},{5,4},{6,7},{7,6},{8,9},{9,8},{10,11... | collective-permute-start | bytes 442376 | tf_op jit(solution)/shard_map/ppermute | solution.py:342
  65.8 15.8 %collective-permute-done.29.refs_22_ = bf16[576,128]{1,0:T(8,128)(2,1)S(1)} collective-permute-done((bf16[576,128]{1,0:T(8,128)(2,1)S(1)}, bf16[576,128]{1,0:T(8,128)(2,1)S(1)}, u32[]{:S(2)}, u32[]{:S(2)}) %collective-permute-start.29) | collective-permute-done | bytes 147488 | tf_op jit(solution)/shard_map/ppermute | solution.py:342
  81.6 1.5 %collective-permute-start.24 = (bf16[576,128]{1,0:T(8,128)(2,1)S(1)}, bf16[576,128]{1,0:T(8,128)(2,1)S(1)}, u32[]{:S(2)}, u32[]{:S(2)}) collective-permute-start(bf16[576,128]{1,0:T(8,128)(2,1)S(1)} %collective-permute-done.refs_1_), channel_id=1, source_target_pairs={{0,1},{1,0},{2,3},{3,2},{4,5},{5,4},{6,7},{7,6},{8,9},{9,8},{10,11... | collective-permute-start | bytes 442376 | tf_op jit(solution)/shard_map/ppermute | solution.py:342
  83.1 1.8 %collective-permute-done.27.refs_20_ = bf16[576,128]{1,0:T(8,128)(2,1)} collective-permute-done((bf16[576,128]{1,0:T(8,128)(2,1)S(1)}, bf16[576,128]{1,0:T(8,128)(2,1)}, u32[]{:S(2)}, u32[]{:S(2)}) %collective-permute-start.27) | collective-permute-done | bytes 147488 | tf_op jit(solution)/shard_map/ppermute | solution.py:342
  85.6 2.5 %collective-permute-done.25.refs_18_ = bf16[576,128]{1,0:T(8,128)(2,1)} collective-permute-done((bf16[576,128]{1,0:T(8,128)(2,1)S(1)}, bf16[576,128]{1,0:T(8,128)(2,1)}, u32[]{:S(2)}, u32[]{:S(2)}) %collective-permute-start.25) | collective-permute-done | bytes 147488 | tf_op jit(solution)/shard_map/ppermute | solution.py:342
  88.1 1.5 %collective-permute-start.30 = (bf16[576,128]{1,0:T(8,128)(2,1)S(1)}, bf16[576,128]{1,0:T(8,128)(2,1)}, u32[]{:S(2)}, u32[]{:S(2)}) collective-permute-start(bf16[576,128]{1,0:T(8,128)(2,1)S(1)} %collective-permute-done.6.refs_7_), channel_id=1, source_target_pairs={{0,1},{1,0},{2,3},{3,2},{4,5},{5,4},{6,7},{7,6},{8,9},{9,8},{10,11... | collective-permute-start | bytes 442376 | tf_op jit(solution)/shard_map/ppermute | solution.py:342
  89.6 1.5 %collective-permute-done.24.refs_17_ = bf16[576,128]{1,0:T(8,128)(2,1)S(1)} collective-permute-done((bf16[576,128]{1,0:T(8,128)(2,1)S(1)}, bf16[576,128]{1,0:T(8,128)(2,1)S(1)}, u32[]{:S(2)}, u32[]{:S(2)}) %collective-permute-start.24) | collective-permute-done | bytes 147488 | tf_op jit(solution)/shard_map/ppermute | solution.py:342
  92.5 1.5 %collective-permute-start.28 = (bf16[576,128]{1,0:T(8,128)(2,1)S(1)}, bf16[576,128]{1,0:T(8,128)(2,1)}, u32[]{:S(2)}, u32[]{:S(2)}) collective-permute-start(bf16[576,128]{1,0:T(8,128)(2,1)S(1)} %collective-permute-done.4.refs_5_), channel_id=1, source_target_pairs={{0,1},{1,0},{2,3},{3,2},{4,5},{5,4},{6,7},{7,6},{8,9},{9,8},{10,11... | collective-permute-start | bytes 442376 | tf_op jit(solution)/shard_map/ppermute | solution.py:342
  94.0 1.0 copy-done.22
  95.0 2.2 %add_parts.5 = (bf16[576,128]{1,0:T(8,128)(2,1)}, bf16[576,128]{1,0:T(8,128)(2,1)}, bf16[576,128]{1,0:T(8,128)(2,1)}, bf16[576,128]{1,0:T(8,128)(2,1)}) custom-call(bf16[4608,128]{1,0:T(8,128)(2,1)} %copy-done, bf16[4608,128]{1,0:T(8,128)(2,1)} %copy-done.22, bf16[4608,128]{1,0:T(8,128)(2,1)} %copy-done, bf16[4608,128]{1,0:T(8,128)(2,1)} %copy-done.22, ...), custom_call_target="tpu_custom_call" | custom-call | tf_op jit(solution)/shard_map/add_parts/pallas_call | solution.py:294
  97.8 1.5 %collective-permute-start.17 = (bf16[576,128]{1,0:T(8,128)(2,1)}, bf16[576,128]{1,0:T(8,128)(2,1)S(1)}, u32[]{:S(2)}, u32[]{:S(2)}) collective-permute-start(bf16[576,128]{1,0:T(8,128)(2,1)} %get-tuple-element.15), channel_id=1, source_target_pairs={{4,0},{6,2},{0,4},{2,6},{12,8},{14,10},{8,12},{10,14},{20,16},{22,... | collective-permute-start | bytes 442376 | tf_op jit(solution)/shard_map/ppermute | solution.py:339
  99.8 1.5 %collective-permute-start.21 = (bf16[576,128]{1,0:T(8,128)(2,1)}, bf16[576,128]{1,0:T(8,128)(2,1)}, u32[]{:S(2)}, u32[]{:S(2)}) collective-permute-start(bf16[576,128]{1,0:T(8,128)(2,1)} %get-tuple-element.17), channel_id=1, source_target_pairs={{4,0},{6,2},{0,4},{2,6},{12,8},{14,10},{8,12},{10,14},{20,16},{22,... | collective-permute-start | bytes 442376 | tf_op jit(solution)/shard_map/ppermute | solution.py:339
  101.3 2.3 %collective-permute-done.26.refs_19_ = bf16[576,128]{1,0:T(8,128)(2,1)} collective-permute-done((bf16[576,128]{1,0:T(8,128)(2,1)S(1)}, bf16[576,128]{1,0:T(8,128)(2,1)}, u32[]{:S(2)}, u32[]{:S(2)}) %collective-permute-start.26) | collective-permute-done | bytes 147488 | tf_op jit(solution)/shard_map/ppermute | solution.py:342
  103.6 1.1 collective-permute-done.17.refs_2_
  104.7 3.3 %collective-permute-done.19.refs_2_ = bf16[576,128]{1,0:T(8,128)(2,1)} collective-permute-done((bf16[576,128]{1,0:T(8,128)(2,1)}, bf16[576,128]{1,0:T(8,128)(2,1)}, u32[]{:S(2)}, u32[]{:S(2)}) %collective-permute-start.19) | collective-permute-done | bytes 147488 | tf_op jit(solution)/shard_map/ppermute | solution.py:339
  108.0 2.4 %collective-permute-done.21.refs_2_ = bf16[576,128]{1,0:T(8,128)(2,1)} collective-permute-done((bf16[576,128]{1,0:T(8,128)(2,1)}, bf16[576,128]{1,0:T(8,128)(2,1)}, u32[]{:S(2)}, u32[]{:S(2)}) %collective-permute-start.21) | collective-permute-done | bytes 147488 | tf_op jit(solution)/shard_map/ppermute | solution.py:339
  110.4 1.8 %add_parts.6 = bf16[576,128]{1,0:T(8,128)(2,1)} custom-call(bf16[4608,128]{1,0:T(8,128)(2,1)} %copy-done, bf16[4608,128]{1,0:T(8,128)(2,1)} %copy-done.22, bf16[576,128]{1,0:T(8,128)(2,1)} %copy-done.23), custom_call_target="tpu_custom_call" | custom-call | tf_op jit(solution)/shard_map/add_parts/pallas_call | solution.py:294
  112.2 1.8 %add_parts.7 = bf16[576,128]{1,0:T(8,128)(2,1)} custom-call(bf16[4608,128]{1,0:T(8,128)(2,1)} %copy-done, bf16[4608,128]{1,0:T(8,128)(2,1)} %copy-done.22, bf16[576,128]{1,0:T(8,128)(2,1)} %collective-permute-done.19.refs_2_), custom_call_target="tpu_custom_call" | custom-call | tf_op jit(solution)/shard_map/add_parts/pallas_call | solution.py:294
  113.9 1.8 %add_parts.8 = bf16[576,128]{1,0:T(8,128)(2,1)} custom-call(bf16[4608,128]{1,0:T(8,128)(2,1)} %copy-done, bf16[4608,128]{1,0:T(8,128)(2,1)} %copy-done.22, bf16[576,128]{1,0:T(8,128)(2,1)} %collective-permute-done.21.refs_2_), custom_call_target="tpu_custom_call" | custom-call | tf_op jit(solution)/shard_map/add_parts/pallas_call | solution.py:294
  115.7 1.5 %collective-permute-start.16 = (bf16[576,128]{1,0:T(8,128)(2,1)}, bf16[576,128]{1,0:T(8,128)(2,1)}, u32[]{:S(2)}, u32[]{:S(2)}) collective-permute-start(bf16[576,128]{1,0:T(8,128)(2,1)} %get-tuple-element.14), channel_id=1, source_target_pairs={{4,0},{6,2},{0,4},{2,6},{12,8},{14,10},{8,12},{10,14},{20,16},{22,... | collective-permute-start | bytes 442376 | tf_op jit(solution)/shard_map/ppermute | solution.py:339
  117.2 3.2 %collective-permute-start.18 = (bf16[576,128]{1,0:T(8,128)(2,1)}, bf16[576,128]{1,0:T(8,128)(2,1)}, u32[]{:S(2)}, u32[]{:S(2)}) collective-permute-start(bf16[576,128]{1,0:T(8,128)(2,1)} %add_parts.6), channel_id=1, source_target_pairs={{24,0},{26,2},{28,4},{30,6},{0,8},{2,10},{4,12},{6,14},{8,16},{10,... | collective-permute-start | bytes 442376 | tf_op jit(solution)/shard_map/ppermute | solution.py:339
  120.5 2.0 %collective-permute-start.20 = (bf16[576,128]{1,0:T(8,128)(2,1)}, bf16[576,128]{1,0:T(8,128)(2,1)}, u32[]{:S(2)}, u32[]{:S(2)}) collective-permute-start(bf16[576,128]{1,0:T(8,128)(2,1)} %add_parts.7), channel_id=1, source_target_pairs={{16,0},{18,2},{20,4},{22,6},{24,8},{26,10},{28,12},{30,14},{0,16},... | collective-permute-start | bytes 442376 | tf_op jit(solution)/shard_map/ppermute | solution.py:339
  122.5 2.6 %collective-permute-start.22 = (bf16[576,128]{1,0:T(8,128)(2,1)}, bf16[576,128]{1,0:T(8,128)(2,1)}, u32[]{:S(2)}, u32[]{:S(2)}) collective-permute-start(bf16[576,128]{1,0:T(8,128)(2,1)} %add_parts.8), channel_id=1, source_target_pairs={{8,0},{10,2},{12,4},{14,6},{16,8},{18,10},{20,12},{22,14},{24,16},... | collective-permute-start | bytes 442376 | tf_op jit(solution)/shard_map/ppermute | solution.py:339
  126.0 0.9 copy-done.7
  126.9 0.9 copy-done.9
  127.8 0.9 copy-done.11
  128.7 0.9 copy-done.13
  130.6 0.9 copy-done.17
  131.5 0.9 copy-done.19
  132.4 11.8 %weight_grad.1 = f32[24,10,128,128]{3,2,1,0:T(8,128)} custom-call(s32[24,20]{1,0:T(8,128)S(1)} %copy-done.21, s32[16]{0:T(128)S(1)} %fusion.5.offs_s, s32[1]{0:T(128)} %bitcast.2.half_s, bf16[576,128]{1,0:T(8,128)(2,1)S(1)} %bitcast.10, bf16[576,128]{1,0:T(8,128)(2,1)S(1)} %collective-permute-done.refs_1_, ...), custom_call_target="tpu_custom_call" | custom-call | flops 2013265920 | bytes 15728640 | tf_op jit(solution)/shard_map/weight_grad/pallas_call | solution.py:251
  144.3 2.0 %add_parts.9 = bf16[576,128]{1,0:T(8,128)(2,1)} custom-call(bf16[4608,128]{1,0:T(8,128)(2,1)} %copy-done, bf16[4608,128]{1,0:T(8,128)(2,1)} %copy-done.22, bf16[576,128]{1,0:T(8,128)(2,1)} %collective-permute-done.16.refs_2_, bf16[576,128]{1,0:T(8,128)(2,1)} %collective-permute-done.18.refs_3_, bf16[576,128]{1,0:T(8,128)(2,1)} %collective-permute-done.20.refs_4_, ...), custom_call_target="tpu_custom_call" | custom-call | tf_op jit(solution)/shard_map/add_parts/pallas_call | solution.py:294
  (88 shorter events, 10.1 us)
Async XLA Ops:
  0.6 10.1 %collective-permute-start.5 = (bf16[576,128]{1,0:T(8,128)(2,1)}, bf16[576,128]{1,0:T(8,128)(2,1)S(1)}, u32[]{:S(2)}, u32[]{:S(2)}) collective-permute-start(bf16[576,128]{1,0:T(8,128)(2,1)} %bitcast.3), channel_id=1, source_target_pairs={{24,0},{26,2},{28,4},{30,6},{0,8},{2,10},{4,12},{6,14},{8,16},{10,... | collective-permute-start | bytes 442376 | tf_op jit(solution)/shard_map/ppermute | solution.py:339
  3.7 7.0 %collective-permute-start.7 = (bf16[576,128]{1,0:T(8,128)(2,1)}, bf16[576,128]{1,0:T(8,128)(2,1)S(1)}, u32[]{:S(2)}, u32[]{:S(2)}) collective-permute-start(bf16[576,128]{1,0:T(8,128)(2,1)} %bitcast.4), channel_id=1, source_target_pairs={{2,0},{0,2},{6,4},{4,6},{10,8},{8,10},{14,12},{12,14},{18,16},{16,... | collective-permute-start | bytes 442376 | tf_op jit(solution)/shard_map/ppermute | solution.py:339
  3.7 12.5 %collective-permute-start.3 = (bf16[576,128]{1,0:T(8,128)(2,1)}, bf16[576,128]{1,0:T(8,128)(2,1)S(1)}, u32[]{:S(2)}, u32[]{:S(2)}) collective-permute-start(bf16[576,128]{1,0:T(8,128)(2,1)} %bitcast.5), channel_id=1, source_target_pairs={{16,0},{18,2},{20,4},{22,6},{24,8},{26,10},{28,12},{30,14},{0,16},... | collective-permute-start | bytes 442376 | tf_op jit(solution)/shard_map/ppermute | solution.py:339
  6.3 10.0 %collective-permute-start.1 = (bf16[576,128]{1,0:T(8,128)(2,1)}, bf16[576,128]{1,0:T(8,128)(2,1)S(1)}, u32[]{:S(2)}, u32[]{:S(2)}) collective-permute-start(bf16[576,128]{1,0:T(8,128)(2,1)} %bitcast.6), channel_id=1, source_target_pairs={{8,0},{10,2},{12,4},{14,6},{16,8},{18,10},{20,12},{22,14},{24,16},... | collective-permute-start | bytes 442376 | tf_op jit(solution)/shard_map/ppermute | solution.py:339
  7.7 10.1 %collective-permute-start = (bf16[576,128]{1,0:T(8,128)(2,1)}, bf16[576,128]{1,0:T(8,128)(2,1)S(1)}, u32[]{:S(2)}, u32[]{:S(2)}) collective-permute-start(bf16[576,128]{1,0:T(8,128)(2,1)} %bitcast.7), channel_id=1, source_target_pairs={{4,0},{6,2},{0,4},{2,6},{12,8},{14,10},{8,12},{10,14},{20,16},{22,... | collective-permute-start | bytes 442376 | tf_op jit(solution)/shard_map/ppermute | solution.py:339
  10.8 7.5 %collective-permute-start.13 = (bf16[576,128]{1,0:T(8,128)(2,1)S(1)}, bf16[576,128]{1,0:T(8,128)(2,1)S(1)}, u32[]{:S(2)}, u32[]{:S(2)}) collective-permute-start(bf16[576,128]{1,0:T(8,128)(2,1)S(1)} %collective-permute-done.5.refs_6_), channel_id=1, source_target_pairs={{2,0},{0,2},{6,4},{4,6},{10,8},{8,10},{14,12},{12,14},{18,16},{16,... | collective-permute-start | bytes 442376 | tf_op jit(solution)/shard_map/ppermute | solution.py:339
  10.8 7.5 %collective-permute-start.6 = (bf16[576,128]{1,0:T(8,128)(2,1)S(1)}, bf16[576,128]{1,0:T(8,128)(2,1)S(1)}, u32[]{:S(2)}, u32[]{:S(2)}) collective-permute-start(bf16[576,128]{1,0:T(8,128)(2,1)S(1)} %collective-permute-done.5.refs_6_), channel_id=1, source_target_pairs={{4,0},{6,2},{0,4},{2,6},{12,8},{14,10},{8,12},{10,14},{20,16},{22,... | collective-permute-start | bytes 442376 | tf_op jit(solution)/shard_map/ppermute | solution.py:339
  16.2 2.6 %collective-permute-start.11 = (bf16[576,128]{1,0:T(8,128)(2,1)S(1)}, bf16[576,128]{1,0:T(8,128)(2,1)S(1)}, u32[]{:S(2)}, u32[]{:S(2)}) collective-permute-start(bf16[576,128]{1,0:T(8,128)(2,1)S(1)} %collective-permute-done.3.refs_4_), channel_id=1, source_target_pairs={{2,0},{0,2},{6,4},{4,6},{10,8},{8,10},{14,12},{12,14},{18,16},{16,... | collective-permute-start | bytes 442376 | tf_op jit(solution)/shard_map/ppermute | solution.py:339
  16.3 6.7 %collective-permute-start.4 = (bf16[576,128]{1,0:T(8,128)(2,1)S(1)}, bf16[576,128]{1,0:T(8,128)(2,1)S(1)}, u32[]{:S(2)}, u32[]{:S(2)}) collective-permute-start(bf16[576,128]{1,0:T(8,128)(2,1)S(1)} %collective-permute-done.3.refs_4_), channel_id=1, source_target_pairs={{4,0},{6,2},{0,4},{2,6},{12,8},{14,10},{8,12},{10,14},{20,16},{22,... | collective-permute-start | bytes 442376 | tf_op jit(solution)/shard_map/ppermute | solution.py:339
  17.8 7.9 %collective-permute-start.2 = (bf16[576,128]{1,0:T(8,128)(2,1)S(1)}, bf16[576,128]{1,0:T(8,128)(2,1)S(1)}, u32[]{:S(2)}, u32[]{:S(2)}) collective-permute-start(bf16[576,128]{1,0:T(8,128)(2,1)S(1)} %collective-permute-done.1.refs_2_), channel_id=1, source_target_pairs={{4,0},{6,2},{0,4},{2,6},{12,8},{14,10},{8,12},{10,14},{20,16},{22,... | collective-permute-start | bytes 442376 | tf_op jit(solution)/shard_map/ppermute | solution.py:339
  18.3 8.1 %collective-permute-start.9 = (bf16[576,128]{1,0:T(8,128)(2,1)S(1)}, bf16[576,128]{1,0:T(8,128)(2,1)S(1)}, u32[]{:S(2)}, u32[]{:S(2)}) collective-permute-start(bf16[576,128]{1,0:T(8,128)(2,1)S(1)} %collective-permute-done.1.refs_2_), channel_id=1, source_target_pairs={{2,0},{0,2},{6,4},{4,6},{10,8},{8,10},{14,12},{12,14},{18,16},{16,... | collective-permute-start | bytes 442376 | tf_op jit(solution)/shard_map/ppermute | solution.py:339
  18.3 8.1 %collective-permute-start.8 = (bf16[576,128]{1,0:T(8,128)(2,1)S(1)}, bf16[576,128]{1,0:T(8,128)(2,1)S(1)}, u32[]{:S(2)}, u32[]{:S(2)}) collective-permute-start(bf16[576,128]{1,0:T(8,128)(2,1)S(1)} %collective-permute-done.refs_1_), channel_id=1, source_target_pairs={{2,0},{0,2},{6,4},{4,6},{10,8},{8,10},{14,12},{12,14},{18,16},{16,... | collective-permute-start | bytes 442376 | tf_op jit(solution)/shard_map/ppermute | solution.py:339
  18.8 7.6 %collective-permute-start.14 = (bf16[576,128]{1,0:T(8,128)(2,1)S(1)}, bf16[576,128]{1,0:T(8,128)(2,1)S(1)}, u32[]{:S(2)}, u32[]{:S(2)}) collective-permute-start(bf16[576,128]{1,0:T(8,128)(2,1)S(1)} %collective-permute-done.6.refs_7_), channel_id=1, source_target_pairs={{2,0},{0,2},{6,4},{4,6},{10,8},{8,10},{14,12},{12,14},{18,16},{16,... | collective-permute-start | bytes 442376 | tf_op jit(solution)/shard_map/ppermute | solution.py:339
  23.0 3.4 %collective-permute-start.12 = (bf16[576,128]{1,0:T(8,128)(2,1)S(1)}, bf16[576,128]{1,0:T(8,128)(2,1)S(1)}, u32[]{:S(2)}, u32[]{:S(2)}) collective-permute-start(bf16[576,128]{1,0:T(8,128)(2,1)S(1)} %collective-permute-done.4.refs_5_), channel_id=1, source_target_pairs={{2,0},{0,2},{6,4},{4,6},{10,8},{8,10},{14,12},{12,14},{18,16},{16,... | collective-permute-start | bytes 442376 | tf_op jit(solution)/shard_map/ppermute | solution.py:339
  25.7 1.4 collective-permute-start.10
  26.4 27.3 %copy-start.4 = (bf16[576,128]{1,0:T(8,128)(2,1)}, bf16[576,128]{1,0:T(8,128)(2,1)S(1)}, u32[]{:S(2)}) copy-start(bf16[576,128]{1,0:T(8,128)(2,1)S(1)} %collective-permute-done.14.refs_15_) | copy-start | bytes 442372
  26.4 27.2 %copy-start.6 = (bf16[576,128]{1,0:T(8,128)(2,1)}, bf16[576,128]{1,0:T(8,128)(2,1)S(1)}, u32[]{:S(2)}) copy-start(bf16[576,128]{1,0:T(8,128)(2,1)S(1)} %collective-permute-done.12.refs_13_) | copy-start | bytes 442372
  27.0 1.1 copy-start.1
  29.8 23.9 %copy-start.8 = (bf16[576,128]{1,0:T(8,128)(2,1)}, bf16[576,128]{1,0:T(8,128)(2,1)S(1)}, u32[]{:S(2)}) copy-start(bf16[576,128]{1,0:T(8,128)(2,1)S(1)} %collective-permute-done.10.refs_11_) | copy-start | bytes 442372
  54.7 39.2 %collective-permute-start.15 = (bf16[4608,128]{1,0:T(8,128)(2,1)S(1)}, bf16[4608,128]{1,0:T(8,128)(2,1)S(1)}, u32[]{:S(2)}, u32[]{:S(2)}) collective-permute-start(bf16[4608,128]{1,0:T(8,128)(2,1)S(1)} %get-tuple-element.13), channel_id=1, source_target_pairs={{2,0},{0,2},{6,4},{4,6},{10,8},{8,10},{14,12},{12,14},{18,16},{16,... | collective-permute-start | bytes 3538952 | tf_op jit(solution)/shard_map/ppermute | solution.py:339
  54.9 6.7 %collective-permute-start.23 = (bf16[576,128]{1,0:T(8,128)(2,1)S(1)}, bf16[576,128]{1,0:T(8,128)(2,1)S(1)}, u32[]{:S(2)}, u32[]{:S(2)}) collective-permute-start(bf16[576,128]{1,0:T(8,128)(2,1)S(1)} %bitcast.9), channel_id=1, source_target_pairs={{0,1},{1,0},{2,3},{3,2},{4,5},{5,4},{6,7},{7,6},{8,9},{9,8},{10,11... | collective-permute-start | bytes 442376 | tf_op jit(solution)/shard_map/ppermute | solution.py:342
  56.4 68.7 %collective-permute-start.39 = (bf16[128,3072]{1,0:T(8,128)(2,1)S(1)}, bf16[128,3072]{1,0:T(8,128)(2,1)S(1)}, u32[]{:S(2)}, u32[]{:S(2)}) collective-permute-start(bf16[128,3072]{1,0:T(8,128)(2,1)S(1)} %get-tuple-element.18.refs_32_), channel_id=1, source_target_pairs={{0,1},{1,0},{2,3},{3,2},{4,5},{5,4},{6,7},{7,6},{8,9},{9,8},{10,11... | collective-permute-start | bytes 2359304 | tf_op jit(solution)/shard_map/ppermute | solution.py:342
  61.6 35.6 %copy-start.10 = (bf16[576,128]{1,0:T(8,128)(2,1)}, bf16[576,128]{1,0:T(8,128)(2,1)S(1)}, u32[]{:S(2)}) copy-start(bf16[576,128]{1,0:T(8,128)(2,1)S(1)} %collective-permute-done.23.refs_16_) | copy-start | bytes 442372
  61.6 2.0 %collective-permute-start.31 = (bf16[576,128]{1,0:T(8,128)(2,1)S(1)}, bf16[576,128]{1,0:T(8,128)(2,1)S(1)}, u32[]{:S(2)}, u32[]{:S(2)}) collective-permute-start(bf16[576,128]{1,0:T(8,128)(2,1)S(1)} %collective-permute-done.23.refs_16_), channel_id=1, source_target_pairs={{2,0},{0,2},{6,4},{4,6},{10,8},{8,10},{14,12},{12,14},{18,16},{16,... | collective-permute-start | bytes 442376 | tf_op jit(solution)/shard_map/ppermute | solution.py:339
  61.6 20.0 %collective-permute-start.29 = (bf16[576,128]{1,0:T(8,128)(2,1)S(1)}, bf16[576,128]{1,0:T(8,128)(2,1)S(1)}, u32[]{:S(2)}, u32[]{:S(2)}) collective-permute-start(bf16[576,128]{1,0:T(8,128)(2,1)S(1)} %collective-permute-done.5.refs_6_), channel_id=1, source_target_pairs={{0,1},{1,0},{2,3},{3,2},{4,5},{5,4},{6,7},{7,6},{8,9},{9,8},{10,11... | collective-permute-start | bytes 442376 | tf_op jit(solution)/shard_map/ppermute | solution.py:342
  63.1 21.8 %collective-permute-start.27 = (bf16[576,128]{1,0:T(8,128)(2,1)S(1)}, bf16[576,128]{1,0:T(8,128)(2,1)}, u32[]{:S(2)}, u32[]{:S(2)}) collective-permute-start(bf16[576,128]{1,0:T(8,128)(2,1)S(1)} %collective-permute-done.3.refs_4_), channel_id=1, source_target_pairs={{0,1},{1,0},{2,3},{3,2},{4,5},{5,4},{6,7},{7,6},{8,9},{9,8},{10,11... | collective-permute-start | bytes 442376 | tf_op jit(solution)/shard_map/ppermute | solution.py:342
  64.3 23.7 %collective-permute-start.25 = (bf16[576,128]{1,0:T(8,128)(2,1)S(1)}, bf16[576,128]{1,0:T(8,128)(2,1)}, u32[]{:S(2)}, u32[]{:S(2)}) collective-permute-start(bf16[576,128]{1,0:T(8,128)(2,1)S(1)} %collective-permute-done.1.refs_2_), channel_id=1, source_target_pairs={{0,1},{1,0},{2,3},{3,2},{4,5},{5,4},{6,7},{7,6},{8,9},{9,8},{10,11... | collective-permute-start | bytes 442376 | tf_op jit(solution)/shard_map/ppermute | solution.py:342
  81.6 9.5 %collective-permute-start.24 = (bf16[576,128]{1,0:T(8,128)(2,1)S(1)}, bf16[576,128]{1,0:T(8,128)(2,1)S(1)}, u32[]{:S(2)}, u32[]{:S(2)}) collective-permute-start(bf16[576,128]{1,0:T(8,128)(2,1)S(1)} %collective-permute-done.refs_1_), channel_id=1, source_target_pairs={{0,1},{1,0},{2,3},{3,2},{4,5},{5,4},{6,7},{7,6},{8,9},{9,8},{10,11... | collective-permute-start | bytes 442376 | tf_op jit(solution)/shard_map/ppermute | solution.py:342
  84.9 6.2 %collective-permute-start.37 = (bf16[576,128]{1,0:T(8,128)(2,1)S(1)}, bf16[576,128]{1,0:T(8,128)(2,1)S(1)}, u32[]{:S(2)}, u32[]{:S(2)}) collective-permute-start(bf16[576,128]{1,0:T(8,128)(2,1)S(1)} %collective-permute-done.29.refs_22_), channel_id=1, source_target_pairs={{2,0},{0,2},{6,4},{4,6},{10,8},{8,10},{14,12},{12,14},{18,16},{16,... | collective-permute-start | bytes 442376 | tf_op jit(solution)/shard_map/ppermute | solution.py:339
  88.1 9.1 %collective-permute-start.30 = (bf16[576,128]{1,0:T(8,128)(2,1)S(1)}, bf16[576,128]{1,0:T(8,128)(2,1)}, u32[]{:S(2)}, u32[]{:S(2)}) collective-permute-start(bf16[576,128]{1,0:T(8,128)(2,1)S(1)} %collective-permute-done.6.refs_7_), channel_id=1, source_target_pairs={{0,1},{1,0},{2,3},{3,2},{4,5},{5,4},{6,7},{7,6},{8,9},{9,8},{10,11... | collective-permute-start | bytes 442376 | tf_op jit(solution)/shard_map/ppermute | solution.py:342
  91.1 6.7 %collective-permute-start.35 = (bf16[576,128]{1,0:T(8,128)(2,1)}, bf16[576,128]{1,0:T(8,128)(2,1)}, u32[]{:S(2)}, u32[]{:S(2)}) collective-permute-start(bf16[576,128]{1,0:T(8,128)(2,1)} %collective-permute-done.27.refs_20_), channel_id=1, source_target_pairs={{2,0},{0,2},{6,4},{4,6},{10,8},{8,10},{14,12},{12,14},{18,16},{16,... | collective-permute-start | bytes 442376 | tf_op jit(solution)/shard_map/ppermute | solution.py:339
  92.5 6.8 %collective-permute-start.28 = (bf16[576,128]{1,0:T(8,128)(2,1)S(1)}, bf16[576,128]{1,0:T(8,128)(2,1)}, u32[]{:S(2)}, u32[]{:S(2)}) collective-permute-start(bf16[576,128]{1,0:T(8,128)(2,1)S(1)} %collective-permute-done.4.refs_5_), channel_id=1, source_target_pairs={{0,1},{1,0},{2,3},{3,2},{4,5},{5,4},{6,7},{7,6},{8,9},{9,8},{10,11... | collective-permute-start | bytes 442376 | tf_op jit(solution)/shard_map/ppermute | solution.py:342
  95.0 4.8 %collective-permute-start.33 = (bf16[576,128]{1,0:T(8,128)(2,1)}, bf16[576,128]{1,0:T(8,128)(2,1)}, u32[]{:S(2)}, u32[]{:S(2)}) collective-permute-start(bf16[576,128]{1,0:T(8,128)(2,1)} %collective-permute-done.25.refs_18_), channel_id=1, source_target_pairs={{2,0},{0,2},{6,4},{4,6},{10,8},{8,10},{14,12},{12,14},{18,16},{16,... | collective-permute-start | bytes 442376 | tf_op jit(solution)/shard_map/ppermute | solution.py:339
  97.2 6.4 %collective-permute-start.26 = (bf16[576,128]{1,0:T(8,128)(2,1)S(1)}, bf16[576,128]{1,0:T(8,128)(2,1)}, u32[]{:S(2)}, u32[]{:S(2)}) collective-permute-start(bf16[576,128]{1,0:T(8,128)(2,1)S(1)} %collective-permute-done.2.refs_3_), channel_id=1, source_target_pairs={{0,1},{1,0},{2,3},{3,2},{4,5},{5,4},{6,7},{7,6},{8,9},{9,8},{10,11... | collective-permute-start | bytes 442376 | tf_op jit(solution)/shard_map/ppermute | solution.py:342
  97.8 6.9 %collective-permute-start.17 = (bf16[576,128]{1,0:T(8,128)(2,1)}, bf16[576,128]{1,0:T(8,128)(2,1)S(1)}, u32[]{:S(2)}, u32[]{:S(2)}) collective-permute-start(bf16[576,128]{1,0:T(8,128)(2,1)} %get-tuple-element.15), channel_id=1, source_target_pairs={{4,0},{6,2},{0,4},{2,6},{12,8},{14,10},{8,12},{10,14},{20,16},{22,... | collective-permute-start | bytes 442376 | tf_op jit(solution)/shard_map/ppermute | solution.py:339
  99.3 8.7 %collective-permute-start.19 = (bf16[576,128]{1,0:T(8,128)(2,1)}, bf16[576,128]{1,0:T(8,128)(2,1)}, u32[]{:S(2)}, u32[]{:S(2)}) collective-permute-start(bf16[576,128]{1,0:T(8,128)(2,1)} %get-tuple-element.16), channel_id=1, source_target_pairs={{4,0},{6,2},{0,4},{2,6},{12,8},{14,10},{8,12},{10,14},{20,16},{22,... | collective-permute-start | bytes 442376 | tf_op jit(solution)/shard_map/ppermute | solution.py:339
  99.8 10.6 %collective-permute-start.21 = (bf16[576,128]{1,0:T(8,128)(2,1)}, bf16[576,128]{1,0:T(8,128)(2,1)}, u32[]{:S(2)}, u32[]{:S(2)}) collective-permute-start(bf16[576,128]{1,0:T(8,128)(2,1)} %get-tuple-element.17), channel_id=1, source_target_pairs={{4,0},{6,2},{0,4},{2,6},{12,8},{14,10},{8,12},{10,14},{20,16},{22,... | collective-permute-start | bytes 442376 | tf_op jit(solution)/shard_map/ppermute | solution.py:339
  103.6 12.1 %collective-permute-start.32 = (bf16[576,128]{1,0:T(8,128)(2,1)}, bf16[576,128]{1,0:T(8,128)(2,1)}, u32[]{:S(2)}, u32[]{:S(2)}) collective-permute-start(bf16[576,128]{1,0:T(8,128)(2,1)} %copy-done.16), channel_id=1, source_target_pairs={{2,0},{0,2},{6,4},{4,6},{10,8},{8,10},{14,12},{12,14},{18,16},{16,... | collective-permute-start | bytes 442376 | tf_op jit(solution)/shard_map/ppermute | solution.py:339
  104.7 5.7 %copy-start.23 = (bf16[576,128]{1,0:T(8,128)(2,1)}, bf16[576,128]{1,0:T(8,128)(2,1)S(1)}, u32[]{:S(2)}) copy-start(bf16[576,128]{1,0:T(8,128)(2,1)S(1)} %collective-permute-done.17.refs_2_) | copy-start | bytes 442372
  104.7 12.5 %collective-permute-start.38 = (bf16[576,128]{1,0:T(8,128)(2,1)}, bf16[576,128]{1,0:T(8,128)(2,1)}, u32[]{:S(2)}, u32[]{:S(2)}) collective-permute-start(bf16[576,128]{1,0:T(8,128)(2,1)} %collective-permute-done.30.refs_23_), channel_id=1, source_target_pairs={{2,0},{0,2},{6,4},{4,6},{10,8},{8,10},{14,12},{12,14},{18,16},{16,... | collective-permute-start | bytes 442376 | tf_op jit(solution)/shard_map/ppermute | solution.py:339
  108.0 12.5 %collective-permute-start.36 = (bf16[576,128]{1,0:T(8,128)(2,1)}, bf16[576,128]{1,0:T(8,128)(2,1)}, u32[]{:S(2)}, u32[]{:S(2)}) collective-permute-start(bf16[576,128]{1,0:T(8,128)(2,1)} %collective-permute-done.28.refs_21_), channel_id=1, source_target_pairs={{2,0},{0,2},{6,4},{4,6},{10,8},{8,10},{14,12},{12,14},{18,16},{16,... | collective-permute-start | bytes 442376 | tf_op jit(solution)/shard_map/ppermute | solution.py:339
  110.4 12.1 %collective-permute-start.34 = (bf16[576,128]{1,0:T(8,128)(2,1)}, bf16[576,128]{1,0:T(8,128)(2,1)}, u32[]{:S(2)}, u32[]{:S(2)}) collective-permute-start(bf16[576,128]{1,0:T(8,128)(2,1)} %collective-permute-done.26.refs_19_), channel_id=1, source_target_pairs={{2,0},{0,2},{6,4},{4,6},{10,8},{8,10},{14,12},{12,14},{18,16},{16,... | collective-permute-start | bytes 442376 | tf_op jit(solution)/shard_map/ppermute | solution.py:339
  113.9 11.2 %copy-start.3 = (bf16[128,576]{0,1:T(8,128)(2,1)S(1)}, bf16[128,576]{0,1:T(8,128)(2,1)}, u32[]{:S(2)}) copy-start(bf16[128,576]{0,1:T(8,128)(2,1)} %param.7) | copy-start | bytes 442372
  113.9 11.2 %copy-start.21 = (s32[24,20]{1,0:T(8,128)S(1)}, s32[24,20]{1,0:T(8,128)}, u32[]{:S(2)}) copy-start(s32[24,20]{1,0:T(8,128)} %rows_s.3) | copy-start | bytes 5764
  115.7 28.5 %collective-permute-start.16 = (bf16[576,128]{1,0:T(8,128)(2,1)}, bf16[576,128]{1,0:T(8,128)(2,1)}, u32[]{:S(2)}, u32[]{:S(2)}) collective-permute-start(bf16[576,128]{1,0:T(8,128)(2,1)} %get-tuple-element.14), channel_id=1, source_target_pairs={{4,0},{6,2},{0,4},{2,6},{12,8},{14,10},{8,12},{10,14},{20,16},{22,... | collective-permute-start | bytes 442376 | tf_op jit(solution)/shard_map/ppermute | solution.py:339
  117.2 27.0 %collective-permute-start.18 = (bf16[576,128]{1,0:T(8,128)(2,1)}, bf16[576,128]{1,0:T(8,128)(2,1)}, u32[]{:S(2)}, u32[]{:S(2)}) collective-permute-start(bf16[576,128]{1,0:T(8,128)(2,1)} %add_parts.6), channel_id=1, source_target_pairs={{24,0},{26,2},{28,4},{30,6},{0,8},{2,10},{4,12},{6,14},{8,16},{10,... | collective-permute-start | bytes 442376 | tf_op jit(solution)/shard_map/ppermute | solution.py:339
  120.5 23.8 %collective-permute-start.20 = (bf16[576,128]{1,0:T(8,128)(2,1)}, bf16[576,128]{1,0:T(8,128)(2,1)}, u32[]{:S(2)}, u32[]{:S(2)}) collective-permute-start(bf16[576,128]{1,0:T(8,128)(2,1)} %add_parts.7), channel_id=1, source_target_pairs={{16,0},{18,2},{20,4},{22,6},{24,8},{26,10},{28,12},{30,14},{0,16},... | collective-permute-start | bytes 442376 | tf_op jit(solution)/shard_map/ppermute | solution.py:339
  122.5 21.8 %collective-permute-start.22 = (bf16[576,128]{1,0:T(8,128)(2,1)}, bf16[576,128]{1,0:T(8,128)(2,1)}, u32[]{:S(2)}, u32[]{:S(2)}) collective-permute-start(bf16[576,128]{1,0:T(8,128)(2,1)} %add_parts.8), channel_id=1, source_target_pairs={{8,0},{10,2},{12,4},{14,6},{16,8},{18,10},{20,12},{22,14},{24,16},... | collective-permute-start | bytes 442376 | tf_op jit(solution)/shard_map/ppermute | solution.py:339
  (16 other events, 13.7 us)

commit v2 on v0

v2 whole, which is shorter than its diff:
```python
import functools

import jax
import jax.numpy as jnp
import numpy as np
from jax import lax
from jax.experimental import pallas as pl
from jax.experimental.pallas import tpu as pltpu
from jax.sharding import PartitionSpec as P

CORES = 2
SIDES = 2
MAX_LINE = 8


SQRT_2_PI = float(np.sqrt(2.0 / np.pi))
CUBIC = 0.044715

VMEM = pl.BlockSpec(memory_space=pltpu.VMEM)
HBM = pl.BlockSpec(memory_space=pltpu.HBM)
DMA = pltpu.SemaphoreType.DMA
MARGIN = 4 << 20
ROOM = 60 * 1024 * 1024


def grant(*shapes):
    return MARGIN + sum(int(np.prod(s)) * np.dtype(d).itemsize for s, d in shapes)


def shards_of(refs, part):
    for ref in refs:
        for i in range(ref.shape[0] // part):
            yield ref.at[i * part : (i + 1) * part, :]


def block(r, side):
    return pl.ds(pl.multiple_of(r * side, side), side)


def forward_kernel(n_in, n_out, part, rows_s, offs_s, *refs):
    x_refs, refs = refs[:n_in], refs[n_in:]
    w_ref, cot, gelu_ref, slopes = refs[:4]
    dx_refs, (xt, xs, acc, gelu, w, out_sem, w_sem) = refs[4 : 4 + n_out], refs[4 + n_out :]
    cols, slots, side, _ = w.shape
    blocks = xs.shape[0]

    def out(c):
        target = gelu_ref.at[:, block(c, side)]
        return pltpu.make_async_copy(gelu.at[c], target, out_sem.at[c])

    def weights(c):
        return pltpu.make_async_copy(w_ref.at[c], w.at[c], w_sem.at[c])

    def load(c, carry):
        weights(c).start()
        return carry

    lax.fori_loop(0, cols, load, 0)
    for j, shard in enumerate(shards_of(x_refs, part)):
        xt[pl.ds(pl.multiple_of(offs_s[j], 16), part), :] = shard[...]

    def turn(r, carry):
        xs[r] = xt[block(r, side), :].T
        acc[r] = jnp.zeros(acc.shape[1:], acc.dtype)
        return carry

    lax.fori_loop(0, blocks, turn, 0, unroll=4)
    step = 2 if slots % 2 == 0 else 1

    def ahead(c):
        v = 0.0
        for k in range(0, slots, step):
            picked = jnp.concatenate([xs[rows_s[c, k + i]] for i in range(step)], axis=1)
            right = w[c, k : k + step].reshape(step * side, side)
            v = v + jnp.dot(picked, right, preferred_element_type=jnp.float32)
        v2 = v * v
        t = jnp.tanh(SQRT_2_PI * (v + CUBIC * (v * v2)))
        half = 0.5 * (1.0 + t)
        gelu[c] = (v * half).astype(gelu.dtype)
        slope = half + (0.5 * v) * (1.0 - t * t) * (SQRT_2_PI * (1.0 + (3.0 * CUBIC) * v2))
        slope = cot[:, block(c, side)].astype(jnp.float32) * slope
        slopes[:, block(c, side)] = slope.astype(slopes.dtype)

    def back(c):
        turned = slopes[:, block(c, side)].T
        for k in range(0, slots, step):
            left = w[c, k : k + step].reshape(step * side, side)
            part_sum = jnp.dot(left, turned, preferred_element_type=jnp.float32)
            for i in range(step):
                acc[rows_s[c, k + i]] += part_sum[i * side : (i + 1) * side, :]

    def one(c, carry):
        out(c).start()
        weights(c + 1).wait()
        ahead(c + 1)
        back(c)
        return carry

    weights(0).wait()
    ahead(0)
    lax.fori_loop(0, cols - 1, one, 0)
    out(cols - 1).start()
    back(cols - 1)

    def narrow(r, carry):
        xt[block(r, side), :] = acc[r].astype(xt.dtype)
        return carry

    lax.fori_loop(0, blocks, narrow, 0, unroll=4)
    for j, shard in enumerate(shards_of(dx_refs, part)):
        shard[...] = xt[pl.ds(pl.multiple_of(offs_s[j], 16), part), :]

    def drain(c, carry):
        out(c).wait()
        return carry

    lax.fori_loop(0, cols, drain, 0)


def forward(arrays, part, offs, weights, rows, cot, outs):
    cols, _, side, _ = weights.shape
    tokens = arrays[0].shape[1]
    features = sum(a.shape[0] for a in arrays)
    blocks = features // side
    scratch = [
        ((features, tokens), jnp.bfloat16),
        ((blocks, tokens, side), jnp.bfloat16),
        ((blocks, side, tokens), jnp.float32),
        ((cols, tokens, side), jnp.bfloat16),
        (weights.shape, jnp.bfloat16),
    ]
    return pl.pallas_call(
        functools.partial(forward_kernel, len(arrays), len(outs), part),
        grid_spec=pltpu.PrefetchScalarGridSpec(
            num_scalar_prefetch=2,
            in_specs=[VMEM] * len(arrays) + [HBM, VMEM],
            out_specs=[HBM, VMEM] + [VMEM] * len(outs),
            scratch_shapes=[pltpu.VMEM(*s) for s in scratch] + [DMA((cols,))] * 2,
        ),
        out_shape=[jax.ShapeDtypeStruct((tokens, cols * side), jnp.bfloat16)] * 2
        + [jax.ShapeDtypeStruct((m * part, tokens), jnp.bfloat16) for m in outs],
        compiler_params=pltpu.CompilerParams(
            vmem_limit_bytes=max(grant(*scratch), min(ROOM - 2 * weights.size, 48 << 20))
        ),
        cost_estimate=pl.CostEstimate(
            flops=4 * tokens * weights.size,
            bytes_accessed=2 * weights.size,
            transcendentals=tokens * cols * side,
        ),
        name="forward",
    )(rows, offs, *arrays, weights, cot)


def weight_kernel(n_planes, n_in, part, rows_s, offs_s, half_s, *refs):
    x_refs, refs = refs[: n_planes * n_in], refs[n_planes * n_in :]
    slope_refs, (out_ref, xt, out, out_sem) = refs[:n_planes], refs[n_planes:]
    cols, slots, side, _ = out.shape
    tokens = slope_refs[0].shape[0]

    def result(c):
        return pltpu.make_async_copy(out.at[c], out_ref.at[c], out_sem.at[c])

    for p in range(n_planes):
        for j, shard in enumerate(shards_of(x_refs[p * n_in : (p + 1) * n_in], part)):
            rows = pl.ds(pl.multiple_of(offs_s[j], 16), part)
            xt[rows, p * tokens : (p + 1) * tokens] = shard[...]

    def one(c, carry):
        right = jnp.concatenate([ref[:, block(c, side)] for ref in slope_refs], axis=0)
        for k in range(slots):
            left = xt[block(rows_s[c, half_s[0] * slots + k], side), :]
            out[c, k] = jnp.dot(left, right, preferred_element_type=jnp.float32)
        result(c).start()
        return carry

    lax.fori_loop(0, cols, one, 0, unroll=4 if cols % 4 == 0 else 1)

    def drain(c, carry):
        result(c).wait()
        return carry

    lax.fori_loop(0, cols, drain, 0)


def weight_grad(planes, part, offs, slopes, rows, half, slots, side):
    cols = rows.shape[0]
    tokens = slopes[0].shape[0]
    features = sum(a.shape[0] for a in planes[0])
    arrays = [a for plane in planes for a in plane]
    scratch = [
        ((features, len(planes) * tokens), jnp.bfloat16),
        ((cols, slots, side, side), jnp.float32),
    ]
    return pl.pallas_call(
        functools.partial(weight_kernel, len(planes), len(planes[0]), part),
        grid_spec=pltpu.PrefetchScalarGridSpec(
            num_scalar_prefetch=3,
            in_specs=[VMEM] * (len(arrays) + len(slopes)),
            out_specs=HBM,
            scratch_shapes=[pltpu.VMEM(*s) for s in scratch] + [DMA((cols,))],
        ),
        out_shape=jax.ShapeDtypeStruct((cols, slots, side, side), jnp.float32),
        compiler_params=pltpu.CompilerParams(vmem_limit_bytes=grant(*scratch)),
        cost_estimate=pl.CostEstimate(
            flops=2 * len(planes) * tokens * cols * slots * side * side,
            bytes_accessed=4 * cols * slots * side * side,
            transcendentals=0,
        ),
        name="weight_grad",
    )(rows, offs, half, *arrays, *slopes)


def pack_kernel(*refs):
    out, start = refs[-1], 0
    for ref in refs[:-1]:
        out[start : start + ref.shape[0], :] = ref[...]
        start += ref.shape[0]


def pack(arrays):
    rows = sum(a.shape[0] for a in arrays)
    return pl.pallas_call(
        pack_kernel,
        in_specs=[VMEM] * len(arrays),
        out_specs=VMEM,
        out_shape=jax.ShapeDtypeStruct((rows, arrays[0].shape[1]), arrays[0].dtype),
        compiler_params=pltpu.CompilerParams(vmem_limit_bytes=MARGIN),
        name="pack",
    )(*arrays)


def sum_kernel(plan, part, n_in, *refs):
    ins, outs = refs[:n_in], refs[n_in:]
    for terms, out in zip(plan, outs):
        total = 0.0
        for a, i in terms:
            total = total + ins[a][i * part : (i + 1) * part, :].astype(jnp.float32)
        out[...] = total.astype(out.dtype)


def add_parts(arrays, plan, part):
    tokens = arrays[0].shape[1]
    return pl.pallas_call(
        functools.partial(sum_kernel, plan, part, len(arrays)),
        in_specs=[VMEM] * len(arrays),
        out_specs=[VMEM] * len(plan),
        out_shape=[jax.ShapeDtypeStruct((part, tokens), jnp.bfloat16)] * len(plan),
        compiler_params=pltpu.CompilerParams(vmem_limit_bytes=MARGIN),
        name="add_parts",
    )(*arrays)


def direct(n, mp):
    return n % (CORES * SIDES) == 0 and n // (CORES * SIDES) <= MAX_LINE and mp == 2


def body(activations, block_values, block_rows, cotangent):
    n, mp = lax.axis_size("dp"), lax.axis_size("mp")
    me, half = lax.axis_index("dp"), lax.axis_index("mp")
    side, slot_count = block_values.shape[2], block_values.shape[1]
    own = activations.T
    part, _ = own.shape
    half = half.astype(jnp.int32).reshape(1)
    chip = CORES * SIDES
    line = n // chip
    if not direct(n, mp):
        offs = jnp.zeros((1,), jnp.int32)
        x_own = lax.all_gather(own, "dp", axis=0, tiled=True)
        x_all = lax.all_gather(x_own, "mp", axis=0)
        whole = x_own.shape[0]
        gelu_out, slopes, dx = forward(
            [x_own], whole, offs, block_values, block_rows, cotangent, [1]
        )
        slopes_all = lax.all_gather(slopes, "mp", axis=0)
        block_grad = weight_grad(
            [[x_all[p]] for p in range(mp)],
            whole,
            offs,
            [slopes_all[p] for p in range(mp)],
            block_rows,
            half,
            slot_count // mp,
            side,
        )
        dx = dx.astype(jnp.float32)
        dx = lax.psum_scatter(dx, "dp", scatter_dimension=0, tiled=True)
        return gelu_out, dx.astype(jnp.bfloat16).T, block_grad

    def permute(a, k, s, q):
        def source(i):
            z, x, core = i // chip, i // CORES % SIDES, i % CORES
            return ((z + k) % line * SIDES + (x ^ s)) * CORES + (core ^ q)

        return lax.ppermute(a, "dp", [(source(i), i) for i in range(n)])

    def across(a):
        return lax.ppermute(a, "mp", [(i, i ^ 1) for i in range(mp)])

    rel = [(k, s, q) for q in range(CORES) for s in range(SIDES) for k in range(line)]
    ks, ss, qs = (np.array(v, np.int32) for v in zip(*rel))
    z, x, core = me // chip, me // CORES % SIDES, me % CORES
    offs = (((z + ks) % line * SIDES + (x ^ ss)) * CORES + (core ^ qs)) * part
    offs = offs.astype(jnp.int32)

    near = [permute(own, k, 0, 0) if k else own for k in range(line)]
    side_x = [permute(a, 0, 1, 0) for a in near]
    x_own, x_far = [], []
    for s, arrays in enumerate((near, side_x)):
        x_own.append(pack(arrays))
        x_far.append(across(x_own[s]))
    for s in range(SIDES):
        x_own.append(permute(x_own[s], 0, 0, 1))
        x_far.append(permute(x_far[s], 0, 0, 1))

    gelu_out, slopes, keep0, keep1, give0, give1 = forward(
        x_own, part, offs, block_values, block_rows, cotangent, [line] * 4
    )
    got1 = permute(give1, 0, 0, 1)
    got0 = permute(give0, 0, 0, 1)
    slopes_far = across(slopes)
    chips = add_parts([keep1, got1], [[(0, k), (1, k)] for k in range(line)], part)
    pairs = [permute(a, 0, 1, 0) for a in chips]
    total = (
        keep0[:part].astype(jnp.float32)
        + got0[:part].astype(jnp.float32)
        + pairs[0].astype(jnp.float32)
    )
    for k in range(1, line):
        (mine,) = add_parts([keep0, got0, pairs[k]], [[(0, k), (1, k), (2, 0)]], part)
        total = total + permute(mine, line - k, 0, 0).astype(jnp.float32)
    block_grad = weight_grad(
        [x_own, x_far],
        part,
        offs,
        [slopes, slopes_far],
        block_rows,
        half,
        slot_count // mp,
        side,
    )
    return gelu_out, total.astype(jnp.bfloat16).T, block_grad


def solution(mesh):
    in_specs = (P("mp", "dp"), P("dp", None, None, None), P("dp", None), P("mp", "dp"))
    out_specs = (P("mp", "dp"), P("mp", "dp"), P("dp", "mp", None, None))
    return jax.shard_map(
        body, mesh=mesh, in_specs=in_specs, out_specs=out_specs, check_vma=False
    )
```

time: 460 us -> 87.2 us (0.19)
  waiting for transfers between devices: 228 us -> 18 us
  local copies, waits for them, and re-layouts: 105 us -> 4.99 us
  matrix products: 85.8 us -> 0 us
  Pallas kernels: 0 us -> 34.4 us
  starting transfers between devices: 9.49 us -> 27.1 us
  other arithmetic: 16.3 us -> 1.51 us
  between operations: 13.8 us -> 0.82 us
    all_to_all x1 -> x0, waiting for transfers between devices: 157 us -> none  [body(): lax.all_to_all(outgoing, 'mp', split_axis=0, concat_axis=0, tiled=True)]
    dot_general x4 -> x0, matrix products: 85.8 us -> none  [the longest x1 40.7 us: body(): jnp.einsum('tmi,mr->tri', contrib, one_hot, precision=lax.Precision.HIGHEST)]
    all_gather x2 -> x0, waiting for transfers between devices: 41.6 us -> none  [the longest x1 41.6 us: body(): x_full = lax.all_gather(activations, 'dp', axis=1, tiled=True)]
    reshape x6 -> x0, local copies, waits for them, and re-layouts: 36 us -> none  [the longest x1 25.3 us: body(): incoming.reshape(mp_size * rows_here, col_blocks, per_peer, block_size)]
    pallas_call x0 -> x8, Pallas kernels: none -> 34.4 us  [the longest x1 21.8 us: forward(): pl.pallas_call(functools.partial(forward_kernel, len(arrays), len(outs),...]
    all_to_all x1 -> x0, local copies, waits for them, and re-layouts: 29.1 us -> none  [body(): lax.all_to_all(outgoing, 'mp', split_axis=0, concat_axis=0, tiled=True)]
    reduce_scatter x1 -> x0, waiting for transfers between devices: 28.2 us -> none  [body(): lax.psum_scatter(dx_term, 'dp', scatter_dimension=1, tiled=True)]
    ppermute x0 -> x23, starting transfers between devices: none -> 27.1 us  [the longest x20 23.5 us: permute(): return lax.ppermute(a, 'dp', [(source(i), i) for i in range(n)])]
  transfers between devices with their start and end apart: 4 -> 23, of which waited for: 3 -> 7; matrix products, arithmetic and copies ran while one was open for 21% -> 1% of each run, Pallas kernels for 0% -> 40%
where the time goes in v2:
time: 87.2 us; the launch traced here: 86.9 us
  Pallas kernels  34.4 us (39%)
  starting transfers between devices  27.1 us (31%)
  waiting for transfers between devices  18 us (21%)
  local copies, waits for them, and re-layouts  4.99 us (6%)
  other arithmetic  1.51 us (2%)
    ppermute x20, starting transfers between devices, permute(): return lax.ppermute(a, 'dp', [(source(i), i) for i in range(n)])  23.5 us
    pallas_call x1, Pallas kernels, forward(): pl.pallas_call(functools.partial(forward_kernel, len(arrays), len(outs),...  21.8 us
    ppermute x20, waiting for transfers between devices, permute(): return lax.ppermute(a, 'dp', [(source(i), i) for i in range(n)])  17.5 us
    pallas_call x1, Pallas kernels, weight_grad(): pl.pallas_call(functools.partial(weight_kernel, len(planes), len(planes[0...  9.78 us
    unnamed x14, local copies, waits for them, and re-layouts  4.99 us
    ppermute x3, starting transfers between devices, across(): return lax.ppermute(a, 'mp', [(i, i ^ 1) for i in range(mp)])  3.65 us
    pallas_call x4, Pallas kernels, add_parts(): pl.pallas_call(functools.partial(sum_kernel, plan, part, len(arrays)), in...  2.77 us
  transfers between devices with their start and end apart: 23, of which 7 were waited for; matrix products, arithmetic and copies ran while one was open for 1% of the time, Pallas kernels for 40%

profile of v2, /device:TPU:0, one launch (start us, length us, event | category | flops | bytes accessed | tf_op | source)
XLA Modules:
  0.0 86.9 jit_solution(10054472661953836586)
XLA Ops:
  0.6 3.1 %collective-permute-start.2 = (bf16[576,128]{1,0:T(8,128)(2,1)}, bf16[576,128]{1,0:T(8,128)(2,1)S(1)}, u32[]{:S(2)}, u32[]{:S(2)}) collective-permute-start(bf16[576,128]{1,0:T(8,128)(2,1)} %bitcast.4), channel_id=1, source_target_pairs={{24,0},{26,2},{28,4},{30,6},{0,8},{2,10},{4,12},{6,14},{8,16},{10,... | collective-permute-start | bytes 442376 | tf_op jit(solution)/shard_map/ppermute | solution.py:294
  3.7 2.6 %collective-permute-start.1 = (bf16[576,128]{1,0:T(8,128)(2,1)}, bf16[576,128]{1,0:T(8,128)(2,1)S(1)}, u32[]{:S(2)}, u32[]{:S(2)}) collective-permute-start(bf16[576,128]{1,0:T(8,128)(2,1)} %bitcast.5), channel_id=1, source_target_pairs={{16,0},{18,2},{20,4},{22,6},{24,8},{26,10},{28,12},{30,14},{0,16},... | collective-permute-start | bytes 442376 | tf_op jit(solution)/shard_map/ppermute | solution.py:294
  6.3 1.3 %collective-permute-start = (bf16[576,128]{1,0:T(8,128)(2,1)}, bf16[576,128]{1,0:T(8,128)(2,1)S(1)}, u32[]{:S(2)}, u32[]{:S(2)}) collective-permute-start(bf16[576,128]{1,0:T(8,128)(2,1)} %bitcast.6), channel_id=1, source_target_pairs={{8,0},{10,2},{12,4},{14,6},{16,8},{18,10},{20,12},{22,14},{24,16},... | collective-permute-start | bytes 442376 | tf_op jit(solution)/shard_map/ppermute | solution.py:294
  7.7 1.5 %collective-permute-start.3 = (bf16[576,128]{1,0:T(8,128)(2,1)}, bf16[576,128]{1,0:T(8,128)(2,1)S(1)}, u32[]{:S(2)}, u32[]{:S(2)}) collective-permute-start(bf16[576,128]{1,0:T(8,128)(2,1)} %bitcast.7), channel_id=1, source_target_pairs={{4,0},{6,2},{0,4},{2,6},{12,8},{14,10},{8,12},{10,14},{20,16},{22,... | collective-permute-start | bytes 442376 | tf_op jit(solution)/shard_map/ppermute | solution.py:294
  9.2 1.6 %collective-permute-done.2.refs_3_ = bf16[576,128]{1,0:T(8,128)(2,1)S(1)} collective-permute-done((bf16[576,128]{1,0:T(8,128)(2,1)}, bf16[576,128]{1,0:T(8,128)(2,1)S(1)}, u32[]{:S(2)}, u32[]{:S(2)}) %collective-permute-start.2) | collective-permute-done | bytes 147488 | tf_op jit(solution)/shard_map/ppermute | solution.py:294
  10.8 1.7 %collective-permute-start.6 = (bf16[576,128]{1,0:T(8,128)(2,1)S(1)}, bf16[576,128]{1,0:T(8,128)(2,1)S(1)}, u32[]{:S(2)}, u32[]{:S(2)}) collective-permute-start(bf16[576,128]{1,0:T(8,128)(2,1)S(1)} %collective-permute-done.2.refs_3_), channel_id=1, source_target_pairs={{4,0},{6,2},{0,4},{2,6},{12,8},{14,10},{8,12},{10,14},{20,16},{22,... | collective-permute-start | bytes 442376 | tf_op jit(solution)/shard_map/ppermute | solution.py:294
  12.5 3.8 %collective-permute-done.1.refs_2_ = bf16[576,128]{1,0:T(8,128)(2,1)S(1)} collective-permute-done((bf16[576,128]{1,0:T(8,128)(2,1)}, bf16[576,128]{1,0:T(8,128)(2,1)S(1)}, u32[]{:S(2)}, u32[]{:S(2)}) %collective-permute-start.1) | collective-permute-done | bytes 147488 | tf_op jit(solution)/shard_map/ppermute | solution.py:294
  16.2 1.5 %collective-permute-start.5 = (bf16[576,128]{1,0:T(8,128)(2,1)S(1)}, bf16[576,128]{1,0:T(8,128)(2,1)S(1)}, u32[]{:S(2)}, u32[]{:S(2)}) collective-permute-start(bf16[576,128]{1,0:T(8,128)(2,1)S(1)} %collective-permute-done.1.refs_2_), channel_id=1, source_target_pairs={{4,0},{6,2},{0,4},{2,6},{12,8},{14,10},{8,12},{10,14},{20,16},{22,... | collective-permute-start | bytes 442376 | tf_op jit(solution)/shard_map/ppermute | solution.py:294
  17.7 0.0 collective-permute-done.refs_1_
  17.7 0.5 collective-permute-start.4
  18.3 0.9 %copy-done.1 = bf16[128,576]{0,1:T(8,128)(2,1)S(1)} copy-done((bf16[128,576]{0,1:T(8,128)(2,1)S(1)}, bf16[128,576]{0,1:T(8,128)(2,1)}, u32[]{:S(2)}) %copy-start.1) | copy-done | bytes 147480
  19.2 0.1 collective-permute-start.7
  19.3 0.0 collective-permute-done.3.refs_0_
  19.3 0.0 collective-permute-done.6.refs_3_
  19.3 3.6 %collective-permute-done.5.refs_2_ = bf16[576,128]{1,0:T(8,128)(2,1)S(1)} collective-permute-done((bf16[576,128]{1,0:T(8,128)(2,1)S(1)}, bf16[576,128]{1,0:T(8,128)(2,1)S(1)}, u32[]{:S(2)}, u32[]{:S(2)}) %collective-permute-start.5) | collective-permute-done | bytes 147488 | tf_op jit(solution)/shard_map/ppermute | solution.py:294
  23.0 2.1 %collective-permute-done.4.refs_1_ = bf16[576,128]{1,0:T(8,128)(2,1)S(1)} collective-permute-done((bf16[576,128]{1,0:T(8,128)(2,1)S(1)}, bf16[576,128]{1,0:T(8,128)(2,1)S(1)}, u32[]{:S(2)}, u32[]{:S(2)}) %collective-permute-start.4) | collective-permute-done | bytes 147488 | tf_op jit(solution)/shard_map/ppermute | solution.py:294
  25.1 0.1 collective-permute-start.8
  25.2 0.7 fusion.6.offs_s
  25.9 1.6 %collective-permute-start.18 = (bf16[2304,128]{1,0:T(8,128)(2,1)S(1)}, bf16[2304,128]{1,0:T(8,128)(2,1)}, u32[]{:S(2)}, u32[]{:S(2)}) collective-permute-start(bf16[2304,128]{1,0:T(8,128)(2,1)S(1)} %pack.2.refs_0_), channel_id=1, source_target_pairs={{0,1},{1,0},{2,3},{3,2},{4,5},{5,4},{6,7},{7,6},{8,9},{9,8},{10,11... | collective-permute-start | bytes 1769480 | tf_op jit(solution)/shard_map/ppermute | solution.py:297
  27.5 0.5 collective-permute-start.19
  28.0 0.0 collective-permute-done.8.refs_3_
  28.0 1.1 %copy-done = bf16[128,3072]{1,0:T(8,128)(2,1)S(1)} copy-done((bf16[128,3072]{1,0:T(8,128)(2,1)S(1)}, bf16[128,3072]{1,0:T(8,128)(2,1)}, u32[]{:S(2)}) %copy-start) | copy-done | bytes 786456
  29.2 0.7 copy-done.4
  29.9 21.8 %forward.1 = (bf16[128,3072]{1,0:T(8,128)(2,1)}, bf16[128,3072]{1,0:T(8,128)(2,1)}, bf16[2304,128]{1,0:T(8,128)(2,1)S(1)}, bf16[2304,128]{1,0:T(8,128)(2,1)S(1)}...) custom-call(s32[24,20]{1,0:T(8,128)S(1)} %copy-done.4, s32[16]{0:T(128)S(1)} %fusion.6.offs_s, ...), custom_call_target="tpu_custom_call" | custom-call | flops 4026531840 | bytes 15728640 | tf_op jit(solution)/shard_map/forward/pallas_call | solution.py:132
  51.7 0.1 collective-permute-start.10
  51.8 1.6 %collective-permute-start.22 = (bf16[128,3072]{1,0:T(8,128)(2,1)}, bf16[128,3072]{1,0:T(8,128)(2,1)}, u32[]{:S(2)}, u32[]{:S(2)}) collective-permute-start(bf16[128,3072]{1,0:T(8,128)(2,1)} %get-tuple-element.22.refs_8_), channel_id=1, source_target_pairs={{0,1},{1,0},{2,3},{3,2},{4,5},{5,4},{6,7},{7,6},{8,9},{9,8},{10,11... | collective-permute-start | bytes 2359304 | tf_op jit(solution)/shard_map/ppermute | solution.py:297
  53.3 0.2 collective-permute-start.9
  53.5 0.0 collective-permute-done.18.refs_4_
  53.5 0.4 collective-permute-start.20
  53.9 0.6 collective-permute-done.19.refs_5_
  54.4 0.8 add_parts.4
  55.2 0.7 copy-done.6
  55.9 1.5 %collective-permute-start.12 = (bf16[576,128]{1,0:T(8,128)(2,1)S(1)}, bf16[576,128]{1,0:T(8,128)(2,1)S(1)}, u32[]{:S(2)}, u32[]{:S(2)}) collective-permute-start(bf16[576,128]{1,0:T(8,128)(2,1)S(1)} %get-tuple-element.19), channel_id=1, source_target_pairs={{4,0},{6,2},{0,4},{2,6},{12,8},{14,10},{8,12},{10,14},{20,16},{22,... | collective-permute-start | bytes 442376 | tf_op jit(solution)/shard_map/ppermute | solution.py:294
  57.4 0.5 collective-permute-start.14
  57.9 4.7 %collective-permute-done.12.refs_2_ = bf16[576,128]{1,0:T(8,128)(2,1)S(1)} collective-permute-done((bf16[576,128]{1,0:T(8,128)(2,1)S(1)}, bf16[576,128]{1,0:T(8,128)(2,1)S(1)}, u32[]{:S(2)}, u32[]{:S(2)}) %collective-permute-start.12) | collective-permute-done | bytes 147488 | tf_op jit(solution)/shard_map/ppermute | solution.py:294
  62.6 0.7 copy-done.2
  63.3 1.5 %collective-permute-start.16 = (bf16[576,128]{1,0:T(8,128)(2,1)}, bf16[576,128]{1,0:T(8,128)(2,1)}, u32[]{:S(2)}, u32[]{:S(2)}) collective-permute-start(bf16[576,128]{1,0:T(8,128)(2,1)} %get-tuple-element.21), channel_id=1, source_target_pairs={{4,0},{6,2},{0,4},{2,6},{12,8},{14,10},{8,12},{10,14},{20,16},{22,... | collective-permute-start | bytes 442376 | tf_op jit(solution)/shard_map/ppermute | solution.py:294
  64.8 0.9 %copy-done.3 = bf16[576,128]{1,0:T(8,128)(2,1)S(1)} copy-done((bf16[576,128]{1,0:T(8,128)(2,1)S(1)}, bf16[576,128]{1,0:T(8,128)(2,1)}, u32[]{:S(2)}) %copy-start.3) | copy-done | bytes 147480
  65.7 0.1 add_parts.5
  65.7 1.2 %collective-permute-start.11 = (bf16[576,128]{1,0:T(8,128)(2,1)}, bf16[576,128]{1,0:T(8,128)(2,1)S(1)}, u32[]{:S(2)}, u32[]{:S(2)}) collective-permute-start(bf16[576,128]{1,0:T(8,128)(2,1)} %copy-done.6), channel_id=1, source_target_pairs={{4,0},{6,2},{0,4},{2,6},{12,8},{14,10},{8,12},{10,14},{20,16},{22,... | collective-permute-start | bytes 442376 | tf_op jit(solution)/shard_map/ppermute | solution.py:294
  66.9 1.0 %add_parts.6 = bf16[576,128]{1,0:T(8,128)(2,1)S(1)} custom-call(bf16[2304,128]{1,0:T(8,128)(2,1)S(1)} %get-tuple-element.14.refs_0_, bf16[2304,128]{1,0:T(8,128)(2,1)S(1)} %collective-permute-done.9.refs_1_, bf16[576,128]{1,0:T(8,128)(2,1)} %collective-permute-done.14.refs_2_), custom_call_target="tpu_custom_call" | custom-call | tf_op jit(solution)/shard_map/add_parts/pallas_call | solution.py:243
  67.9 1.6 %collective-permute-done.16.refs_2_ = bf16[576,128]{1,0:T(8,128)(2,1)} collective-permute-done((bf16[576,128]{1,0:T(8,128)(2,1)}, bf16[576,128]{1,0:T(8,128)(2,1)}, u32[]{:S(2)}, u32[]{:S(2)}) %collective-permute-start.16) | collective-permute-done | bytes 147488 | tf_op jit(solution)/shard_map/ppermute | solution.py:294
  69.5 2.6 %collective-permute-start.13 = (bf16[576,128]{1,0:T(8,128)(2,1)S(1)}, bf16[576,128]{1,0:T(8,128)(2,1)S(1)}, u32[]{:S(2)}, u32[]{:S(2)}) collective-permute-start(bf16[576,128]{1,0:T(8,128)(2,1)S(1)} %add_parts.5), channel_id=1, source_target_pairs={{24,0},{26,2},{28,4},{30,6},{0,8},{2,10},{4,12},{6,14},{8,16},{10,... | collective-permute-start | bytes 442376 | tf_op jit(solution)/shard_map/ppermute | solution.py:294
  72.1 1.0 %add_parts.7 = bf16[576,128]{1,0:T(8,128)(2,1)S(1)} custom-call(bf16[2304,128]{1,0:T(8,128)(2,1)S(1)} %get-tuple-element.14.refs_0_, bf16[2304,128]{1,0:T(8,128)(2,1)S(1)} %collective-permute-done.9.refs_1_, bf16[576,128]{1,0:T(8,128)(2,1)} %collective-permute-done.16.refs_2_), custom_call_target="tpu_custom_call" | custom-call | tf_op jit(solution)/shard_map/add_parts/pallas_call | solution.py:243
  73.0 1.8 %collective-permute-start.15 = (bf16[576,128]{1,0:T(8,128)(2,1)S(1)}, bf16[576,128]{1,0:T(8,128)(2,1)S(1)}, u32[]{:S(2)}, u32[]{:S(2)}) collective-permute-start(bf16[576,128]{1,0:T(8,128)(2,1)S(1)} %add_parts.6), channel_id=1, source_target_pairs={{16,0},{18,2},{20,4},{22,6},{24,8},{26,10},{28,12},{30,14},{0,16},... | collective-permute-start | bytes 442376 | tf_op jit(solution)/shard_map/ppermute | solution.py:294
  74.8 1.4 %collective-permute-start.17 = (bf16[576,128]{1,0:T(8,128)(2,1)S(1)}, bf16[576,128]{1,0:T(8,128)(2,1)S(1)}, u32[]{:S(2)}, u32[]{:S(2)}) collective-permute-start(bf16[576,128]{1,0:T(8,128)(2,1)S(1)} %add_parts.7), channel_id=1, source_target_pairs={{8,0},{10,2},{12,4},{14,6},{16,8},{18,10},{20,12},{22,14},{24,16},... | collective-permute-start | bytes 442376 | tf_op jit(solution)/shard_map/ppermute | solution.py:294
  76.3 9.8 %weight_grad.1 = f32[24,10,128,128]{3,2,1,0:T(8,128)} custom-call(s32[24,20]{1,0:T(8,128)S(1)} %copy-done.5, s32[16]{0:T(128)S(1)} %fusion.6.offs_s, s32[1]{0:T(128)} %bitcast.2.half_s, bf16[2304,128]{1,0:T(8,128)(2,1)S(1)} %pack.2.refs_0_, bf16[2304,128]{1,0:T(8,128)(2,1)S(1)} %pack.3.refs_1_, bf16[2304,128]{1,0:T(8,128)(2,1)S(1)} %collective-permute-done.7.refs_2_, ...), custom_call_target="tpu_custom_call" | custom-call | flops 2013265920 | bytes 15728640 | tf_op jit(solution)/shard_map/weight_grad/pallas_call | solution.py:194
  86.1 0.8 fusion
  (22 shorter events, 0.1 us)
Async XLA Ops:
  0.6 10.1 %collective-permute-start.2 = (bf16[576,128]{1,0:T(8,128)(2,1)}, bf16[576,128]{1,0:T(8,128)(2,1)S(1)}, u32[]{:S(2)}, u32[]{:S(2)}) collective-permute-start(bf16[576,128]{1,0:T(8,128)(2,1)} %bitcast.4), channel_id=1, source_target_pairs={{24,0},{26,2},{28,4},{30,6},{0,8},{2,10},{4,12},{6,14},{8,16},{10,... | collective-permute-start | bytes 442376 | tf_op jit(solution)/shard_map/ppermute | solution.py:294
  3.7 12.5 %collective-permute-start.1 = (bf16[576,128]{1,0:T(8,128)(2,1)}, bf16[576,128]{1,0:T(8,128)(2,1)S(1)}, u32[]{:S(2)}, u32[]{:S(2)}) collective-permute-start(bf16[576,128]{1,0:T(8,128)(2,1)} %bitcast.5), channel_id=1, source_target_pairs={{16,0},{18,2},{20,4},{22,6},{24,8},{26,10},{28,12},{30,14},{0,16},... | collective-permute-start | bytes 442376 | tf_op jit(solution)/shard_map/ppermute | solution.py:294
  6.3 11.4 %collective-permute-start = (bf16[576,128]{1,0:T(8,128)(2,1)}, bf16[576,128]{1,0:T(8,128)(2,1)S(1)}, u32[]{:S(2)}, u32[]{:S(2)}) collective-permute-start(bf16[576,128]{1,0:T(8,128)(2,1)} %bitcast.6), channel_id=1, source_target_pairs={{8,0},{10,2},{12,4},{14,6},{16,8},{18,10},{20,12},{22,14},{24,16},... | collective-permute-start | bytes 442376 | tf_op jit(solution)/shard_map/ppermute | solution.py:294
  7.7 11.6 %collective-permute-start.3 = (bf16[576,128]{1,0:T(8,128)(2,1)}, bf16[576,128]{1,0:T(8,128)(2,1)S(1)}, u32[]{:S(2)}, u32[]{:S(2)}) collective-permute-start(bf16[576,128]{1,0:T(8,128)(2,1)} %bitcast.7), channel_id=1, source_target_pairs={{4,0},{6,2},{0,4},{2,6},{12,8},{14,10},{8,12},{10,14},{20,16},{22,... | collective-permute-start | bytes 442376 | tf_op jit(solution)/shard_map/ppermute | solution.py:294
  10.8 8.5 %collective-permute-start.6 = (bf16[576,128]{1,0:T(8,128)(2,1)S(1)}, bf16[576,128]{1,0:T(8,128)(2,1)S(1)}, u32[]{:S(2)}, u32[]{:S(2)}) collective-permute-start(bf16[576,128]{1,0:T(8,128)(2,1)S(1)} %collective-permute-done.2.refs_3_), channel_id=1, source_target_pairs={{4,0},{6,2},{0,4},{2,6},{12,8},{14,10},{8,12},{10,14},{20,16},{22,... | collective-permute-start | bytes 442376 | tf_op jit(solution)/shard_map/ppermute | solution.py:294
  16.2 6.7 %collective-permute-start.5 = (bf16[576,128]{1,0:T(8,128)(2,1)S(1)}, bf16[576,128]{1,0:T(8,128)(2,1)S(1)}, u32[]{:S(2)}, u32[]{:S(2)}) collective-permute-start(bf16[576,128]{1,0:T(8,128)(2,1)S(1)} %collective-permute-done.1.refs_2_), channel_id=1, source_target_pairs={{4,0},{6,2},{0,4},{2,6},{12,8},{14,10},{8,12},{10,14},{20,16},{22,... | collective-permute-start | bytes 442376 | tf_op jit(solution)/shard_map/ppermute | solution.py:294
  17.7 7.3 %collective-permute-start.4 = (bf16[576,128]{1,0:T(8,128)(2,1)S(1)}, bf16[576,128]{1,0:T(8,128)(2,1)S(1)}, u32[]{:S(2)}, u32[]{:S(2)}) collective-permute-start(bf16[576,128]{1,0:T(8,128)(2,1)S(1)} %collective-permute-done.refs_1_), channel_id=1, source_target_pairs={{4,0},{6,2},{0,4},{2,6},{12,8},{14,10},{8,12},{10,14},{20,16},{22,... | collective-permute-start | bytes 442376 | tf_op jit(solution)/shard_map/ppermute | solution.py:294
  18.3 0.9 %copy-start.1 = (bf16[128,576]{0,1:T(8,128)(2,1)S(1)}, bf16[128,576]{0,1:T(8,128)(2,1)}, u32[]{:S(2)}) copy-start(bf16[128,576]{0,1:T(8,128)(2,1)} %param.7) | copy-start | bytes 442372
  19.2 57.1 %copy-start.5 = (s32[24,20]{1,0:T(8,128)S(1)}, s32[24,20]{1,0:T(8,128)}, u32[]{:S(2)}) copy-start(s32[24,20]{1,0:T(8,128)} %rows_s.3) | copy-start | bytes 5764
  19.2 8.8 %collective-permute-start.7 = (bf16[2304,128]{1,0:T(8,128)(2,1)S(1)}, bf16[2304,128]{1,0:T(8,128)(2,1)S(1)}, u32[]{:S(2)}, u32[]{:S(2)}) collective-permute-start(bf16[2304,128]{1,0:T(8,128)(2,1)S(1)} %pack.2.refs_0_), channel_id=1, source_target_pairs={{2,0},{0,2},{6,4},{4,6},{10,8},{8,10},{14,12},{12,14},{18,16},{16,... | collective-permute-start | bytes 1769480 | tf_op jit(solution)/shard_map/ppermute | solution.py:294
  25.1 2.9 %collective-permute-start.8 = (bf16[2304,128]{1,0:T(8,128)(2,1)S(1)}, bf16[2304,128]{1,0:T(8,128)(2,1)S(1)}, u32[]{:S(2)}, u32[]{:S(2)}) collective-permute-start(bf16[2304,128]{1,0:T(8,128)(2,1)S(1)} %pack.3.refs_1_), channel_id=1, source_target_pairs={{2,0},{0,2},{6,4},{4,6},{10,8},{8,10},{14,12},{12,14},{18,16},{16,... | collective-permute-start | bytes 1769480 | tf_op jit(solution)/shard_map/ppermute | solution.py:294
  25.9 27.6 %collective-permute-start.18 = (bf16[2304,128]{1,0:T(8,128)(2,1)S(1)}, bf16[2304,128]{1,0:T(8,128)(2,1)}, u32[]{:S(2)}, u32[]{:S(2)}) collective-permute-start(bf16[2304,128]{1,0:T(8,128)(2,1)S(1)} %pack.2.refs_0_), channel_id=1, source_target_pairs={{0,1},{1,0},{2,3},{3,2},{4,5},{5,4},{6,7},{7,6},{8,9},{9,8},{10,11... | collective-permute-start | bytes 1769480 | tf_op jit(solution)/shard_map/ppermute | solution.py:297
  27.5 26.9 %collective-permute-start.19 = (bf16[2304,128]{1,0:T(8,128)(2,1)S(1)}, bf16[2304,128]{1,0:T(8,128)(2,1)}, u32[]{:S(2)}, u32[]{:S(2)}) collective-permute-start(bf16[2304,128]{1,0:T(8,128)(2,1)S(1)} %pack.3.refs_1_), channel_id=1, source_target_pairs={{0,1},{1,0},{2,3},{3,2},{4,5},{5,4},{6,7},{7,6},{8,9},{9,8},{10,11... | collective-permute-start | bytes 1769480 | tf_op jit(solution)/shard_map/ppermute | solution.py:297
  28.0 1.1 %copy-start = (bf16[128,3072]{1,0:T(8,128)(2,1)S(1)}, bf16[128,3072]{1,0:T(8,128)(2,1)}, u32[]{:S(2)}) copy-start(bf16[128,3072]{1,0:T(8,128)(2,1)} %refs_5_.1) | copy-start | bytes 2359300
  29.2 0.7 copy-start.4
  51.7 2.7 %collective-permute-start.10 = (bf16[2304,128]{1,0:T(8,128)(2,1)S(1)}, bf16[2304,128]{1,0:T(8,128)(2,1)S(1)}, u32[]{:S(2)}, u32[]{:S(2)}) collective-permute-start(bf16[2304,128]{1,0:T(8,128)(2,1)S(1)} %get-tuple-element.17), channel_id=1, source_target_pairs={{2,0},{0,2},{6,4},{4,6},{10,8},{8,10},{14,12},{12,14},{18,16},{16,... | collective-permute-start | bytes 1769480 | tf_op jit(solution)/shard_map/ppermute | solution.py:294
  51.8 24.5 %collective-permute-start.22 = (bf16[128,3072]{1,0:T(8,128)(2,1)}, bf16[128,3072]{1,0:T(8,128)(2,1)}, u32[]{:S(2)}, u32[]{:S(2)}) collective-permute-start(bf16[128,3072]{1,0:T(8,128)(2,1)} %get-tuple-element.22.refs_8_), channel_id=1, source_target_pairs={{0,1},{1,0},{2,3},{3,2},{4,5},{5,4},{6,7},{7,6},{8,9},{9,8},{10,11... | collective-permute-start | bytes 2359304 | tf_op jit(solution)/shard_map/ppermute | solution.py:297
  53.3 4.0 %collective-permute-start.9 = (bf16[2304,128]{1,0:T(8,128)(2,1)S(1)}, bf16[2304,128]{1,0:T(8,128)(2,1)S(1)}, u32[]{:S(2)}, u32[]{:S(2)}) collective-permute-start(bf16[2304,128]{1,0:T(8,128)(2,1)S(1)} %get-tuple-element.15), channel_id=1, source_target_pairs={{2,0},{0,2},{6,4},{4,6},{10,8},{8,10},{14,12},{12,14},{18,16},{16,... | collective-permute-start | bytes 1769480 | tf_op jit(solution)/shard_map/ppermute | solution.py:294
  53.5 19.5 %collective-permute-start.20 = (bf16[2304,128]{1,0:T(8,128)(2,1)}, bf16[2304,128]{1,0:T(8,128)(2,1)}, u32[]{:S(2)}, u32[]{:S(2)}) collective-permute-start(bf16[2304,128]{1,0:T(8,128)(2,1)} %collective-permute-done.18.refs_4_), channel_id=1, source_target_pairs={{2,0},{0,2},{6,4},{4,6},{10,8},{8,10},{14,12},{12,14},{18,16},{16,... | collective-permute-start | bytes 1769480 | tf_op jit(solution)/shard_map/ppermute | solution.py:294
  54.4 20.4 %collective-permute-start.21 = (bf16[2304,128]{1,0:T(8,128)(2,1)}, bf16[2304,128]{1,0:T(8,128)(2,1)}, u32[]{:S(2)}, u32[]{:S(2)}) collective-permute-start(bf16[2304,128]{1,0:T(8,128)(2,1)} %collective-permute-done.19.refs_5_), channel_id=1, source_target_pairs={{2,0},{0,2},{6,4},{4,6},{10,8},{8,10},{14,12},{12,14},{18,16},{16,... | collective-permute-start | bytes 1769480 | tf_op jit(solution)/shard_map/ppermute | solution.py:294
  55.2 0.7 copy-start.6
  55.9 6.7 %collective-permute-start.12 = (bf16[576,128]{1,0:T(8,128)(2,1)S(1)}, bf16[576,128]{1,0:T(8,128)(2,1)S(1)}, u32[]{:S(2)}, u32[]{:S(2)}) collective-permute-start(bf16[576,128]{1,0:T(8,128)(2,1)S(1)} %get-tuple-element.19), channel_id=1, source_target_pairs={{4,0},{6,2},{0,4},{2,6},{12,8},{14,10},{8,12},{10,14},{20,16},{22,... | collective-permute-start | bytes 442376 | tf_op jit(solution)/shard_map/ppermute | solution.py:294
  57.4 8.4 %collective-permute-start.14 = (bf16[576,128]{1,0:T(8,128)(2,1)}, bf16[576,128]{1,0:T(8,128)(2,1)}, u32[]{:S(2)}, u32[]{:S(2)}) collective-permute-start(bf16[576,128]{1,0:T(8,128)(2,1)} %get-tuple-element.20), channel_id=1, source_target_pairs={{4,0},{6,2},{0,4},{2,6},{12,8},{14,10},{8,12},{10,14},{20,16},{22,... | collective-permute-start | bytes 442376 | tf_op jit(solution)/shard_map/ppermute | solution.py:294
  62.6 0.7 copy-start.2
  63.3 6.2 %collective-permute-start.16 = (bf16[576,128]{1,0:T(8,128)(2,1)}, bf16[576,128]{1,0:T(8,128)(2,1)}, u32[]{:S(2)}, u32[]{:S(2)}) collective-permute-start(bf16[576,128]{1,0:T(8,128)(2,1)} %get-tuple-element.21), channel_id=1, source_target_pairs={{4,0},{6,2},{0,4},{2,6},{12,8},{14,10},{8,12},{10,14},{20,16},{22,... | collective-permute-start | bytes 442376 | tf_op jit(solution)/shard_map/ppermute | solution.py:294
  64.8 0.9 %copy-start.3 = (bf16[576,128]{1,0:T(8,128)(2,1)S(1)}, bf16[576,128]{1,0:T(8,128)(2,1)}, u32[]{:S(2)}) copy-start(bf16[576,128]{1,0:T(8,128)(2,1)} %copy-done.2) | copy-start | bytes 442372
  65.7 20.3 %collective-permute-start.11 = (bf16[576,128]{1,0:T(8,128)(2,1)}, bf16[576,128]{1,0:T(8,128)(2,1)S(1)}, u32[]{:S(2)}, u32[]{:S(2)}) collective-permute-start(bf16[576,128]{1,0:T(8,128)(2,1)} %copy-done.6), channel_id=1, source_target_pairs={{4,0},{6,2},{0,4},{2,6},{12,8},{14,10},{8,12},{10,14},{20,16},{22,... | collective-permute-start | bytes 442376 | tf_op jit(solution)/shard_map/ppermute | solution.py:294
  69.5 16.6 %collective-permute-start.13 = (bf16[576,128]{1,0:T(8,128)(2,1)S(1)}, bf16[576,128]{1,0:T(8,128)(2,1)S(1)}, u32[]{:S(2)}, u32[]{:S(2)}) collective-permute-start(bf16[576,128]{1,0:T(8,128)(2,1)S(1)} %add_parts.5), channel_id=1, source_target_pairs={{24,0},{26,2},{28,4},{30,6},{0,8},{2,10},{4,12},{6,14},{8,16},{10,... | collective-permute-start | bytes 442376 | tf_op jit(solution)/shard_map/ppermute | solution.py:294
  73.0 13.0 %collective-permute-start.15 = (bf16[576,128]{1,0:T(8,128)(2,1)S(1)}, bf16[576,128]{1,0:T(8,128)(2,1)S(1)}, u32[]{:S(2)}, u32[]{:S(2)}) collective-permute-start(bf16[576,128]{1,0:T(8,128)(2,1)S(1)} %add_parts.6), channel_id=1, source_target_pairs={{16,0},{18,2},{20,4},{22,6},{24,8},{26,10},{28,12},{30,14},{0,16},... | collective-permute-start | bytes 442376 | tf_op jit(solution)/shard_map/ppermute | solution.py:294
  74.8 11.3 %collective-permute-start.17 = (bf16[576,128]{1,0:T(8,128)(2,1)S(1)}, bf16[576,128]{1,0:T(8,128)(2,1)S(1)}, u32[]{:S(2)}, u32[]{:S(2)}) collective-permute-start(bf16[576,128]{1,0:T(8,128)(2,1)S(1)} %add_parts.7), channel_id=1, source_target_pairs={{8,0},{10,2},{12,4},{14,6},{16,8},{18,10},{20,12},{22,14},{24,16},... | collective-permute-start | bytes 442376 | tf_op jit(solution)/shard_map/ppermute | solution.py:294

commit v3 on v2

--- a/solution.py
+++ b/solution.py
@@ -61,7 +61,7 @@
 
     def turn(r, carry):
         xs[r] = xt[block(r, side), :].T
-        acc[r] = jnp.zeros(acc.shape[1:], acc.dtype)
+        acc[block(r, side), :] = jnp.zeros((side, acc.shape[1]), acc.dtype)
         return carry
 
     lax.fori_loop(0, blocks, turn, 0, unroll=4)
@@ -87,7 +87,7 @@
             left = w[c, k : k + step].reshape(step * side, side)
             part_sum = jnp.dot(left, turned, preferred_element_type=jnp.float32)
             for i in range(step):
-                acc[rows_s[c, k + i]] += part_sum[i * side : (i + 1) * side, :]
+                acc[block(rows_s[c, k + i], side), :] += part_sum[i * side : (i + 1) * side]
 
     def one(c, carry):
         out(c).start()
@@ -102,13 +102,9 @@
     out(cols - 1).start()
     back(cols - 1)
 
-    def narrow(r, carry):
-        xt[block(r, side), :] = acc[r].astype(xt.dtype)
-        return carry
-
-    lax.fori_loop(0, blocks, narrow, 0, unroll=4)
     for j, shard in enumerate(shards_of(dx_refs, part)):
-        shard[...] = xt[pl.ds(pl.multiple_of(offs_s[j], 16), part), :]
+        rows = pl.ds(pl.multiple_of(offs_s[j], 16), part)
+        shard[...] = acc[rows, :].astype(shard.dtype)
 
     def drain(c, carry):
         out(c).wait()
@@ -125,7 +121,7 @@
     scratch = [
         ((features, tokens), jnp.bfloat16),
         ((blocks, tokens, side), jnp.bfloat16),
-        ((blocks, side, tokens), jnp.float32),
+        ((features, tokens), jnp.float32),
         ((cols, tokens, side), jnp.bfloat16),
         (weights.shape, jnp.bfloat16),
     ]
@@ -229,6 +225,23 @@
     )(*arrays)
 
 
+def stage_kernel(*refs):
+    half = len(refs) // 2
+    for source, target in zip(refs[:half], refs[half:]):
+        target[...] = source[...]
+
+
+def stage(*arrays):
+    return pl.pallas_call(
+        stage_kernel,
+        in_specs=[VMEM] * len(arrays),
+        out_specs=[VMEM] * len(arrays),
+        out_shape=[jax.ShapeDtypeStruct(a.shape, a.dtype) for a in arrays],
+        compiler_params=pltpu.CompilerParams(vmem_limit_bytes=MARGIN),
+        name="stage",
+    )(*arrays)
+
+
 def sum_kernel(plan, part, n_in, *refs):
     ins, outs = refs[:n_in], refs[n_in:]
     for terms, out in zip(plan, outs):
@@ -251,7 +264,7 @@
 
 
 def direct(n, mp):
-    return n % (CORES * SIDES) == 0 and n // (CORES * SIDES) <= MAX_LINE and mp == 2
+    return n % (CORES * SIDES) == 0 and 2 <= n // (CORES * SIDES) <= MAX_LINE and mp == 2
 
 
 def body(activations, block_values, block_rows, cotangent):
@@ -286,12 +299,18 @@
         dx = lax.psum_scatter(dx, "dp", scatter_dimension=0, tiled=True)
         return gelu_out, dx.astype(jnp.bfloat16).T, block_grad
 
+    def along(z, k):
+        return z ^ k if line & (line - 1) == 0 else (z + k) % line
+
     def permute(a, k, s, q):
         def source(i):
             z, x, core = i // chip, i // CORES % SIDES, i % CORES
-            return ((z + k) % line * SIDES + (x ^ s)) * CORES + (core ^ q)
+            return (along(z, k) * SIDES + (x ^ s)) * CORES + (core ^ q)
 
         return lax.ppermute(a, "dp", [(source(i), i) for i in range(n)])
+
+    def back_to(k):
+        return next(i for i in range(line) if along(along(0, k), i) == 0)
 
     def across(a):
         return lax.ppermute(a, "mp", [(i, i ^ 1) for i in range(mp)])
@@ -299,9 +318,10 @@
     rel = [(k, s, q) for q in range(CORES) for s in range(SIDES) for k in range(line)]
     ks, ss, qs = (np.array(v, np.int32) for v in zip(*rel))
     z, x, core = me // chip, me // CORES % SIDES, me % CORES
-    offs = (((z + ks) % line * SIDES + (x ^ ss)) * CORES + (core ^ qs)) * part
+    offs = ((along(z, ks) * SIDES + (x ^ ss)) * CORES + (core ^ qs)) * part
     offs = offs.astype(jnp.int32)
 
+    cotangent, block_rows = stage(cotangent, block_rows)
     near = [permute(own, k, 0, 0) if k else own for k in range(line)]
     side_x = [permute(a, 0, 1, 0) for a in near]
     x_own, x_far = [], []
@@ -318,7 +338,8 @@
     got1 = permute(give1, 0, 0, 1)
     got0 = permute(give0, 0, 0, 1)
     slopes_far = across(slopes)
-    chips = add_parts([keep1, got1], [[(0, k), (1, k)] for k in range(line)], part)
+    first = add_parts([keep1, got1], [[(0, k), (1, k)] for k in range(1, line)], part)
+    chips = add_parts([keep1, got1], [[(0, 0), (1, 0)]], part) + first
     pairs = [permute(a, 0, 1, 0) for a in chips]
     total = (
         keep0[:part].astype(jnp.float32)
@@ -327,7 +348,7 @@
     )
     for k in range(1, line):
         (mine,) = add_parts([keep0, got0, pairs[k]], [[(0, k), (1, k), (2, 0)]], part)
-        total = total + permute(mine, line - k, 0, 0).astype(jnp.float32)
+        total = total + permute(mine, back_to(k), 0, 0).astype(jnp.float32)
     block_grad = weight_grad(
         [x_own, x_far],
         part,
@@ -344,6 +365,8 @@
 def solution(mesh):
     in_specs = (P("mp", "dp"), P("dp", None, None, None), P("dp", None), P("mp", "dp"))
     out_specs = (P("mp", "dp"), P("mp", "dp"), P("dp", "mp", None, None))
-    return jax.shard_map(
-        body, mesh=mesh, in_specs=in_specs, out_specs=out_specs, check_vma=False
-    )
+    step = jax.shard_map(body, mesh=mesh, in_specs=in_specs, out_specs=out_specs, check_vma=False)
+    n, mp = mesh.shape["dp"], mesh.shape["mp"]
+    if not direct(n, mp):
+        return step
+    return step

time: 87.2 us -> 89.3 us (1.024)
  waiting for transfers between devices: 18 us -> 21.1 us
  starting transfers between devices: 27.1 us -> 24.1 us
  local copies, waits for them, and re-layouts: 4.99 us -> 6.46 us
    ppermute x20, starting transfers between devices: 23.5 us -> 20.5 us  [permute(): return lax.ppermute(a, 'dp', [(source(i), i) for i in range(n)])]
    ppermute x3, waiting for transfers between devices: 0.58 us -> 2.71 us  [across(): return lax.ppermute(a, 'mp', [(i, i ^ 1) for i in range(mp)])]
    unnamed x14 -> x18, local copies, waits for them, and re-layouts: 4.99 us -> 6.46 us
    ppermute x20, waiting for transfers between devices: 17.5 us -> 18.4 us  [permute(): return lax.ppermute(a, 'dp', [(source(i), i) for i in range(n)])]
    pallas_call x4 -> x5, Pallas kernels: 2.77 us -> 2.89 us  [add_parts(): pl.pallas_call(functools.partial(sum_kernel, plan, part, len(arrays)), in...]
  transfers between devices with their start and end apart: 23 -> 23, of which waited for: 7 -> 6; matrix products, arithmetic and copies ran while one was open for 1% -> 1% of each run, Pallas kernels for 40% -> 39%
where the time goes in v3:
time: 89.3 us; the launch traced here: 88.9 us
  Pallas kernels  34.9 us (39%)
  starting transfers between devices  24.1 us (27%)
  waiting for transfers between devices  21.1 us (24%)
  local copies, waits for them, and re-layouts  6.46 us (7%)
  other arithmetic  1.48 us (2%)
    pallas_call x1, Pallas kernels, forward(): pl.pallas_call(functools.partial(forward_kernel, len(arrays), len(outs),...  22.1 us
    ppermute x20, starting transfers between devices, permute(): return lax.ppermute(a, 'dp', [(source(i), i) for i in range(n)])  20.5 us
    ppermute x20, waiting for transfers between devices, permute(): return lax.ppermute(a, 'dp', [(source(i), i) for i in range(n)])  18.4 us
    pallas_call x1, Pallas kernels, weight_grad(): pl.pallas_call(functools.partial(weight_kernel, len(planes), len(planes[0...  9.78 us
    unnamed x18, local copies, waits for them, and re-layouts  6.46 us
    ppermute x3, starting transfers between devices, across(): return lax.ppermute(a, 'mp', [(i, i ^ 1) for i in range(mp)])  3.57 us
    pallas_call x5, Pallas kernels, add_parts(): pl.pallas_call(functools.partial(sum_kernel, plan, part, len(arrays)), in...  2.89 us
    ppermute x3, waiting for transfers between devices, across(): return lax.ppermute(a, 'mp', [(i, i ^ 1) for i in range(mp)])  2.71 us
  transfers between devices with their start and end apart: 23, of which 6 were waited for; matrix products, arithmetic and copies ran while one was open for 1% of the time, Pallas kernels for 39%

profile of v3, /device:TPU:0, one launch (start us, length us, event | category | flops | bytes accessed | tf_op | source)
XLA Modules:
  0.0 88.9 jit_solution(4150027786728317499)
XLA Ops:
  0.6 5.1 %collective-permute-start.2 = (bf16[576,128]{1,0:T(8,128)(2,1)}, bf16[576,128]{1,0:T(8,128)(2,1)S(1)}, u32[]{:S(2)}, u32[]{:S(2)}) collective-permute-start(bf16[576,128]{1,0:T(8,128)(2,1)} %bitcast.4), channel_id=1, source_target_pairs={{24,0},{26,2},{28,4},{30,6},{16,8},{18,10},{20,12},{22,14},{8,16},... | collective-permute-start | bytes 442376 | tf_op jit(solution)/shard_map/ppermute | solution.py:310
  5.8 0.0 collective-permute-start.1
  5.8 0.6 collective-permute-start
  6.4 1.6 %collective-permute-start.3 = (bf16[576,128]{1,0:T(8,128)(2,1)}, bf16[576,128]{1,0:T(8,128)(2,1)S(1)}, u32[]{:S(2)}, u32[]{:S(2)}) collective-permute-start(bf16[576,128]{1,0:T(8,128)(2,1)} %bitcast.7), channel_id=1, source_target_pairs={{4,0},{6,2},{0,4},{2,6},{12,8},{14,10},{8,12},{10,14},{20,16},{22,... | collective-permute-start | bytes 442376 | tf_op jit(solution)/shard_map/ppermute | solution.py:310
  8.1 2.7 %collective-permute-done.2.refs_3_ = bf16[576,128]{1,0:T(8,128)(2,1)S(1)} collective-permute-done((bf16[576,128]{1,0:T(8,128)(2,1)}, bf16[576,128]{1,0:T(8,128)(2,1)S(1)}, u32[]{:S(2)}, u32[]{:S(2)}) %collective-permute-start.2) | collective-permute-done | bytes 147488 | tf_op jit(solution)/shard_map/ppermute | solution.py:310
  10.8 1.7 %collective-permute-start.6 = (bf16[576,128]{1,0:T(8,128)(2,1)S(1)}, bf16[576,128]{1,0:T(8,128)(2,1)S(1)}, u32[]{:S(2)}, u32[]{:S(2)}) collective-permute-start(bf16[576,128]{1,0:T(8,128)(2,1)S(1)} %collective-permute-done.2.refs_3_), channel_id=1, source_target_pairs={{4,0},{6,2},{0,4},{2,6},{12,8},{14,10},{8,12},{10,14},{20,16},{22,... | collective-permute-start | bytes 442376 | tf_op jit(solution)/shard_map/ppermute | solution.py:310
  12.4 6.0 %collective-permute-done.1.refs_2_ = bf16[576,128]{1,0:T(8,128)(2,1)S(1)} collective-permute-done((bf16[576,128]{1,0:T(8,128)(2,1)}, bf16[576,128]{1,0:T(8,128)(2,1)S(1)}, u32[]{:S(2)}, u32[]{:S(2)}) %collective-permute-start.1) | collective-permute-done | bytes 147488 | tf_op jit(solution)/shard_map/ppermute | solution.py:310
  18.5 1.5 %collective-permute-start.5 = (bf16[576,128]{1,0:T(8,128)(2,1)S(1)}, bf16[576,128]{1,0:T(8,128)(2,1)S(1)}, u32[]{:S(2)}, u32[]{:S(2)}) collective-permute-start(bf16[576,128]{1,0:T(8,128)(2,1)S(1)} %collective-permute-done.1.refs_2_), channel_id=1, source_target_pairs={{4,0},{6,2},{0,4},{2,6},{12,8},{14,10},{8,12},{10,14},{20,16},{22,... | collective-permute-start | bytes 442376 | tf_op jit(solution)/shard_map/ppermute | solution.py:310
  20.0 0.0 collective-permute-done.refs_1_
  20.0 0.5 collective-permute-start.4
  20.5 0.9 %copy-done.5 = bf16[128,576]{0,1:T(8,128)(2,1)S(1)} copy-done((bf16[128,576]{0,1:T(8,128)(2,1)S(1)}, bf16[128,576]{0,1:T(8,128)(2,1)}, u32[]{:S(2)}) %copy-start.5) | copy-done | bytes 147480
  21.4 0.1 collective-permute-start.7
  21.5 0.0 collective-permute-done.3.refs_0_
  21.5 3.4 %collective-permute-done.5.refs_2_ = bf16[576,128]{1,0:T(8,128)(2,1)S(1)} collective-permute-done((bf16[576,128]{1,0:T(8,128)(2,1)S(1)}, bf16[576,128]{1,0:T(8,128)(2,1)S(1)}, u32[]{:S(2)}, u32[]{:S(2)}) %collective-permute-start.5) | collective-permute-done | bytes 147488 | tf_op jit(solution)/shard_map/ppermute | solution.py:310
  25.0 1.6 %collective-permute-done.4.refs_1_ = bf16[576,128]{1,0:T(8,128)(2,1)S(1)} collective-permute-done((bf16[576,128]{1,0:T(8,128)(2,1)S(1)}, bf16[576,128]{1,0:T(8,128)(2,1)S(1)}, u32[]{:S(2)}, u32[]{:S(2)}) %collective-permute-start.4) | collective-permute-done | bytes 147488 | tf_op jit(solution)/shard_map/ppermute | solution.py:310
  26.6 0.1 collective-permute-start.8
  26.7 0.0 copy-start.4
  26.7 1.1 %copy-done.4 = bf16[128,3072]{1,0:T(8,128)(2,1)S(1)} copy-done((bf16[128,3072]{1,0:T(8,128)(2,1)S(1)}, bf16[128,3072]{1,0:T(8,128)(2,1)}, u32[]{:S(2)}) %copy-start.4) | copy-done | bytes 786456
  27.8 0.7 copy-done.8
  28.6 0.1 stage.1
  28.6 0.7 add_multiply_fusion.offs_s
  29.3 1.5 %collective-permute-start.18 = (bf16[2304,128]{1,0:T(8,128)(2,1)S(1)}, bf16[2304,128]{1,0:T(8,128)(2,1)}, u32[]{:S(2)}, u32[]{:S(2)}) collective-permute-start(bf16[2304,128]{1,0:T(8,128)(2,1)S(1)} %pack.2.refs_0_), channel_id=1, source_target_pairs={{0,1},{1,0},{2,3},{3,2},{4,5},{5,4},{6,7},{7,6},{8,9},{9,8},{10,11... | collective-permute-start | bytes 1769480 | tf_op jit(solution)/shard_map/ppermute | solution.py:316
  30.8 0.5 collective-permute-start.19
  31.3 22.1 %forward.1 = (bf16[128,3072]{1,0:T(8,128)(2,1)}, bf16[128,3072]{1,0:T(8,128)(2,1)}, bf16[2304,128]{1,0:T(8,128)(2,1)S(1)}, bf16[2304,128]{1,0:T(8,128)(2,1)S(1)}...) custom-call(s32[24,20]{1,0:T(8,128)S(1)} %get-tuple-element.14.rows_s, s32[16]{0:T(128)S(1)} %add_multiply_fusion.offs_s, ...), custom_call_target="tpu_custom_call" | custom-call | flops 4026531840 | bytes 15728640 | tf_op jit(solution)/shard_map/forward/pallas_call | solution.py:128
  53.4 0.0 copy-start
  53.4 0.1 collective-permute-start.10
  53.5 1.5 %collective-permute-start.22 = (bf16[128,3072]{1,0:T(8,128)(2,1)}, bf16[128,3072]{1,0:T(8,128)(2,1)}, u32[]{:S(2)}, u32[]{:S(2)}) collective-permute-start(bf16[128,3072]{1,0:T(8,128)(2,1)} %get-tuple-element.24.refs_8_), channel_id=1, source_target_pairs={{0,1},{1,0},{2,3},{3,2},{4,5},{5,4},{6,7},{7,6},{8,9},{9,8},{10,11... | collective-permute-start | bytes 2359304 | tf_op jit(solution)/shard_map/ppermute | solution.py:316
  55.0 0.2 collective-permute-start.9
  55.2 0.4 collective-permute-start.20
  55.5 2.7 %collective-permute-done.19.refs_5_ = bf16[2304,128]{1,0:T(8,128)(2,1)} collective-permute-done((bf16[2304,128]{1,0:T(8,128)(2,1)S(1)}, bf16[2304,128]{1,0:T(8,128)(2,1)}, u32[]{:S(2)}, u32[]{:S(2)}) %collective-permute-start.19) | collective-permute-done | bytes 589856 | tf_op jit(solution)/shard_map/ppermute | solution.py:316
  58.3 0.9 add_parts.6
  59.1 1.5 %collective-permute-start.12 = (bf16[576,128]{1,0:T(8,128)(2,1)S(1)}, bf16[576,128]{1,0:T(8,128)(2,1)S(1)}, u32[]{:S(2)}, u32[]{:S(2)}) collective-permute-start(bf16[576,128]{1,0:T(8,128)(2,1)S(1)} %get-tuple-element.21), channel_id=1, source_target_pairs={{4,0},{6,2},{0,4},{2,6},{12,8},{14,10},{8,12},{10,14},{20,16},{22,... | collective-permute-start | bytes 442376 | tf_op jit(solution)/shard_map/ppermute | solution.py:310
  60.6 0.6 collective-permute-start.14
  61.2 4.6 %collective-permute-done.12.refs_2_ = bf16[576,128]{1,0:T(8,128)(2,1)S(1)} collective-permute-done((bf16[576,128]{1,0:T(8,128)(2,1)S(1)}, bf16[576,128]{1,0:T(8,128)(2,1)S(1)}, u32[]{:S(2)}, u32[]{:S(2)}) %collective-permute-start.12) | collective-permute-done | bytes 147488 | tf_op jit(solution)/shard_map/ppermute | solution.py:310
  65.9 0.7 copy-done.6
  66.5 1.5 %collective-permute-start.16 = (bf16[576,128]{1,0:T(8,128)(2,1)}, bf16[576,128]{1,0:T(8,128)(2,1)}, u32[]{:S(2)}, u32[]{:S(2)}) collective-permute-start(bf16[576,128]{1,0:T(8,128)(2,1)} %get-tuple-element.23), channel_id=1, source_target_pairs={{4,0},{6,2},{0,4},{2,6},{12,8},{14,10},{8,12},{10,14},{20,16},{22,... | collective-permute-start | bytes 442376 | tf_op jit(solution)/shard_map/ppermute | solution.py:310
  68.0 1.1 %copy-done.1 = bf16[2304,128]{1,0:T(8,128)(2,1)S(1)} copy-done((bf16[2304,128]{1,0:T(8,128)(2,1)S(1)}, bf16[2304,128]{1,0:T(8,128)(2,1)}, u32[]{:S(2)}) %copy-start.1) | copy-done | bytes 589848
  69.1 1.1 %copy-done.3 = bf16[2304,128]{1,0:T(8,128)(2,1)S(1)} copy-done((bf16[2304,128]{1,0:T(8,128)(2,1)S(1)}, bf16[2304,128]{1,0:T(8,128)(2,1)}, u32[]{:S(2)}) %copy-start.3) | copy-done | bytes 589848
  70.2 0.9 %copy-done.7 = bf16[576,128]{1,0:T(8,128)(2,1)S(1)} copy-done((bf16[576,128]{1,0:T(8,128)(2,1)S(1)}, bf16[576,128]{1,0:T(8,128)(2,1)}, u32[]{:S(2)}) %copy-start.7) | copy-done | bytes 147480
  71.1 0.1 add_parts.7
  71.2 0.6 collective-permute-start.11
  71.8 1.0 %add_parts.8 = bf16[576,128]{1,0:T(8,128)(2,1)S(1)} custom-call(bf16[2304,128]{1,0:T(8,128)(2,1)S(1)} %get-tuple-element.17.refs_0_, bf16[2304,128]{1,0:T(8,128)(2,1)S(1)} %collective-permute-done.9.refs_1_, bf16[576,128]{1,0:T(8,128)(2,1)} %collective-permute-done.14.refs_2_), custom_call_target="tpu_custom_call" | custom-call | tf_op jit(solution)/shard_map/add_parts/pallas_call | solution.py:256
  72.7 1.3 %collective-permute-start.13 = (bf16[576,128]{1,0:T(8,128)(2,1)S(1)}, bf16[576,128]{1,0:T(8,128)(2,1)S(1)}, u32[]{:S(2)}, u32[]{:S(2)}) collective-permute-start(bf16[576,128]{1,0:T(8,128)(2,1)S(1)} %add_parts.7), channel_id=1, source_target_pairs={{8,0},{10,2},{12,4},{14,6},{0,8},{2,10},{4,12},{6,14},{24,16},{26,... | collective-permute-start | bytes 442376 | tf_op jit(solution)/shard_map/ppermute | solution.py:310
  74.0 1.0 %add_parts.9 = bf16[576,128]{1,0:T(8,128)(2,1)S(1)} custom-call(bf16[2304,128]{1,0:T(8,128)(2,1)S(1)} %get-tuple-element.17.refs_0_, bf16[2304,128]{1,0:T(8,128)(2,1)S(1)} %collective-permute-done.9.refs_1_, bf16[576,128]{1,0:T(8,128)(2,1)} %collective-permute-done.16.refs_2_), custom_call_target="tpu_custom_call" | custom-call | tf_op jit(solution)/shard_map/add_parts/pallas_call | solution.py:256
  75.0 1.8 %collective-permute-start.15 = (bf16[576,128]{1,0:T(8,128)(2,1)S(1)}, bf16[576,128]{1,0:T(8,128)(2,1)S(1)}, u32[]{:S(2)}, u32[]{:S(2)}) collective-permute-start(bf16[576,128]{1,0:T(8,128)(2,1)S(1)} %add_parts.8), channel_id=1, source_target_pairs={{16,0},{18,2},{20,4},{22,6},{24,8},{26,10},{28,12},{30,14},{0,16},... | collective-permute-start | bytes 442376 | tf_op jit(solution)/shard_map/ppermute | solution.py:310
  76.7 1.5 %collective-permute-start.17 = (bf16[576,128]{1,0:T(8,128)(2,1)S(1)}, bf16[576,128]{1,0:T(8,128)(2,1)S(1)}, u32[]{:S(2)}, u32[]{:S(2)}) collective-permute-start(bf16[576,128]{1,0:T(8,128)(2,1)S(1)} %add_parts.9), channel_id=1, source_target_pairs={{24,0},{26,2},{28,4},{30,6},{16,8},{18,10},{20,12},{22,14},{8,16},... | collective-permute-start | bytes 442376 | tf_op jit(solution)/shard_map/ppermute | solution.py:310
  78.3 9.8 %weight_grad.1 = f32[24,10,128,128]{3,2,1,0:T(8,128)} custom-call(s32[24,20]{1,0:T(8,128)S(1)} %get-tuple-element.14.rows_s, s32[16]{0:T(128)S(1)} %add_multiply_fusion.offs_s, s32[1]{0:T(128)} %bitcast.2.half_s, bf16[2304,128]{1,0:T(8,128)(2,1)S(1)} %pack.2.refs_0_, bf16[2304,128]{1,0:T(8,128)(2,1)S(1)} %pack.3.refs_1_, ...), custom_call_target="tpu_custom_call" | custom-call | flops 2013265920 | bytes 15728640 | tf_op jit(solution)/shard_map/weight_grad/pallas_call | solution.py:190
  88.1 0.8 fusion
  (28 shorter events, 0.2 us)
Async XLA Ops:
  0.6 10.2 %collective-permute-start.2 = (bf16[576,128]{1,0:T(8,128)(2,1)}, bf16[576,128]{1,0:T(8,128)(2,1)S(1)}, u32[]{:S(2)}, u32[]{:S(2)}) collective-permute-start(bf16[576,128]{1,0:T(8,128)(2,1)} %bitcast.4), channel_id=1, source_target_pairs={{24,0},{26,2},{28,4},{30,6},{16,8},{18,10},{20,12},{22,14},{8,16},... | collective-permute-start | bytes 442376 | tf_op jit(solution)/shard_map/ppermute | solution.py:310
  5.8 12.7 %collective-permute-start.1 = (bf16[576,128]{1,0:T(8,128)(2,1)}, bf16[576,128]{1,0:T(8,128)(2,1)S(1)}, u32[]{:S(2)}, u32[]{:S(2)}) collective-permute-start(bf16[576,128]{1,0:T(8,128)(2,1)} %bitcast.5), channel_id=1, source_target_pairs={{16,0},{18,2},{20,4},{22,6},{24,8},{26,10},{28,12},{30,14},{0,16},... | collective-permute-start | bytes 442376 | tf_op jit(solution)/shard_map/ppermute | solution.py:310
  5.8 14.2 %collective-permute-start = (bf16[576,128]{1,0:T(8,128)(2,1)}, bf16[576,128]{1,0:T(8,128)(2,1)S(1)}, u32[]{:S(2)}, u32[]{:S(2)}) collective-permute-start(bf16[576,128]{1,0:T(8,128)(2,1)} %bitcast.6), channel_id=1, source_target_pairs={{8,0},{10,2},{12,4},{14,6},{0,8},{2,10},{4,12},{6,14},{24,16},{26,... | collective-permute-start | bytes 442376 | tf_op jit(solution)/shard_map/ppermute | solution.py:310
  6.4 15.1 %collective-permute-start.3 = (bf16[576,128]{1,0:T(8,128)(2,1)}, bf16[576,128]{1,0:T(8,128)(2,1)S(1)}, u32[]{:S(2)}, u32[]{:S(2)}) collective-permute-start(bf16[576,128]{1,0:T(8,128)(2,1)} %bitcast.7), channel_id=1, source_target_pairs={{4,0},{6,2},{0,4},{2,6},{12,8},{14,10},{8,12},{10,14},{20,16},{22,... | collective-permute-start | bytes 442376 | tf_op jit(solution)/shard_map/ppermute | solution.py:310
  10.8 10.8 %collective-permute-start.6 = (bf16[576,128]{1,0:T(8,128)(2,1)S(1)}, bf16[576,128]{1,0:T(8,128)(2,1)S(1)}, u32[]{:S(2)}, u32[]{:S(2)}) collective-permute-start(bf16[576,128]{1,0:T(8,128)(2,1)S(1)} %collective-permute-done.2.refs_3_), channel_id=1, source_target_pairs={{4,0},{6,2},{0,4},{2,6},{12,8},{14,10},{8,12},{10,14},{20,16},{22,... | collective-permute-start | bytes 442376 | tf_op jit(solution)/shard_map/ppermute | solution.py:310
  18.5 6.5 %collective-permute-start.5 = (bf16[576,128]{1,0:T(8,128)(2,1)S(1)}, bf16[576,128]{1,0:T(8,128)(2,1)S(1)}, u32[]{:S(2)}, u32[]{:S(2)}) collective-permute-start(bf16[576,128]{1,0:T(8,128)(2,1)S(1)} %collective-permute-done.1.refs_2_), channel_id=1, source_target_pairs={{4,0},{6,2},{0,4},{2,6},{12,8},{14,10},{8,12},{10,14},{20,16},{22,... | collective-permute-start | bytes 442376 | tf_op jit(solution)/shard_map/ppermute | solution.py:310
  20.0 6.6 %collective-permute-start.4 = (bf16[576,128]{1,0:T(8,128)(2,1)S(1)}, bf16[576,128]{1,0:T(8,128)(2,1)S(1)}, u32[]{:S(2)}, u32[]{:S(2)}) collective-permute-start(bf16[576,128]{1,0:T(8,128)(2,1)S(1)} %collective-permute-done.refs_1_), channel_id=1, source_target_pairs={{4,0},{6,2},{0,4},{2,6},{12,8},{14,10},{8,12},{10,14},{20,16},{22,... | collective-permute-start | bytes 442376 | tf_op jit(solution)/shard_map/ppermute | solution.py:310
  20.5 0.9 %copy-start.5 = (bf16[128,576]{0,1:T(8,128)(2,1)S(1)}, bf16[128,576]{0,1:T(8,128)(2,1)}, u32[]{:S(2)}) copy-start(bf16[128,576]{0,1:T(8,128)(2,1)} %param.7) | copy-start | bytes 442372
  21.4 9.9 %collective-permute-start.7 = (bf16[2304,128]{1,0:T(8,128)(2,1)S(1)}, bf16[2304,128]{1,0:T(8,128)(2,1)S(1)}, u32[]{:S(2)}, u32[]{:S(2)}) collective-permute-start(bf16[2304,128]{1,0:T(8,128)(2,1)S(1)} %pack.2.refs_0_), channel_id=1, source_target_pairs={{2,0},{0,2},{6,4},{4,6},{10,8},{8,10},{14,12},{12,14},{18,16},{16,... | collective-permute-start | bytes 1769480 | tf_op jit(solution)/shard_map/ppermute | solution.py:310
  26.6 4.8 %collective-permute-start.8 = (bf16[2304,128]{1,0:T(8,128)(2,1)S(1)}, bf16[2304,128]{1,0:T(8,128)(2,1)S(1)}, u32[]{:S(2)}, u32[]{:S(2)}) collective-permute-start(bf16[2304,128]{1,0:T(8,128)(2,1)S(1)} %pack.3.refs_1_), channel_id=1, source_target_pairs={{2,0},{0,2},{6,4},{4,6},{10,8},{8,10},{14,12},{12,14},{18,16},{16,... | collective-permute-start | bytes 1769480 | tf_op jit(solution)/shard_map/ppermute | solution.py:310
  26.7 1.1 %copy-start.4 = (bf16[128,3072]{1,0:T(8,128)(2,1)S(1)}, bf16[128,3072]{1,0:T(8,128)(2,1)}, u32[]{:S(2)}) copy-start(bf16[128,3072]{1,0:T(8,128)(2,1)} %refs_0_.1) | copy-start | bytes 2359300
  27.8 0.7 copy-start.8
  29.3 25.9 %collective-permute-start.18 = (bf16[2304,128]{1,0:T(8,128)(2,1)S(1)}, bf16[2304,128]{1,0:T(8,128)(2,1)}, u32[]{:S(2)}, u32[]{:S(2)}) collective-permute-start(bf16[2304,128]{1,0:T(8,128)(2,1)S(1)} %pack.2.refs_0_), channel_id=1, source_target_pairs={{0,1},{1,0},{2,3},{3,2},{4,5},{5,4},{6,7},{7,6},{8,9},{9,8},{10,11... | collective-permute-start | bytes 1769480 | tf_op jit(solution)/shard_map/ppermute | solution.py:316
  30.8 27.4 %collective-permute-start.19 = (bf16[2304,128]{1,0:T(8,128)(2,1)S(1)}, bf16[2304,128]{1,0:T(8,128)(2,1)}, u32[]{:S(2)}, u32[]{:S(2)}) collective-permute-start(bf16[2304,128]{1,0:T(8,128)(2,1)S(1)} %pack.3.refs_1_), channel_id=1, source_target_pairs={{0,1},{1,0},{2,3},{3,2},{4,5},{5,4},{6,7},{7,6},{8,9},{9,8},{10,11... | collective-permute-start | bytes 1769480 | tf_op jit(solution)/shard_map/ppermute | solution.py:316
  53.4 7.2 %copy-start = (bf16[2304,128]{1,0:T(8,128)(2,1)}, bf16[2304,128]{1,0:T(8,128)(2,1)S(1)}, u32[]{:S(2)}) copy-start(bf16[2304,128]{1,0:T(8,128)(2,1)S(1)} %get-tuple-element.19.refs_0_) | copy-start | bytes 1769476
  53.4 4.8 %collective-permute-start.10 = (bf16[2304,128]{1,0:T(8,128)(2,1)S(1)}, bf16[2304,128]{1,0:T(8,128)(2,1)S(1)}, u32[]{:S(2)}, u32[]{:S(2)}) collective-permute-start(bf16[2304,128]{1,0:T(8,128)(2,1)S(1)} %get-tuple-element.20), channel_id=1, source_target_pairs={{2,0},{0,2},{6,4},{4,6},{10,8},{8,10},{14,12},{12,14},{18,16},{16,... | collective-permute-start | bytes 1769480 | tf_op jit(solution)/shard_map/ppermute | solution.py:310
  53.5 24.8 %collective-permute-start.22 = (bf16[128,3072]{1,0:T(8,128)(2,1)}, bf16[128,3072]{1,0:T(8,128)(2,1)}, u32[]{:S(2)}, u32[]{:S(2)}) collective-permute-start(bf16[128,3072]{1,0:T(8,128)(2,1)} %get-tuple-element.24.refs_8_), channel_id=1, source_target_pairs={{0,1},{1,0},{2,3},{3,2},{4,5},{5,4},{6,7},{7,6},{8,9},{9,8},{10,11... | collective-permute-start | bytes 2359304 | tf_op jit(solution)/shard_map/ppermute | solution.py:316
  55.0 5.6 %collective-permute-start.9 = (bf16[2304,128]{1,0:T(8,128)(2,1)S(1)}, bf16[2304,128]{1,0:T(8,128)(2,1)S(1)}, u32[]{:S(2)}, u32[]{:S(2)}) collective-permute-start(bf16[2304,128]{1,0:T(8,128)(2,1)S(1)} %get-tuple-element.18), channel_id=1, source_target_pairs={{2,0},{0,2},{6,4},{4,6},{10,8},{8,10},{14,12},{12,14},{18,16},{16,... | collective-permute-start | bytes 1769480 | tf_op jit(solution)/shard_map/ppermute | solution.py:310
  55.2 19.8 %collective-permute-start.20 = (bf16[2304,128]{1,0:T(8,128)(2,1)}, bf16[2304,128]{1,0:T(8,128)(2,1)}, u32[]{:S(2)}, u32[]{:S(2)}) collective-permute-start(bf16[2304,128]{1,0:T(8,128)(2,1)} %collective-permute-done.18.refs_4_), channel_id=1, source_target_pairs={{2,0},{0,2},{6,4},{4,6},{10,8},{8,10},{14,12},{12,14},{18,16},{16,... | collective-permute-start | bytes 1769480 | tf_op jit(solution)/shard_map/ppermute | solution.py:310
  58.3 18.5 %collective-permute-start.21 = (bf16[2304,128]{1,0:T(8,128)(2,1)}, bf16[2304,128]{1,0:T(8,128)(2,1)}, u32[]{:S(2)}, u32[]{:S(2)}) collective-permute-start(bf16[2304,128]{1,0:T(8,128)(2,1)} %collective-permute-done.19.refs_5_), channel_id=1, source_target_pairs={{2,0},{0,2},{6,4},{4,6},{10,8},{8,10},{14,12},{12,14},{18,16},{16,... | collective-permute-start | bytes 1769480 | tf_op jit(solution)/shard_map/ppermute | solution.py:310
  58.3 2.4 %copy-start.2 = (bf16[2304,128]{1,0:T(8,128)(2,1)}, bf16[2304,128]{1,0:T(8,128)(2,1)S(1)}, u32[]{:S(2)}) copy-start(bf16[2304,128]{1,0:T(8,128)(2,1)S(1)} %collective-permute-done.10.refs_1_) | copy-start | bytes 1769476
  59.1 6.7 %collective-permute-start.12 = (bf16[576,128]{1,0:T(8,128)(2,1)S(1)}, bf16[576,128]{1,0:T(8,128)(2,1)S(1)}, u32[]{:S(2)}, u32[]{:S(2)}) collective-permute-start(bf16[576,128]{1,0:T(8,128)(2,1)S(1)} %get-tuple-element.21), channel_id=1, source_target_pairs={{4,0},{6,2},{0,4},{2,6},{12,8},{14,10},{8,12},{10,14},{20,16},{22,... | collective-permute-start | bytes 442376 | tf_op jit(solution)/shard_map/ppermute | solution.py:310
  60.6 10.5 %collective-permute-start.14 = (bf16[576,128]{1,0:T(8,128)(2,1)}, bf16[576,128]{1,0:T(8,128)(2,1)}, u32[]{:S(2)}, u32[]{:S(2)}) collective-permute-start(bf16[576,128]{1,0:T(8,128)(2,1)} %get-tuple-element.22), channel_id=1, source_target_pairs={{4,0},{6,2},{0,4},{2,6},{12,8},{14,10},{8,12},{10,14},{20,16},{22,... | collective-permute-start | bytes 442376 | tf_op jit(solution)/shard_map/ppermute | solution.py:310
  65.9 0.7 copy-start.6
  66.5 6.2 %collective-permute-start.16 = (bf16[576,128]{1,0:T(8,128)(2,1)}, bf16[576,128]{1,0:T(8,128)(2,1)}, u32[]{:S(2)}, u32[]{:S(2)}) collective-permute-start(bf16[576,128]{1,0:T(8,128)(2,1)} %get-tuple-element.23), channel_id=1, source_target_pairs={{4,0},{6,2},{0,4},{2,6},{12,8},{14,10},{8,12},{10,14},{20,16},{22,... | collective-permute-start | bytes 442376 | tf_op jit(solution)/shard_map/ppermute | solution.py:310
  68.0 1.1 %copy-start.1 = (bf16[2304,128]{1,0:T(8,128)(2,1)S(1)}, bf16[2304,128]{1,0:T(8,128)(2,1)}, u32[]{:S(2)}) copy-start(bf16[2304,128]{1,0:T(8,128)(2,1)} %copy-done) | copy-start | bytes 1769476
  69.1 1.1 %copy-start.3 = (bf16[2304,128]{1,0:T(8,128)(2,1)S(1)}, bf16[2304,128]{1,0:T(8,128)(2,1)}, u32[]{:S(2)}) copy-start(bf16[2304,128]{1,0:T(8,128)(2,1)} %copy-done.2) | copy-start | bytes 1769476
  70.2 0.9 %copy-start.7 = (bf16[576,128]{1,0:T(8,128)(2,1)S(1)}, bf16[576,128]{1,0:T(8,128)(2,1)}, u32[]{:S(2)}) copy-start(bf16[576,128]{1,0:T(8,128)(2,1)} %copy-done.6) | copy-start | bytes 442372
  71.2 16.9 %collective-permute-start.11 = (bf16[576,128]{1,0:T(8,128)(2,1)S(1)}, bf16[576,128]{1,0:T(8,128)(2,1)S(1)}, u32[]{:S(2)}, u32[]{:S(2)}) collective-permute-start(bf16[576,128]{1,0:T(8,128)(2,1)S(1)} %add_parts.5), channel_id=1, source_target_pairs={{4,0},{6,2},{0,4},{2,6},{12,8},{14,10},{8,12},{10,14},{20,16},{22,... | collective-permute-start | bytes 442376 | tf_op jit(solution)/shard_map/ppermute | solution.py:310
  72.7 15.3 %collective-permute-start.13 = (bf16[576,128]{1,0:T(8,128)(2,1)S(1)}, bf16[576,128]{1,0:T(8,128)(2,1)S(1)}, u32[]{:S(2)}, u32[]{:S(2)}) collective-permute-start(bf16[576,128]{1,0:T(8,128)(2,1)S(1)} %add_parts.7), channel_id=1, source_target_pairs={{8,0},{10,2},{12,4},{14,6},{0,8},{2,10},{4,12},{6,14},{24,16},{26,... | collective-permute-start | bytes 442376 | tf_op jit(solution)/shard_map/ppermute | solution.py:310
  75.0 13.1 %collective-permute-start.15 = (bf16[576,128]{1,0:T(8,128)(2,1)S(1)}, bf16[576,128]{1,0:T(8,128)(2,1)S(1)}, u32[]{:S(2)}, u32[]{:S(2)}) collective-permute-start(bf16[576,128]{1,0:T(8,128)(2,1)S(1)} %add_parts.8), channel_id=1, source_target_pairs={{16,0},{18,2},{20,4},{22,6},{24,8},{26,10},{28,12},{30,14},{0,16},... | collective-permute-start | bytes 442376 | tf_op jit(solution)/shard_map/ppermute | solution.py:310
  76.7 11.3 %collective-permute-start.17 = (bf16[576,128]{1,0:T(8,128)(2,1)S(1)}, bf16[576,128]{1,0:T(8,128)(2,1)S(1)}, u32[]{:S(2)}, u32[]{:S(2)}) collective-permute-start(bf16[576,128]{1,0:T(8,128)(2,1)S(1)} %add_parts.9), channel_id=1, source_target_pairs={{24,0},{26,2},{28,4},{30,6},{16,8},{18,10},{20,12},{22,14},{8,16},... | collective-permute-start | bytes 442376 | tf_op jit(solution)/shard_map/ppermute | solution.py:310

commit v4 on v3

--- a/solution.py
+++ b/solution.py
@@ -67,12 +67,7 @@
     lax.fori_loop(0, blocks, turn, 0, unroll=4)
     step = 2 if slots % 2 == 0 else 1
 
-    def ahead(c):
-        v = 0.0
-        for k in range(0, slots, step):
-            picked = jnp.concatenate([xs[rows_s[c, k + i]] for i in range(step)], axis=1)
-            right = w[c, k : k + step].reshape(step * side, side)
-            v = v + jnp.dot(picked, right, preferred_element_type=jnp.float32)
+    def activate(c, v):
         v2 = v * v
         t = jnp.tanh(SQRT_2_PI * (v + CUBIC * (v * v2)))
         half = 0.5 * (1.0 + t)
@@ -81,26 +76,35 @@
         slope = cot[:, block(c, side)].astype(jnp.float32) * slope
         slopes[:, block(c, side)] = slope.astype(slopes.dtype)
 
-    def back(c):
-        turned = slopes[:, block(c, side)].T
-        for k in range(0, slots, step):
-            left = w[c, k : k + step].reshape(step * side, side)
-            part_sum = jnp.dot(left, turned, preferred_element_type=jnp.float32)
-            for i in range(step):
-                acc[block(rows_s[c, k + i], side), :] += part_sum[i * side : (i + 1) * side]
+    def ahead(c, k):
+        picked = jnp.concatenate([xs[rows_s[c, k + i]] for i in range(step)], axis=1)
+        right = w[c, k : k + step].reshape(step * side, side)
+        return jnp.dot(picked, right, preferred_element_type=jnp.float32)
+
+    def back(c, k, turned):
+        left = w[c, k : k + step].reshape(step * side, side)
+        part_sum = jnp.dot(left, turned, preferred_element_type=jnp.float32)
+        for i in range(step):
+            acc[block(rows_s[c, k + i], side), :] += part_sum[i * side : (i + 1) * side]
 
     def one(c, carry):
         out(c).start()
         weights(c + 1).wait()
-        ahead(c + 1)
-        back(c)
+        turned = slopes[:, block(c, side)].T
+        v = 0.0
+        for k in range(0, slots, step):
+            v = v + ahead(c + 1, k)
+            back(c, k, turned)
+        activate(c + 1, v)
         return carry
 
     weights(0).wait()
-    ahead(0)
+    activate(0, sum(ahead(0, k) for k in range(0, slots, step)))
     lax.fori_loop(0, cols - 1, one, 0)
     out(cols - 1).start()
-    back(cols - 1)
+    turned = slopes[:, block(cols - 1, side)].T
+    for k in range(0, slots, step):
+        back(cols - 1, k, turned)
 
     for j, shard in enumerate(shards_of(dx_refs, part)):
         rows = pl.ds(pl.multiple_of(offs_s[j], 16), part)
@@ -365,7 +369,9 @@
 def solution(mesh):
     in_specs = (P("mp", "dp"), P("dp", None, None, None), P("dp", None), P("mp", "dp"))
     out_specs = (P("mp", "dp"), P("mp", "dp"), P("dp", "mp", None, None))
-    step = jax.shard_map(body, mesh=mesh, in_specs=in_specs, out_specs=out_specs, check_vma=False)
+    step = jax.shard_map(
+        body, mesh=mesh, in_specs=in_specs, out_specs=out_specs, check_vma=False
+    )
     n, mp = mesh.shape["dp"], mesh.shape["mp"]
     if not direct(n, mp):
         return step

time: 89.3 us -> 89.3 us (level)
  Pallas kernels: 34.9 us -> 30.3 us
  waiting for transfers between devices: 21.1 us -> 25.6 us
    pallas_call x1, Pallas kernels: 22.1 us -> 17.5 us  [forward(): pl.pallas_call(functools.partial(forward_kernel, len(arrays), len(outs),...]
    ppermute x3, waiting for transfers between devices: 2.71 us -> 7.21 us  [across(): return lax.ppermute(a, 'mp', [(i, i ^ 1) for i in range(mp)])]
  transfers between devices with their start and end apart: 23 -> 23, of which waited for: 6 -> 6; matrix products, arithmetic and copies ran while one was open for 1% -> 1% of each run, Pallas kernels for 39% -> 34%
where the time goes in v4:
time: 89.3 us; the launch traced here: 88.9 us
  Pallas kernels  30.3 us (34%)
  waiting for transfers between devices  25.6 us (29%)
  starting transfers between devices  24.1 us (27%)
  local copies, waits for them, and re-layouts  6.46 us (7%)
  other arithmetic  1.48 us (2%)
    ppermute x20, starting transfers between devices, permute(): return lax.ppermute(a, 'dp', [(source(i), i) for i in range(n)])  20.5 us
    ppermute x20, waiting for transfers between devices, permute(): return lax.ppermute(a, 'dp', [(source(i), i) for i in range(n)])  18.4 us
    pallas_call x1, Pallas kernels, forward(): pl.pallas_call(functools.partial(forward_kernel, len(arrays), len(outs),...  17.5 us
    pallas_call x1, Pallas kernels, weight_grad(): pl.pallas_call(functools.partial(weight_kernel, len(planes), len(planes[0...  9.78 us
    ppermute x3, waiting for transfers between devices, across(): return lax.ppermute(a, 'mp', [(i, i ^ 1) for i in range(mp)])  7.21 us
    unnamed x18, local copies, waits for them, and re-layouts  6.46 us
    ppermute x3, starting transfers between devices, across(): return lax.ppermute(a, 'mp', [(i, i ^ 1) for i in range(mp)])  3.61 us
    pallas_call x5, Pallas kernels, add_parts(): pl.pallas_call(functools.partial(sum_kernel, plan, part, len(arrays)), in...  2.89 us
  transfers between devices with their start and end apart: 23, of which 6 were waited for; matrix products, arithmetic and copies ran while one was open for 1% of the time, Pallas kernels for 34%

profile of v4, /device:TPU:0, one launch (start us, length us, event | category | flops | bytes accessed | tf_op | source)
XLA Modules:
  0.0 88.9 jit_solution(8678333252348349779)
XLA Ops:
  0.6 5.1 %collective-permute-start.2 = (bf16[576,128]{1,0:T(8,128)(2,1)}, bf16[576,128]{1,0:T(8,128)(2,1)S(1)}, u32[]{:S(2)}, u32[]{:S(2)}) collective-permute-start(bf16[576,128]{1,0:T(8,128)(2,1)} %bitcast.4), channel_id=1, source_target_pairs={{24,0},{26,2},{28,4},{30,6},{16,8},{18,10},{20,12},{22,14},{8,16},... | collective-permute-start | bytes 442376 | tf_op jit(solution)/shard_map/ppermute | solution.py:314
  5.8 0.0 collective-permute-start.1
  5.8 0.6 collective-permute-start
  6.4 1.6 %collective-permute-start.3 = (bf16[576,128]{1,0:T(8,128)(2,1)}, bf16[576,128]{1,0:T(8,128)(2,1)S(1)}, u32[]{:S(2)}, u32[]{:S(2)}) collective-permute-start(bf16[576,128]{1,0:T(8,128)(2,1)} %bitcast.7), channel_id=1, source_target_pairs={{4,0},{6,2},{0,4},{2,6},{12,8},{14,10},{8,12},{10,14},{20,16},{22,... | collective-permute-start | bytes 442376 | tf_op jit(solution)/shard_map/ppermute | solution.py:314
  8.1 2.7 %collective-permute-done.2.refs_3_ = bf16[576,128]{1,0:T(8,128)(2,1)S(1)} collective-permute-done((bf16[576,128]{1,0:T(8,128)(2,1)}, bf16[576,128]{1,0:T(8,128)(2,1)S(1)}, u32[]{:S(2)}, u32[]{:S(2)}) %collective-permute-start.2) | collective-permute-done | bytes 147488 | tf_op jit(solution)/shard_map/ppermute | solution.py:314
  10.8 1.7 %collective-permute-start.6 = (bf16[576,128]{1,0:T(8,128)(2,1)S(1)}, bf16[576,128]{1,0:T(8,128)(2,1)S(1)}, u32[]{:S(2)}, u32[]{:S(2)}) collective-permute-start(bf16[576,128]{1,0:T(8,128)(2,1)S(1)} %collective-permute-done.2.refs_3_), channel_id=1, source_target_pairs={{4,0},{6,2},{0,4},{2,6},{12,8},{14,10},{8,12},{10,14},{20,16},{22,... | collective-permute-start | bytes 442376 | tf_op jit(solution)/shard_map/ppermute | solution.py:314
  12.4 6.0 %collective-permute-done.1.refs_2_ = bf16[576,128]{1,0:T(8,128)(2,1)S(1)} collective-permute-done((bf16[576,128]{1,0:T(8,128)(2,1)}, bf16[576,128]{1,0:T(8,128)(2,1)S(1)}, u32[]{:S(2)}, u32[]{:S(2)}) %collective-permute-start.1) | collective-permute-done | bytes 147488 | tf_op jit(solution)/shard_map/ppermute | solution.py:314
  18.5 1.5 %collective-permute-start.5 = (bf16[576,128]{1,0:T(8,128)(2,1)S(1)}, bf16[576,128]{1,0:T(8,128)(2,1)S(1)}, u32[]{:S(2)}, u32[]{:S(2)}) collective-permute-start(bf16[576,128]{1,0:T(8,128)(2,1)S(1)} %collective-permute-done.1.refs_2_), channel_id=1, source_target_pairs={{4,0},{6,2},{0,4},{2,6},{12,8},{14,10},{8,12},{10,14},{20,16},{22,... | collective-permute-start | bytes 442376 | tf_op jit(solution)/shard_map/ppermute | solution.py:314
  20.0 0.0 collective-permute-done.refs_1_
  20.0 0.5 collective-permute-start.4
  20.5 0.9 %copy-done.5 = bf16[128,576]{0,1:T(8,128)(2,1)S(1)} copy-done((bf16[128,576]{0,1:T(8,128)(2,1)S(1)}, bf16[128,576]{0,1:T(8,128)(2,1)}, u32[]{:S(2)}) %copy-start.5) | copy-done | bytes 147480
  21.4 0.1 collective-permute-start.7
  21.5 0.0 collective-permute-done.3.refs_0_
  21.5 3.4 %collective-permute-done.5.refs_2_ = bf16[576,128]{1,0:T(8,128)(2,1)S(1)} collective-permute-done((bf16[576,128]{1,0:T(8,128)(2,1)S(1)}, bf16[576,128]{1,0:T(8,128)(2,1)S(1)}, u32[]{:S(2)}, u32[]{:S(2)}) %collective-permute-start.5) | collective-permute-done | bytes 147488 | tf_op jit(solution)/shard_map/ppermute | solution.py:314
  25.0 1.6 %collective-permute-done.4.refs_1_ = bf16[576,128]{1,0:T(8,128)(2,1)S(1)} collective-permute-done((bf16[576,128]{1,0:T(8,128)(2,1)S(1)}, bf16[576,128]{1,0:T(8,128)(2,1)S(1)}, u32[]{:S(2)}, u32[]{:S(2)}) %collective-permute-start.4) | collective-permute-done | bytes 147488 | tf_op jit(solution)/shard_map/ppermute | solution.py:314
  26.6 0.1 collective-permute-start.8
  26.7 0.0 copy-start.4
  26.7 1.1 %copy-done.4 = bf16[128,3072]{1,0:T(8,128)(2,1)S(1)} copy-done((bf16[128,3072]{1,0:T(8,128)(2,1)S(1)}, bf16[128,3072]{1,0:T(8,128)(2,1)}, u32[]{:S(2)}) %copy-start.4) | copy-done | bytes 786456
  27.8 0.7 copy-done.8
  28.6 0.1 stage.1
  28.6 0.7 add_multiply_fusion.offs_s
  29.3 1.5 %collective-permute-start.18 = (bf16[2304,128]{1,0:T(8,128)(2,1)S(1)}, bf16[2304,128]{1,0:T(8,128)(2,1)}, u32[]{:S(2)}, u32[]{:S(2)}) collective-permute-start(bf16[2304,128]{1,0:T(8,128)(2,1)S(1)} %pack.2.refs_0_), channel_id=1, source_target_pairs={{0,1},{1,0},{2,3},{3,2},{4,5},{5,4},{6,7},{7,6},{8,9},{9,8},{10,11... | collective-permute-start | bytes 1769480 | tf_op jit(solution)/shard_map/ppermute | solution.py:320
  30.8 0.5 collective-permute-start.19
  31.3 17.5 %forward.1 = (bf16[128,3072]{1,0:T(8,128)(2,1)}, bf16[128,3072]{1,0:T(8,128)(2,1)}, bf16[2304,128]{1,0:T(8,128)(2,1)S(1)}, bf16[2304,128]{1,0:T(8,128)(2,1)S(1)}...) custom-call(s32[24,20]{1,0:T(8,128)S(1)} %get-tuple-element.14.rows_s, s32[16]{0:T(128)S(1)} %add_multiply_fusion.offs_s, ...), custom_call_target="tpu_custom_call" | custom-call | flops 4026531840 | bytes 15728640 | tf_op jit(solution)/shard_map/forward/pallas_call | solution.py:132
  48.9 0.0 copy-start
  48.9 0.1 collective-permute-start.10
  48.9 1.6 %collective-permute-start.22 = (bf16[128,3072]{1,0:T(8,128)(2,1)}, bf16[128,3072]{1,0:T(8,128)(2,1)}, u32[]{:S(2)}, u32[]{:S(2)}) collective-permute-start(bf16[128,3072]{1,0:T(8,128)(2,1)} %get-tuple-element.24.refs_8_), channel_id=1, source_target_pairs={{0,1},{1,0},{2,3},{3,2},{4,5},{5,4},{6,7},{7,6},{8,9},{9,8},{10,11... | collective-permute-start | bytes 2359304 | tf_op jit(solution)/shard_map/ppermute | solution.py:320
  50.5 0.2 collective-permute-start.9
  50.7 0.4 collective-permute-start.20
  51.0 7.2 %collective-permute-done.19.refs_5_ = bf16[2304,128]{1,0:T(8,128)(2,1)} collective-permute-done((bf16[2304,128]{1,0:T(8,128)(2,1)S(1)}, bf16[2304,128]{1,0:T(8,128)(2,1)}, u32[]{:S(2)}, u32[]{:S(2)}) %collective-permute-start.19) | collective-permute-done | bytes 589856 | tf_op jit(solution)/shard_map/ppermute | solution.py:320
  58.3 0.9 add_parts.6
  59.1 1.5 %collective-permute-start.12 = (bf16[576,128]{1,0:T(8,128)(2,1)S(1)}, bf16[576,128]{1,0:T(8,128)(2,1)S(1)}, u32[]{:S(2)}, u32[]{:S(2)}) collective-permute-start(bf16[576,128]{1,0:T(8,128)(2,1)S(1)} %get-tuple-element.21), channel_id=1, source_target_pairs={{4,0},{6,2},{0,4},{2,6},{12,8},{14,10},{8,12},{10,14},{20,16},{22,... | collective-permute-start | bytes 442376 | tf_op jit(solution)/shard_map/ppermute | solution.py:314
  60.6 0.6 collective-permute-start.14
  61.2 4.6 %collective-permute-done.12.refs_2_ = bf16[576,128]{1,0:T(8,128)(2,1)S(1)} collective-permute-done((bf16[576,128]{1,0:T(8,128)(2,1)S(1)}, bf16[576,128]{1,0:T(8,128)(2,1)S(1)}, u32[]{:S(2)}, u32[]{:S(2)}) %collective-permute-start.12) | collective-permute-done | bytes 147488 | tf_op jit(solution)/shard_map/ppermute | solution.py:314
  65.9 0.7 copy-done.6
  66.5 1.5 %collective-permute-start.16 = (bf16[576,128]{1,0:T(8,128)(2,1)}, bf16[576,128]{1,0:T(8,128)(2,1)}, u32[]{:S(2)}, u32[]{:S(2)}) collective-permute-start(bf16[576,128]{1,0:T(8,128)(2,1)} %get-tuple-element.23), channel_id=1, source_target_pairs={{4,0},{6,2},{0,4},{2,6},{12,8},{14,10},{8,12},{10,14},{20,16},{22,... | collective-permute-start | bytes 442376 | tf_op jit(solution)/shard_map/ppermute | solution.py:314
  68.0 1.1 %copy-done.1 = bf16[2304,128]{1,0:T(8,128)(2,1)S(1)} copy-done((bf16[2304,128]{1,0:T(8,128)(2,1)S(1)}, bf16[2304,128]{1,0:T(8,128)(2,1)}, u32[]{:S(2)}) %copy-start.1) | copy-done | bytes 589848
  69.1 1.1 %copy-done.3 = bf16[2304,128]{1,0:T(8,128)(2,1)S(1)} copy-done((bf16[2304,128]{1,0:T(8,128)(2,1)S(1)}, bf16[2304,128]{1,0:T(8,128)(2,1)}, u32[]{:S(2)}) %copy-start.3) | copy-done | bytes 589848
  70.2 0.9 %copy-done.7 = bf16[576,128]{1,0:T(8,128)(2,1)S(1)} copy-done((bf16[576,128]{1,0:T(8,128)(2,1)S(1)}, bf16[576,128]{1,0:T(8,128)(2,1)}, u32[]{:S(2)}) %copy-start.7) | copy-done | bytes 147480
  71.1 0.1 add_parts.7
  71.2 0.6 collective-permute-start.11
  71.8 1.0 %add_parts.8 = bf16[576,128]{1,0:T(8,128)(2,1)S(1)} custom-call(bf16[2304,128]{1,0:T(8,128)(2,1)S(1)} %get-tuple-element.17.refs_0_, bf16[2304,128]{1,0:T(8,128)(2,1)S(1)} %collective-permute-done.9.refs_1_, bf16[576,128]{1,0:T(8,128)(2,1)} %collective-permute-done.14.refs_2_), custom_call_target="tpu_custom_call" | custom-call | tf_op jit(solution)/shard_map/add_parts/pallas_call | solution.py:260
  72.7 1.3 %collective-permute-start.13 = (bf16[576,128]{1,0:T(8,128)(2,1)S(1)}, bf16[576,128]{1,0:T(8,128)(2,1)S(1)}, u32[]{:S(2)}, u32[]{:S(2)}) collective-permute-start(bf16[576,128]{1,0:T(8,128)(2,1)S(1)} %add_parts.7), channel_id=1, source_target_pairs={{8,0},{10,2},{12,4},{14,6},{0,8},{2,10},{4,12},{6,14},{24,16},{26,... | collective-permute-start | bytes 442376 | tf_op jit(solution)/shard_map/ppermute | solution.py:314
  74.0 1.0 %add_parts.9 = bf16[576,128]{1,0:T(8,128)(2,1)S(1)} custom-call(bf16[2304,128]{1,0:T(8,128)(2,1)S(1)} %get-tuple-element.17.refs_0_, bf16[2304,128]{1,0:T(8,128)(2,1)S(1)} %collective-permute-done.9.refs_1_, bf16[576,128]{1,0:T(8,128)(2,1)} %collective-permute-done.16.refs_2_), custom_call_target="tpu_custom_call" | custom-call | tf_op jit(solution)/shard_map/add_parts/pallas_call | solution.py:260
  75.0 1.8 %collective-permute-start.15 = (bf16[576,128]{1,0:T(8,128)(2,1)S(1)}, bf16[576,128]{1,0:T(8,128)(2,1)S(1)}, u32[]{:S(2)}, u32[]{:S(2)}) collective-permute-start(bf16[576,128]{1,0:T(8,128)(2,1)S(1)} %add_parts.8), channel_id=1, source_target_pairs={{16,0},{18,2},{20,4},{22,6},{24,8},{26,10},{28,12},{30,14},{0,16},... | collective-permute-start | bytes 442376 | tf_op jit(solution)/shard_map/ppermute | solution.py:314
  76.7 1.5 %collective-permute-start.17 = (bf16[576,128]{1,0:T(8,128)(2,1)S(1)}, bf16[576,128]{1,0:T(8,128)(2,1)S(1)}, u32[]{:S(2)}, u32[]{:S(2)}) collective-permute-start(bf16[576,128]{1,0:T(8,128)(2,1)S(1)} %add_parts.9), channel_id=1, source_target_pairs={{24,0},{26,2},{28,4},{30,6},{16,8},{18,10},{20,12},{22,14},{8,16},... | collective-permute-start | bytes 442376 | tf_op jit(solution)/shard_map/ppermute | solution.py:314
  78.3 9.8 %weight_grad.1 = f32[24,10,128,128]{3,2,1,0:T(8,128)} custom-call(s32[24,20]{1,0:T(8,128)S(1)} %get-tuple-element.14.rows_s, s32[16]{0:T(128)S(1)} %add_multiply_fusion.offs_s, s32[1]{0:T(128)} %bitcast.2.half_s, bf16[2304,128]{1,0:T(8,128)(2,1)S(1)} %pack.2.refs_0_, bf16[2304,128]{1,0:T(8,128)(2,1)S(1)} %pack.3.refs_1_, ...), custom_call_target="tpu_custom_call" | custom-call | flops 2013265920 | bytes 15728640 | tf_op jit(solution)/shard_map/weight_grad/pallas_call | solution.py:194
  88.1 0.8 fusion
  (28 shorter events, 0.2 us)
Async XLA Ops:
  0.6 10.2 %collective-permute-start.2 = (bf16[576,128]{1,0:T(8,128)(2,1)}, bf16[576,128]{1,0:T(8,128)(2,1)S(1)}, u32[]{:S(2)}, u32[]{:S(2)}) collective-permute-start(bf16[576,128]{1,0:T(8,128)(2,1)} %bitcast.4), channel_id=1, source_target_pairs={{24,0},{26,2},{28,4},{30,6},{16,8},{18,10},{20,12},{22,14},{8,16},... | collective-permute-start | bytes 442376 | tf_op jit(solution)/shard_map/ppermute | solution.py:314
  5.8 12.7 %collective-permute-start.1 = (bf16[576,128]{1,0:T(8,128)(2,1)}, bf16[576,128]{1,0:T(8,128)(2,1)S(1)}, u32[]{:S(2)}, u32[]{:S(2)}) collective-permute-start(bf16[576,128]{1,0:T(8,128)(2,1)} %bitcast.5), channel_id=1, source_target_pairs={{16,0},{18,2},{20,4},{22,6},{24,8},{26,10},{28,12},{30,14},{0,16},... | collective-permute-start | bytes 442376 | tf_op jit(solution)/shard_map/ppermute | solution.py:314
  5.8 14.2 %collective-permute-start = (bf16[576,128]{1,0:T(8,128)(2,1)}, bf16[576,128]{1,0:T(8,128)(2,1)S(1)}, u32[]{:S(2)}, u32[]{:S(2)}) collective-permute-start(bf16[576,128]{1,0:T(8,128)(2,1)} %bitcast.6), channel_id=1, source_target_pairs={{8,0},{10,2},{12,4},{14,6},{0,8},{2,10},{4,12},{6,14},{24,16},{26,... | collective-permute-start | bytes 442376 | tf_op jit(solution)/shard_map/ppermute | solution.py:314
  6.4 15.1 %collective-permute-start.3 = (bf16[576,128]{1,0:T(8,128)(2,1)}, bf16[576,128]{1,0:T(8,128)(2,1)S(1)}, u32[]{:S(2)}, u32[]{:S(2)}) collective-permute-start(bf16[576,128]{1,0:T(8,128)(2,1)} %bitcast.7), channel_id=1, source_target_pairs={{4,0},{6,2},{0,4},{2,6},{12,8},{14,10},{8,12},{10,14},{20,16},{22,... | collective-permute-start | bytes 442376 | tf_op jit(solution)/shard_map/ppermute | solution.py:314
  10.8 10.8 %collective-permute-start.6 = (bf16[576,128]{1,0:T(8,128)(2,1)S(1)}, bf16[576,128]{1,0:T(8,128)(2,1)S(1)}, u32[]{:S(2)}, u32[]{:S(2)}) collective-permute-start(bf16[576,128]{1,0:T(8,128)(2,1)S(1)} %collective-permute-done.2.refs_3_), channel_id=1, source_target_pairs={{4,0},{6,2},{0,4},{2,6},{12,8},{14,10},{8,12},{10,14},{20,16},{22,... | collective-permute-start | bytes 442376 | tf_op jit(solution)/shard_map/ppermute | solution.py:314
  18.5 6.5 %collective-permute-start.5 = (bf16[576,128]{1,0:T(8,128)(2,1)S(1)}, bf16[576,128]{1,0:T(8,128)(2,1)S(1)}, u32[]{:S(2)}, u32[]{:S(2)}) collective-permute-start(bf16[576,128]{1,0:T(8,128)(2,1)S(1)} %collective-permute-done.1.refs_2_), channel_id=1, source_target_pairs={{4,0},{6,2},{0,4},{2,6},{12,8},{14,10},{8,12},{10,14},{20,16},{22,... | collective-permute-start | bytes 442376 | tf_op jit(solution)/shard_map/ppermute | solution.py:314
  20.0 6.6 %collective-permute-start.4 = (bf16[576,128]{1,0:T(8,128)(2,1)S(1)}, bf16[576,128]{1,0:T(8,128)(2,1)S(1)}, u32[]{:S(2)}, u32[]{:S(2)}) collective-permute-start(bf16[576,128]{1,0:T(8,128)(2,1)S(1)} %collective-permute-done.refs_1_), channel_id=1, source_target_pairs={{4,0},{6,2},{0,4},{2,6},{12,8},{14,10},{8,12},{10,14},{20,16},{22,... | collective-permute-start | bytes 442376 | tf_op jit(solution)/shard_map/ppermute | solution.py:314
  20.5 0.9 %copy-start.5 = (bf16[128,576]{0,1:T(8,128)(2,1)S(1)}, bf16[128,576]{0,1:T(8,128)(2,1)}, u32[]{:S(2)}) copy-start(bf16[128,576]{0,1:T(8,128)(2,1)} %param.7) | copy-start | bytes 442372
  21.4 9.9 %collective-permute-start.7 = (bf16[2304,128]{1,0:T(8,128)(2,1)S(1)}, bf16[2304,128]{1,0:T(8,128)(2,1)S(1)}, u32[]{:S(2)}, u32[]{:S(2)}) collective-permute-start(bf16[2304,128]{1,0:T(8,128)(2,1)S(1)} %pack.2.refs_0_), channel_id=1, source_target_pairs={{2,0},{0,2},{6,4},{4,6},{10,8},{8,10},{14,12},{12,14},{18,16},{16,... | collective-permute-start | bytes 1769480 | tf_op jit(solution)/shard_map/ppermute | solution.py:314
  26.6 4.8 %collective-permute-start.8 = (bf16[2304,128]{1,0:T(8,128)(2,1)S(1)}, bf16[2304,128]{1,0:T(8,128)(2,1)S(1)}, u32[]{:S(2)}, u32[]{:S(2)}) collective-permute-start(bf16[2304,128]{1,0:T(8,128)(2,1)S(1)} %pack.3.refs_1_), channel_id=1, source_target_pairs={{2,0},{0,2},{6,4},{4,6},{10,8},{8,10},{14,12},{12,14},{18,16},{16,... | collective-permute-start | bytes 1769480 | tf_op jit(solution)/shard_map/ppermute | solution.py:314
  26.7 1.1 %copy-start.4 = (bf16[128,3072]{1,0:T(8,128)(2,1)S(1)}, bf16[128,3072]{1,0:T(8,128)(2,1)}, u32[]{:S(2)}) copy-start(bf16[128,3072]{1,0:T(8,128)(2,1)} %refs_0_.1) | copy-start | bytes 2359300
  27.8 0.7 copy-start.8
  29.3 21.4 %collective-permute-start.18 = (bf16[2304,128]{1,0:T(8,128)(2,1)S(1)}, bf16[2304,128]{1,0:T(8,128)(2,1)}, u32[]{:S(2)}, u32[]{:S(2)}) collective-permute-start(bf16[2304,128]{1,0:T(8,128)(2,1)S(1)} %pack.2.refs_0_), channel_id=1, source_target_pairs={{0,1},{1,0},{2,3},{3,2},{4,5},{5,4},{6,7},{7,6},{8,9},{9,8},{10,11... | collective-permute-start | bytes 1769480 | tf_op jit(solution)/shard_map/ppermute | solution.py:320
  30.8 27.4 %collective-permute-start.19 = (bf16[2304,128]{1,0:T(8,128)(2,1)S(1)}, bf16[2304,128]{1,0:T(8,128)(2,1)}, u32[]{:S(2)}, u32[]{:S(2)}) collective-permute-start(bf16[2304,128]{1,0:T(8,128)(2,1)S(1)} %pack.3.refs_1_), channel_id=1, source_target_pairs={{0,1},{1,0},{2,3},{3,2},{4,5},{5,4},{6,7},{7,6},{8,9},{9,8},{10,11... | collective-permute-start | bytes 1769480 | tf_op jit(solution)/shard_map/ppermute | solution.py:320
  48.9 11.8 %copy-start = (bf16[2304,128]{1,0:T(8,128)(2,1)}, bf16[2304,128]{1,0:T(8,128)(2,1)S(1)}, u32[]{:S(2)}) copy-start(bf16[2304,128]{1,0:T(8,128)(2,1)S(1)} %get-tuple-element.19.refs_0_) | copy-start | bytes 1769476
  48.9 9.4 %collective-permute-start.10 = (bf16[2304,128]{1,0:T(8,128)(2,1)S(1)}, bf16[2304,128]{1,0:T(8,128)(2,1)S(1)}, u32[]{:S(2)}, u32[]{:S(2)}) collective-permute-start(bf16[2304,128]{1,0:T(8,128)(2,1)S(1)} %get-tuple-element.20), channel_id=1, source_target_pairs={{2,0},{0,2},{6,4},{4,6},{10,8},{8,10},{14,12},{12,14},{18,16},{16,... | collective-permute-start | bytes 1769480 | tf_op jit(solution)/shard_map/ppermute | solution.py:314
  48.9 29.3 %collective-permute-start.22 = (bf16[128,3072]{1,0:T(8,128)(2,1)}, bf16[128,3072]{1,0:T(8,128)(2,1)}, u32[]{:S(2)}, u32[]{:S(2)}) collective-permute-start(bf16[128,3072]{1,0:T(8,128)(2,1)} %get-tuple-element.24.refs_8_), channel_id=1, source_target_pairs={{0,1},{1,0},{2,3},{3,2},{4,5},{5,4},{6,7},{7,6},{8,9},{9,8},{10,11... | collective-permute-start | bytes 2359304 | tf_op jit(solution)/shard_map/ppermute | solution.py:320
  50.5 10.1 %collective-permute-start.9 = (bf16[2304,128]{1,0:T(8,128)(2,1)S(1)}, bf16[2304,128]{1,0:T(8,128)(2,1)S(1)}, u32[]{:S(2)}, u32[]{:S(2)}) collective-permute-start(bf16[2304,128]{1,0:T(8,128)(2,1)S(1)} %get-tuple-element.18), channel_id=1, source_target_pairs={{2,0},{0,2},{6,4},{4,6},{10,8},{8,10},{14,12},{12,14},{18,16},{16,... | collective-permute-start | bytes 1769480 | tf_op jit(solution)/shard_map/ppermute | solution.py:314
  50.7 24.3 %collective-permute-start.20 = (bf16[2304,128]{1,0:T(8,128)(2,1)}, bf16[2304,128]{1,0:T(8,128)(2,1)}, u32[]{:S(2)}, u32[]{:S(2)}) collective-permute-start(bf16[2304,128]{1,0:T(8,128)(2,1)} %collective-permute-done.18.refs_4_), channel_id=1, source_target_pairs={{2,0},{0,2},{6,4},{4,6},{10,8},{8,10},{14,12},{12,14},{18,16},{16,... | collective-permute-start | bytes 1769480 | tf_op jit(solution)/shard_map/ppermute | solution.py:314
  58.3 18.5 %collective-permute-start.21 = (bf16[2304,128]{1,0:T(8,128)(2,1)}, bf16[2304,128]{1,0:T(8,128)(2,1)}, u32[]{:S(2)}, u32[]{:S(2)}) collective-permute-start(bf16[2304,128]{1,0:T(8,128)(2,1)} %collective-permute-done.19.refs_5_), channel_id=1, source_target_pairs={{2,0},{0,2},{6,4},{4,6},{10,8},{8,10},{14,12},{12,14},{18,16},{16,... | collective-permute-start | bytes 1769480 | tf_op jit(solution)/shard_map/ppermute | solution.py:314
  58.3 2.4 %copy-start.2 = (bf16[2304,128]{1,0:T(8,128)(2,1)}, bf16[2304,128]{1,0:T(8,128)(2,1)S(1)}, u32[]{:S(2)}) copy-start(bf16[2304,128]{1,0:T(8,128)(2,1)S(1)} %collective-permute-done.10.refs_1_) | copy-start | bytes 1769476
  59.1 6.7 %collective-permute-start.12 = (bf16[576,128]{1,0:T(8,128)(2,1)S(1)}, bf16[576,128]{1,0:T(8,128)(2,1)S(1)}, u32[]{:S(2)}, u32[]{:S(2)}) collective-permute-start(bf16[576,128]{1,0:T(8,128)(2,1)S(1)} %get-tuple-element.21), channel_id=1, source_target_pairs={{4,0},{6,2},{0,4},{2,6},{12,8},{14,10},{8,12},{10,14},{20,16},{22,... | collective-permute-start | bytes 442376 | tf_op jit(solution)/shard_map/ppermute | solution.py:314
  60.6 10.5 %collective-permute-start.14 = (bf16[576,128]{1,0:T(8,128)(2,1)}, bf16[576,128]{1,0:T(8,128)(2,1)}, u32[]{:S(2)}, u32[]{:S(2)}) collective-permute-start(bf16[576,128]{1,0:T(8,128)(2,1)} %get-tuple-element.22), channel_id=1, source_target_pairs={{4,0},{6,2},{0,4},{2,6},{12,8},{14,10},{8,12},{10,14},{20,16},{22,... | collective-permute-start | bytes 442376 | tf_op jit(solution)/shard_map/ppermute | solution.py:314
  65.9 0.7 copy-start.6
  66.5 6.2 %collective-permute-start.16 = (bf16[576,128]{1,0:T(8,128)(2,1)}, bf16[576,128]{1,0:T(8,128)(2,1)}, u32[]{:S(2)}, u32[]{:S(2)}) collective-permute-start(bf16[576,128]{1,0:T(8,128)(2,1)} %get-tuple-element.23), channel_id=1, source_target_pairs={{4,0},{6,2},{0,4},{2,6},{12,8},{14,10},{8,12},{10,14},{20,16},{22,... | collective-permute-start | bytes 442376 | tf_op jit(solution)/shard_map/ppermute | solution.py:314
  68.0 1.1 %copy-start.1 = (bf16[2304,128]{1,0:T(8,128)(2,1)S(1)}, bf16[2304,128]{1,0:T(8,128)(2,1)}, u32[]{:S(2)}) copy-start(bf16[2304,128]{1,0:T(8,128)(2,1)} %copy-done) | copy-start | bytes 1769476
  69.1 1.1 %copy-start.3 = (bf16[2304,128]{1,0:T(8,128)(2,1)S(1)}, bf16[2304,128]{1,0:T(8,128)(2,1)}, u32[]{:S(2)}) copy-start(bf16[2304,128]{1,0:T(8,128)(2,1)} %copy-done.2) | copy-start | bytes 1769476
  70.2 0.9 %copy-start.7 = (bf16[576,128]{1,0:T(8,128)(2,1)S(1)}, bf16[576,128]{1,0:T(8,128)(2,1)}, u32[]{:S(2)}) copy-start(bf16[576,128]{1,0:T(8,128)(2,1)} %copy-done.6) | copy-start | bytes 442372
  71.2 16.9 %collective-permute-start.11 = (bf16[576,128]{1,0:T(8,128)(2,1)S(1)}, bf16[576,128]{1,0:T(8,128)(2,1)S(1)}, u32[]{:S(2)}, u32[]{:S(2)}) collective-permute-start(bf16[576,128]{1,0:T(8,128)(2,1)S(1)} %add_parts.5), channel_id=1, source_target_pairs={{4,0},{6,2},{0,4},{2,6},{12,8},{14,10},{8,12},{10,14},{20,16},{22,... | collective-permute-start | bytes 442376 | tf_op jit(solution)/shard_map/ppermute | solution.py:314
  72.7 15.3 %collective-permute-start.13 = (bf16[576,128]{1,0:T(8,128)(2,1)S(1)}, bf16[576,128]{1,0:T(8,128)(2,1)S(1)}, u32[]{:S(2)}, u32[]{:S(2)}) collective-permute-start(bf16[576,128]{1,0:T(8,128)(2,1)S(1)} %add_parts.7), channel_id=1, source_target_pairs={{8,0},{10,2},{12,4},{14,6},{0,8},{2,10},{4,12},{6,14},{24,16},{26,... | collective-permute-start | bytes 442376 | tf_op jit(solution)/shard_map/ppermute | solution.py:314
  75.0 13.1 %collective-permute-start.15 = (bf16[576,128]{1,0:T(8,128)(2,1)S(1)}, bf16[576,128]{1,0:T(8,128)(2,1)S(1)}, u32[]{:S(2)}, u32[]{:S(2)}) collective-permute-start(bf16[576,128]{1,0:T(8,128)(2,1)S(1)} %add_parts.8), channel_id=1, source_target_pairs={{16,0},{18,2},{20,4},{22,6},{24,8},{26,10},{28,12},{30,14},{0,16},... | collective-permute-start | bytes 442376 | tf_op jit(solution)/shard_map/ppermute | solution.py:314
  76.7 11.3 %collective-permute-start.17 = (bf16[576,128]{1,0:T(8,128)(2,1)S(1)}, bf16[576,128]{1,0:T(8,128)(2,1)S(1)}, u32[]{:S(2)}, u32[]{:S(2)}) collective-permute-start(bf16[576,128]{1,0:T(8,128)(2,1)S(1)} %add_parts.9), channel_id=1, source_target_pairs={{24,0},{26,2},{28,4},{30,6},{16,8},{18,10},{20,12},{22,14},{8,16},... | collective-permute-start | bytes 442376 | tf_op jit(solution)/shard_map/ppermute | solution.py:314

commit v5 on v4

--- a/solution.py
+++ b/solution.py
@@ -151,19 +151,35 @@
     )(rows, offs, *arrays, weights, cot)
 
 
-def weight_kernel(n_planes, n_in, part, rows_s, offs_s, half_s, *refs):
-    x_refs, refs = refs[: n_planes * n_in], refs[n_planes * n_in :]
-    slope_refs, (out_ref, xt, out, out_sem) = refs[:n_planes], refs[n_planes:]
-    cols, slots, side, _ = out.shape
-    tokens = slope_refs[0].shape[0]
-
-    def result(c):
-        return pltpu.make_async_copy(out.at[c], out_ref.at[c], out_sem.at[c])
-
+def assemble_kernel(n_planes, n_in, part, offs_s, *refs):
+    x_refs, xt = refs[:-1], refs[-1]
+    tokens = x_refs[0].shape[1]
     for p in range(n_planes):
         for j, shard in enumerate(shards_of(x_refs[p * n_in : (p + 1) * n_in], part)):
             rows = pl.ds(pl.multiple_of(offs_s[j], 16), part)
             xt[rows, p * tokens : (p + 1) * tokens] = shard[...]
+
+
+def assemble(planes, part, offs):
+    arrays = [a for plane in planes for a in plane]
+    rows = sum(a.shape[0] for a in planes[0])
+    return pl.pallas_call(
+        functools.partial(assemble_kernel, len(planes), len(planes[0]), part),
+        grid_spec=pltpu.PrefetchScalarGridSpec(
+            num_scalar_prefetch=1, in_specs=[VMEM] * len(arrays), out_specs=VMEM
+        ),
+        out_shape=jax.ShapeDtypeStruct((rows, len(planes) * arrays[0].shape[1]), jnp.bfloat16),
+        compiler_params=pltpu.CompilerParams(vmem_limit_bytes=MARGIN),
+        name="assemble",
+    )(offs, *arrays)
+
+
+def weight_kernel(n_planes, rows_s, half_s, xt, *refs):
+    slope_refs, (out_ref, out, out_sem) = refs[:n_planes], refs[n_planes:]
+    cols, slots, side, _ = out.shape
+
+    def result(c):
+        return pltpu.make_async_copy(out.at[c], out_ref.at[c], out_sem.at[c])
 
     def one(c, carry):
         right = jnp.concatenate([ref[:, block(c, side)] for ref in slope_refs], axis=0)
@@ -182,32 +198,27 @@
     lax.fori_loop(0, cols, drain, 0)
 
 
-def weight_grad(planes, part, offs, slopes, rows, half, slots, side):
+def weight_grad(features, slopes, rows, half, slots, side):
     cols = rows.shape[0]
     tokens = slopes[0].shape[0]
-    features = sum(a.shape[0] for a in planes[0])
-    arrays = [a for plane in planes for a in plane]
-    scratch = [
-        ((features, len(planes) * tokens), jnp.bfloat16),
-        ((cols, slots, side, side), jnp.float32),
-    ]
-    return pl.pallas_call(
-        functools.partial(weight_kernel, len(planes), len(planes[0]), part),
+    scratch = [((cols, slots, side, side), jnp.float32)]
+    return pl.pallas_call(
+        functools.partial(weight_kernel, len(slopes)),
         grid_spec=pltpu.PrefetchScalarGridSpec(
-            num_scalar_prefetch=3,
-            in_specs=[VMEM] * (len(arrays) + len(slopes)),
+            num_scalar_prefetch=2,
+            in_specs=[VMEM] * (1 + len(slopes)),
             out_specs=HBM,
             scratch_shapes=[pltpu.VMEM(*s) for s in scratch] + [DMA((cols,))],
         ),
         out_shape=jax.ShapeDtypeStruct((cols, slots, side, side), jnp.float32),
         compiler_params=pltpu.CompilerParams(vmem_limit_bytes=grant(*scratch)),
         cost_estimate=pl.CostEstimate(
-            flops=2 * len(planes) * tokens * cols * slots * side * side,
+            flops=2 * len(slopes) * tokens * cols * slots * side * side,
             bytes_accessed=4 * cols * slots * side * side,
             transcendentals=0,
         ),
         name="weight_grad",
-    )(rows, offs, half, *arrays, *slopes)
+    )(rows, half, features, *slopes)
 
 
 def pack_kernel(*refs):
@@ -290,9 +301,7 @@
         )
         slopes_all = lax.all_gather(slopes, "mp", axis=0)
         block_grad = weight_grad(
-            [[x_all[p]] for p in range(mp)],
-            whole,
-            offs,
+            assemble([[x_all[p]] for p in range(mp)], whole, offs),
             [slopes_all[p] for p in range(mp)],
             block_rows,
             half,
@@ -353,10 +362,9 @@
     for k in range(1, line):
         (mine,) = add_parts([keep0, got0, pairs[k]], [[(0, k), (1, k), (2, 0)]], part)
         total = total + permute(mine, back_to(k), 0, 0).astype(jnp.float32)
+    features = assemble([x_own, x_far], part, offs)
     block_grad = weight_grad(
-        [x_own, x_far],
-        part,
-        offs,
+        features,
         [slopes, slopes_far],
         block_rows,
         half,
@@ -369,9 +377,7 @@
 def solution(mesh):
     in_specs = (P("mp", "dp"), P("dp", None, None, None), P("dp", None), P("mp", "dp"))
     out_specs = (P("mp", "dp"), P("mp", "dp"), P("dp", "mp", None, None))
-    step = jax.shard_map(
-        body, mesh=mesh, in_specs=in_specs, out_specs=out_specs, check_vma=False
-    )
+    step = jax.shard_map(body, mesh=mesh, in_specs=in_specs, out_specs=out_specs, check_vma=False)
     n, mp = mesh.shape["dp"], mesh.shape["mp"]
     if not direct(n, mp):
         return step

time: 89.3 us -> 91.8 us (1.028)
  local copies, waits for them, and re-layouts: 6.46 us -> 12.5 us
  waiting for transfers between devices: 25.6 us -> 20.5 us
  Pallas kernels: 30.3 us -> 31.3 us
    unnamed x18 -> x30, local copies, waits for them, and re-layouts: 6.46 us -> 12.5 us
    ppermute x20, waiting for transfers between devices: 18.4 us -> 14.1 us  [permute(): return lax.ppermute(a, 'dp', [(source(i), i) for i in range(n)])]
    pallas_call x5, Pallas kernels: 2.89 us -> 3.84 us  [add_parts(): pl.pallas_call(functools.partial(sum_kernel, plan, part, len(arrays)), in...]
    pallas_call x1 -> x2, Pallas kernels: 9.78 us -> 9.62 us  [the longest x1 8.26 us: weight_grad(): pl.pallas_call(functools.partial(weight_kernel, len(slopes)), grid_spec=p...]
where the time goes in v5:
time: 91.8 us; the launch traced here: 91.2 us
  Pallas kernels  31.3 us (34%)
  starting transfers between devices  24.6 us (27%)
  waiting for transfers between devices  20.5 us (22%)
  local copies, waits for them, and re-layouts  12.5 us (14%)
  other arithmetic  1.48 us (2%)
    ppermute x20, starting transfers between devices, permute(): return lax.ppermute(a, 'dp', [(source(i), i) for i in range(n)])  21 us
    pallas_call x1, Pallas kernels, forward(): pl.pallas_call(functools.partial(forward_kernel, len(arrays), len(outs),...  17.7 us
    ppermute x20, waiting for transfers between devices, permute(): return lax.ppermute(a, 'dp', [(source(i), i) for i in range(n)])  14.1 us
    unnamed x30, local copies, waits for them, and re-layouts  12.5 us
    pallas_call x1, Pallas kernels, weight_grad(): pl.pallas_call(functools.partial(weight_kernel, len(slopes)), grid_spec=p...  8.26 us
    ppermute x3, waiting for transfers between devices, across(): return lax.ppermute(a, 'mp', [(i, i ^ 1) for i in range(mp)])  6.32 us
    pallas_call x5, Pallas kernels, add_parts(): pl.pallas_call(functools.partial(sum_kernel, plan, part, len(arrays)), in...  3.84 us
    ppermute x3, starting transfers between devices, across(): return lax.ppermute(a, 'mp', [(i, i ^ 1) for i in range(mp)])  3.67 us
  transfers between devices with their start and end apart: 23, of which 6 were waited for; matrix products, arithmetic and copies ran while one was open for 1% of the time, Pallas kernels for 34%

profile of v5, /device:TPU:0, one launch (start us, length us, event | category | flops | bytes accessed | tf_op | source)
XLA Modules:
  0.0 91.2 jit_solution(1944146502545874013)
XLA Ops:
  0.6 5.1 %collective-permute-start.2 = (bf16[576,128]{1,0:T(8,128)(2,1)}, bf16[576,128]{1,0:T(8,128)(2,1)S(1)}, u32[]{:S(2)}, u32[]{:S(2)}) collective-permute-start(bf16[576,128]{1,0:T(8,128)(2,1)} %bitcast.4), channel_id=1, source_target_pairs={{24,0},{26,2},{28,4},{30,6},{16,8},{18,10},{20,12},{22,14},{8,16},... | collective-permute-start | bytes 442376 | tf_op jit(solution)/shard_map/ppermute | solution.py:323
  5.8 0.6 collective-permute-start
  6.4 1.6 %collective-permute-start.3 = (bf16[576,128]{1,0:T(8,128)(2,1)}, bf16[576,128]{1,0:T(8,128)(2,1)S(1)}, u32[]{:S(2)}, u32[]{:S(2)}) collective-permute-start(bf16[576,128]{1,0:T(8,128)(2,1)} %bitcast.7), channel_id=1, source_target_pairs={{4,0},{6,2},{0,4},{2,6},{12,8},{14,10},{8,12},{10,14},{20,16},{22,... | collective-permute-start | bytes 442376 | tf_op jit(solution)/shard_map/ppermute | solution.py:323
  8.1 2.7 %collective-permute-done.2.refs_3_ = bf16[576,128]{1,0:T(8,128)(2,1)S(1)} collective-permute-done((bf16[576,128]{1,0:T(8,128)(2,1)}, bf16[576,128]{1,0:T(8,128)(2,1)S(1)}, u32[]{:S(2)}, u32[]{:S(2)}) %collective-permute-start.2) | collective-permute-done | bytes 147488 | tf_op jit(solution)/shard_map/ppermute | solution.py:323
  10.8 1.7 %collective-permute-start.6 = (bf16[576,128]{1,0:T(8,128)(2,1)S(1)}, bf16[576,128]{1,0:T(8,128)(2,1)S(1)}, u32[]{:S(2)}, u32[]{:S(2)}) collective-permute-start(bf16[576,128]{1,0:T(8,128)(2,1)S(1)} %collective-permute-done.2.refs_3_), channel_id=1, source_target_pairs={{4,0},{6,2},{0,4},{2,6},{12,8},{14,10},{8,12},{10,14},{20,16},{22,... | collective-permute-start | bytes 442376 | tf_op jit(solution)/shard_map/ppermute | solution.py:323
  12.4 6.0 %collective-permute-done.1.refs_2_ = bf16[576,128]{1,0:T(8,128)(2,1)S(1)} collective-permute-done((bf16[576,128]{1,0:T(8,128)(2,1)}, bf16[576,128]{1,0:T(8,128)(2,1)S(1)}, u32[]{:S(2)}, u32[]{:S(2)}) %collective-permute-start.1) | collective-permute-done | bytes 147488 | tf_op jit(solution)/shard_map/ppermute | solution.py:323
  18.5 1.5 %collective-permute-start.5 = (bf16[576,128]{1,0:T(8,128)(2,1)S(1)}, bf16[576,128]{1,0:T(8,128)(2,1)S(1)}, u32[]{:S(2)}, u32[]{:S(2)}) collective-permute-start(bf16[576,128]{1,0:T(8,128)(2,1)S(1)} %collective-permute-done.1.refs_2_), channel_id=1, source_target_pairs={{4,0},{6,2},{0,4},{2,6},{12,8},{14,10},{8,12},{10,14},{20,16},{22,... | collective-permute-start | bytes 442376 | tf_op jit(solution)/shard_map/ppermute | solution.py:323
  20.0 0.5 collective-permute-start.4
  20.5 0.9 copy-done.13
  21.4 0.1 collective-permute-start.7
  21.5 3.4 %collective-permute-done.5.refs_2_ = bf16[576,128]{1,0:T(8,128)(2,1)S(1)} collective-permute-done((bf16[576,128]{1,0:T(8,128)(2,1)S(1)}, bf16[576,128]{1,0:T(8,128)(2,1)S(1)}, u32[]{:S(2)}, u32[]{:S(2)}) %collective-permute-start.5) | collective-permute-done | bytes 147488 | tf_op jit(solution)/shard_map/ppermute | solution.py:323
  25.0 1.6 %collective-permute-done.4.refs_1_ = bf16[576,128]{1,0:T(8,128)(2,1)S(1)} collective-permute-done((bf16[576,128]{1,0:T(8,128)(2,1)S(1)}, bf16[576,128]{1,0:T(8,128)(2,1)S(1)}, u32[]{:S(2)}, u32[]{:S(2)}) %collective-permute-start.4) | collective-permute-done | bytes 147488 | tf_op jit(solution)/shard_map/ppermute | solution.py:323
  26.7 1.1 %copy-done.4 = bf16[128,3072]{1,0:T(8,128)(2,1)S(1)} copy-done((bf16[128,3072]{1,0:T(8,128)(2,1)S(1)}, bf16[128,3072]{1,0:T(8,128)(2,1)}, u32[]{:S(2)}) %copy-start.4) | copy-done | bytes 786456
  27.8 0.7 copy-done.14
  28.6 1.6 %collective-permute-start.18 = (bf16[2304,128]{1,0:T(8,128)(2,1)S(1)}, bf16[2304,128]{1,0:T(8,128)(2,1)S(1)}, u32[]{:S(2)}, u32[]{:S(2)}) collective-permute-start(bf16[2304,128]{1,0:T(8,128)(2,1)S(1)} %pack.2.refs_0_), channel_id=1, source_target_pairs={{0,1},{1,0},{2,3},{3,2},{4,5},{5,4},{6,7},{7,6},{8,9},{9,8},{10,11... | collective-permute-start | bytes 1769480 | tf_op jit(solution)/shard_map/ppermute | solution.py:329
  30.2 0.5 collective-permute-start.19
  30.7 0.7 add_multiply_fusion.offs_s
  31.4 17.7 %forward.1 = (bf16[128,3072]{1,0:T(8,128)(2,1)}, bf16[128,3072]{1,0:T(8,128)(2,1)}, bf16[2304,128]{1,0:T(8,128)(2,1)S(1)}, bf16[2304,128]{1,0:T(8,128)(2,1)S(1)}...) custom-call(s32[24,20]{1,0:T(8,128)S(1)} %get-tuple-element.14.rows_s, s32[16]{0:T(128)S(1)} %add_multiply_fusion.offs_s, ...), custom_call_target="tpu_custom_call" | custom-call | flops 4026531840 | bytes 15728640 | tf_op jit(solution)/shard_map/forward/pallas_call | solution.py:132
  49.1 1.6 %collective-permute-start.22 = (bf16[128,3072]{1,0:T(8,128)(2,1)}, bf16[128,3072]{1,0:T(8,128)(2,1)}, u32[]{:S(2)}, u32[]{:S(2)}) collective-permute-start(bf16[128,3072]{1,0:T(8,128)(2,1)} %get-tuple-element.24.refs_0_), channel_id=1, source_target_pairs={{0,1},{1,0},{2,3},{3,2},{4,5},{5,4},{6,7},{7,6},{8,9},{9,8},{10,11... | collective-permute-start | bytes 2359304 | tf_op jit(solution)/shard_map/ppermute | solution.py:329
  50.7 0.5 collective-permute-start.20
  51.2 6.3 %collective-permute-done.19.refs_5_ = bf16[2304,128]{1,0:T(8,128)(2,1)S(1)} collective-permute-done((bf16[2304,128]{1,0:T(8,128)(2,1)S(1)}, bf16[2304,128]{1,0:T(8,128)(2,1)S(1)}, u32[]{:S(2)}, u32[]{:S(2)}) %collective-permute-start.19) | collective-permute-done | bytes 589856 | tf_op jit(solution)/shard_map/ppermute | solution.py:329
  57.5 0.8 copy-done.7
  58.3 0.5 collective-permute-start.9
  58.9 0.9 add_parts.6
  59.8 0.1 copy-done.2
  59.8 0.8 copy-done
  60.7 1.5 %collective-permute-start.12 = (bf16[576,128]{1,0:T(8,128)(2,1)}, bf16[576,128]{1,0:T(8,128)(2,1)}, u32[]{:S(2)}, u32[]{:S(2)}) collective-permute-start(bf16[576,128]{1,0:T(8,128)(2,1)} %get-tuple-element.21), channel_id=1, source_target_pairs={{4,0},{6,2},{0,4},{2,6},{12,8},{14,10},{8,12},{10,14},{20,16},{22,... | collective-permute-start | bytes 442376 | tf_op jit(solution)/shard_map/ppermute | solution.py:323
  62.2 0.8 copy-done.9
  63.0 0.5 collective-permute-start.14
  63.5 0.8 copy-done.11
  64.4 1.5 %collective-permute-start.16 = (bf16[576,128]{1,0:T(8,128)(2,1)}, bf16[576,128]{1,0:T(8,128)(2,1)}, u32[]{:S(2)}, u32[]{:S(2)}) collective-permute-start(bf16[576,128]{1,0:T(8,128)(2,1)} %get-tuple-element.23), channel_id=1, source_target_pairs={{4,0},{6,2},{0,4},{2,6},{12,8},{14,10},{8,12},{10,14},{20,16},{22,... | collective-permute-start | bytes 442376 | tf_op jit(solution)/shard_map/ppermute | solution.py:323
  65.9 1.1 %copy-done.1 = bf16[2304,128]{1,0:T(8,128)(2,1)S(1)} copy-done((bf16[2304,128]{1,0:T(8,128)(2,1)S(1)}, bf16[2304,128]{1,0:T(8,128)(2,1)}, u32[]{:S(2)}) %copy-start.1) | copy-done | bytes 589848
  66.9 1.1 %copy-done.3 = bf16[2304,128]{1,0:T(8,128)(2,1)S(1)} copy-done((bf16[2304,128]{1,0:T(8,128)(2,1)S(1)}, bf16[2304,128]{1,0:T(8,128)(2,1)}, u32[]{:S(2)}) %copy-start.3) | copy-done | bytes 589848
  68.0 1.1 %copy-done.6 = bf16[2304,128]{1,0:T(8,128)(2,1)S(1)} copy-done((bf16[2304,128]{1,0:T(8,128)(2,1)S(1)}, bf16[2304,128]{1,0:T(8,128)(2,1)}, u32[]{:S(2)}) %copy-start.6) | copy-done | bytes 589848
  69.1 1.1 %copy-done.8 = bf16[2304,128]{1,0:T(8,128)(2,1)S(1)} copy-done((bf16[2304,128]{1,0:T(8,128)(2,1)S(1)}, bf16[2304,128]{1,0:T(8,128)(2,1)}, u32[]{:S(2)}) %copy-start.8) | copy-done | bytes 589848
  70.2 1.1 %copy-done.10 = bf16[2304,128]{1,0:T(8,128)(2,1)S(1)} copy-done((bf16[2304,128]{1,0:T(8,128)(2,1)S(1)}, bf16[2304,128]{1,0:T(8,128)(2,1)}, u32[]{:S(2)}) %copy-start.10) | copy-done | bytes 589848
  71.2 1.1 %copy-done.12 = bf16[2304,128]{1,0:T(8,128)(2,1)S(1)} copy-done((bf16[2304,128]{1,0:T(8,128)(2,1)S(1)}, bf16[2304,128]{1,0:T(8,128)(2,1)}, u32[]{:S(2)}) %copy-start.12) | copy-done | bytes 589848
  72.3 1.4 %assemble.1.xt = bf16[9216,256]{1,0:T(8,128)(2,1)S(1)} custom-call(s32[16]{0:T(128)S(1)} %add_multiply_fusion.offs_s, bf16[2304,128]{1,0:T(8,128)(2,1)S(1)} %pack.2.refs_0_, bf16[2304,128]{1,0:T(8,128)(2,1)S(1)} %pack.3.refs_1_, bf16[2304,128]{1,0:T(8,128)(2,1)S(1)} %collective-permute-done.7.refs_2_, bf16[2304,128]{1,0:T(8,128)(2,1)S(1)} %collective-permute-done.8.refs_3_, ...), custom_call_target="tpu_custom_call" | custom-call | tf_op jit(solution)/shard_map/assemble/pallas_call | solution.py:166
  73.7 0.6 collective-permute-start.11
  74.3 1.0 %add_parts.7 = bf16[576,128]{1,0:T(8,128)(2,1)S(1)} custom-call(bf16[2304,128]{1,0:T(8,128)(2,1)S(1)} %get-tuple-element.17.refs_0_, bf16[2304,128]{1,0:T(8,128)(2,1)S(1)} %collective-permute-done.9.refs_1_, bf16[576,128]{1,0:T(8,128)(2,1)} %collective-permute-done.12.refs_2_), custom_call_target="tpu_custom_call" | custom-call | tf_op jit(solution)/shard_map/add_parts/pallas_call | solution.py:271
  75.2 1.3 %collective-permute-start.13 = (bf16[576,128]{1,0:T(8,128)(2,1)S(1)}, bf16[576,128]{1,0:T(8,128)(2,1)S(1)}, u32[]{:S(2)}, u32[]{:S(2)}) collective-permute-start(bf16[576,128]{1,0:T(8,128)(2,1)S(1)} %add_parts.7), channel_id=1, source_target_pairs={{8,0},{10,2},{12,4},{14,6},{0,8},{2,10},{4,12},{6,14},{24,16},{26,... | collective-permute-start | bytes 442376 | tf_op jit(solution)/shard_map/ppermute | solution.py:323
  76.5 1.0 %add_parts.8 = bf16[576,128]{1,0:T(8,128)(2,1)S(1)} custom-call(bf16[2304,128]{1,0:T(8,128)(2,1)S(1)} %get-tuple-element.17.refs_0_, bf16[2304,128]{1,0:T(8,128)(2,1)S(1)} %collective-permute-done.9.refs_1_, bf16[576,128]{1,0:T(8,128)(2,1)} %collective-permute-done.14.refs_2_), custom_call_target="tpu_custom_call" | custom-call | tf_op jit(solution)/shard_map/add_parts/pallas_call | solution.py:271
  77.5 1.8 %collective-permute-start.15 = (bf16[576,128]{1,0:T(8,128)(2,1)S(1)}, bf16[576,128]{1,0:T(8,128)(2,1)S(1)}, u32[]{:S(2)}, u32[]{:S(2)}) collective-permute-start(bf16[576,128]{1,0:T(8,128)(2,1)S(1)} %add_parts.8), channel_id=1, source_target_pairs={{16,0},{18,2},{20,4},{22,6},{24,8},{26,10},{28,12},{30,14},{0,16},... | collective-permute-start | bytes 442376 | tf_op jit(solution)/shard_map/ppermute | solution.py:323
  79.2 1.0 %add_parts.9 = bf16[576,128]{1,0:T(8,128)(2,1)S(1)} custom-call(bf16[2304,128]{1,0:T(8,128)(2,1)S(1)} %get-tuple-element.17.refs_0_, bf16[2304,128]{1,0:T(8,128)(2,1)S(1)} %collective-permute-done.9.refs_1_, bf16[576,128]{1,0:T(8,128)(2,1)} %collective-permute-done.16.refs_2_), custom_call_target="tpu_custom_call" | custom-call | tf_op jit(solution)/shard_map/add_parts/pallas_call | solution.py:271
  80.2 1.6 %collective-permute-start.17 = (bf16[576,128]{1,0:T(8,128)(2,1)S(1)}, bf16[576,128]{1,0:T(8,128)(2,1)S(1)}, u32[]{:S(2)}, u32[]{:S(2)}) collective-permute-start(bf16[576,128]{1,0:T(8,128)(2,1)S(1)} %add_parts.9), channel_id=1, source_target_pairs={{24,0},{26,2},{28,4},{30,6},{16,8},{18,10},{20,12},{22,14},{8,16},... | collective-permute-start | bytes 442376 | tf_op jit(solution)/shard_map/ppermute | solution.py:323
  81.8 8.3 %weight_grad.1 = f32[24,10,128,128]{3,2,1,0:T(8,128)} custom-call(s32[24,20]{1,0:T(8,128)S(1)} %get-tuple-element.14.rows_s, s32[1]{0:T(128)} %bitcast.2.half_s, bf16[9216,256]{1,0:T(8,128)(2,1)S(1)} %assemble.1.xt, bf16[128,3072]{1,0:T(8,128)(2,1)} %get-tuple-element.24.refs_0_, bf16[128,3072]{1,0:T(8,128)(2,1)} %collective-permute-done.22.refs_1_), custom_call_target="tpu_custom_call" | custom-call | flops 2013265920 | bytes 15728640 | tf_op jit(solution)/shard_map/weight_grad/pallas_call | solution.py:205
  90.1 0.4 collective-permute-done.15
  90.4 0.8 fusion
  (41 shorter events, 0.3 us)
Async XLA Ops:
  0.6 10.2 %collective-permute-start.2 = (bf16[576,128]{1,0:T(8,128)(2,1)}, bf16[576,128]{1,0:T(8,128)(2,1)S(1)}, u32[]{:S(2)}, u32[]{:S(2)}) collective-permute-start(bf16[576,128]{1,0:T(8,128)(2,1)} %bitcast.4), channel_id=1, source_target_pairs={{24,0},{26,2},{28,4},{30,6},{16,8},{18,10},{20,12},{22,14},{8,16},... | collective-permute-start | bytes 442376 | tf_op jit(solution)/shard_map/ppermute | solution.py:323
  5.8 12.7 %collective-permute-start.1 = (bf16[576,128]{1,0:T(8,128)(2,1)}, bf16[576,128]{1,0:T(8,128)(2,1)S(1)}, u32[]{:S(2)}, u32[]{:S(2)}) collective-permute-start(bf16[576,128]{1,0:T(8,128)(2,1)} %bitcast.5), channel_id=1, source_target_pairs={{16,0},{18,2},{20,4},{22,6},{24,8},{26,10},{28,12},{30,14},{0,16},... | collective-permute-start | bytes 442376 | tf_op jit(solution)/shard_map/ppermute | solution.py:323
  5.8 14.2 %collective-permute-start = (bf16[576,128]{1,0:T(8,128)(2,1)}, bf16[576,128]{1,0:T(8,128)(2,1)S(1)}, u32[]{:S(2)}, u32[]{:S(2)}) collective-permute-start(bf16[576,128]{1,0:T(8,128)(2,1)} %bitcast.6), channel_id=1, source_target_pairs={{8,0},{10,2},{12,4},{14,6},{0,8},{2,10},{4,12},{6,14},{24,16},{26,... | collective-permute-start | bytes 442376 | tf_op jit(solution)/shard_map/ppermute | solution.py:323
  6.4 15.1 %collective-permute-start.3 = (bf16[576,128]{1,0:T(8,128)(2,1)}, bf16[576,128]{1,0:T(8,128)(2,1)S(1)}, u32[]{:S(2)}, u32[]{:S(2)}) collective-permute-start(bf16[576,128]{1,0:T(8,128)(2,1)} %bitcast.7), channel_id=1, source_target_pairs={{4,0},{6,2},{0,4},{2,6},{12,8},{14,10},{8,12},{10,14},{20,16},{22,... | collective-permute-start | bytes 442376 | tf_op jit(solution)/shard_map/ppermute | solution.py:323
  10.8 10.8 %collective-permute-start.6 = (bf16[576,128]{1,0:T(8,128)(2,1)S(1)}, bf16[576,128]{1,0:T(8,128)(2,1)S(1)}, u32[]{:S(2)}, u32[]{:S(2)}) collective-permute-start(bf16[576,128]{1,0:T(8,128)(2,1)S(1)} %collective-permute-done.2.refs_3_), channel_id=1, source_target_pairs={{4,0},{6,2},{0,4},{2,6},{12,8},{14,10},{8,12},{10,14},{20,16},{22,... | collective-permute-start | bytes 442376 | tf_op jit(solution)/shard_map/ppermute | solution.py:323
  18.5 6.5 %collective-permute-start.5 = (bf16[576,128]{1,0:T(8,128)(2,1)S(1)}, bf16[576,128]{1,0:T(8,128)(2,1)S(1)}, u32[]{:S(2)}, u32[]{:S(2)}) collective-permute-start(bf16[576,128]{1,0:T(8,128)(2,1)S(1)} %collective-permute-done.1.refs_2_), channel_id=1, source_target_pairs={{4,0},{6,2},{0,4},{2,6},{12,8},{14,10},{8,12},{10,14},{20,16},{22,... | collective-permute-start | bytes 442376 | tf_op jit(solution)/shard_map/ppermute | solution.py:323
  20.0 6.6 %collective-permute-start.4 = (bf16[576,128]{1,0:T(8,128)(2,1)S(1)}, bf16[576,128]{1,0:T(8,128)(2,1)S(1)}, u32[]{:S(2)}, u32[]{:S(2)}) collective-permute-start(bf16[576,128]{1,0:T(8,128)(2,1)S(1)} %collective-permute-done.refs_1_), channel_id=1, source_target_pairs={{4,0},{6,2},{0,4},{2,6},{12,8},{14,10},{8,12},{10,14},{20,16},{22,... | collective-permute-start | bytes 442376 | tf_op jit(solution)/shard_map/ppermute | solution.py:323
  20.5 0.9 copy-start.13
  21.4 10.0 %collective-permute-start.7 = (bf16[2304,128]{1,0:T(8,128)(2,1)S(1)}, bf16[2304,128]{1,0:T(8,128)(2,1)S(1)}, u32[]{:S(2)}, u32[]{:S(2)}) collective-permute-start(bf16[2304,128]{1,0:T(8,128)(2,1)S(1)} %pack.2.refs_0_), channel_id=1, source_target_pairs={{2,0},{0,2},{6,4},{4,6},{10,8},{8,10},{14,12},{12,14},{18,16},{16,... | collective-permute-start | bytes 1769480 | tf_op jit(solution)/shard_map/ppermute | solution.py:323
  26.6 4.8 %collective-permute-start.8 = (bf16[2304,128]{1,0:T(8,128)(2,1)S(1)}, bf16[2304,128]{1,0:T(8,128)(2,1)S(1)}, u32[]{:S(2)}, u32[]{:S(2)}) collective-permute-start(bf16[2304,128]{1,0:T(8,128)(2,1)S(1)} %pack.3.refs_1_), channel_id=1, source_target_pairs={{2,0},{0,2},{6,4},{4,6},{10,8},{8,10},{14,12},{12,14},{18,16},{16,... | collective-permute-start | bytes 1769480 | tf_op jit(solution)/shard_map/ppermute | solution.py:323
  26.7 1.1 %copy-start.4 = (bf16[128,3072]{1,0:T(8,128)(2,1)S(1)}, bf16[128,3072]{1,0:T(8,128)(2,1)}, u32[]{:S(2)}) copy-start(bf16[128,3072]{1,0:T(8,128)(2,1)} %refs_0_.1) | copy-start | bytes 2359300
  27.8 0.7 copy-start.14
  28.6 22.1 %collective-permute-start.18 = (bf16[2304,128]{1,0:T(8,128)(2,1)S(1)}, bf16[2304,128]{1,0:T(8,128)(2,1)S(1)}, u32[]{:S(2)}, u32[]{:S(2)}) collective-permute-start(bf16[2304,128]{1,0:T(8,128)(2,1)S(1)} %pack.2.refs_0_), channel_id=1, source_target_pairs={{0,1},{1,0},{2,3},{3,2},{4,5},{5,4},{6,7},{7,6},{8,9},{9,8},{10,11... | collective-permute-start | bytes 1769480 | tf_op jit(solution)/shard_map/ppermute | solution.py:329
  30.2 27.3 %collective-permute-start.19 = (bf16[2304,128]{1,0:T(8,128)(2,1)S(1)}, bf16[2304,128]{1,0:T(8,128)(2,1)S(1)}, u32[]{:S(2)}, u32[]{:S(2)}) collective-permute-start(bf16[2304,128]{1,0:T(8,128)(2,1)S(1)} %pack.3.refs_1_), channel_id=1, source_target_pairs={{0,1},{1,0},{2,3},{3,2},{4,5},{5,4},{6,7},{7,6},{8,9},{9,8},{10,11... | collective-permute-start | bytes 1769480 | tf_op jit(solution)/shard_map/ppermute | solution.py:329
  49.1 32.7 %collective-permute-start.22 = (bf16[128,3072]{1,0:T(8,128)(2,1)}, bf16[128,3072]{1,0:T(8,128)(2,1)}, u32[]{:S(2)}, u32[]{:S(2)}) collective-permute-start(bf16[128,3072]{1,0:T(8,128)(2,1)} %get-tuple-element.24.refs_0_), channel_id=1, source_target_pairs={{0,1},{1,0},{2,3},{3,2},{4,5},{5,4},{6,7},{7,6},{8,9},{9,8},{10,11... | collective-permute-start | bytes 2359304 | tf_op jit(solution)/shard_map/ppermute | solution.py:329
  50.7 8.2 %collective-permute-start.10 = (bf16[2304,128]{1,0:T(8,128)(2,1)S(1)}, bf16[2304,128]{1,0:T(8,128)(2,1)S(1)}, u32[]{:S(2)}, u32[]{:S(2)}) collective-permute-start(bf16[2304,128]{1,0:T(8,128)(2,1)S(1)} %get-tuple-element.20), channel_id=1, source_target_pairs={{2,0},{0,2},{6,4},{4,6},{10,8},{8,10},{14,12},{12,14},{18,16},{16,... | collective-permute-start | bytes 1769480 | tf_op jit(solution)/shard_map/ppermute | solution.py:323
  50.7 10.0 %copy-start.5 = (bf16[2304,128]{1,0:T(8,128)(2,1)}, bf16[2304,128]{1,0:T(8,128)(2,1)S(1)}, u32[]{:S(2)}) copy-start(bf16[2304,128]{1,0:T(8,128)(2,1)S(1)} %collective-permute-done.18.refs_4_) | copy-start | bytes 1769476
  50.7 11.5 %collective-permute-start.20 = (bf16[2304,128]{1,0:T(8,128)(2,1)S(1)}, bf16[2304,128]{1,0:T(8,128)(2,1)S(1)}, u32[]{:S(2)}, u32[]{:S(2)}) collective-permute-start(bf16[2304,128]{1,0:T(8,128)(2,1)S(1)} %collective-permute-done.18.refs_4_), channel_id=1, source_target_pairs={{2,0},{0,2},{6,4},{4,6},{10,8},{8,10},{14,12},{12,14},{18,16},{16,... | collective-permute-start | bytes 1769480 | tf_op jit(solution)/shard_map/ppermute | solution.py:323
  57.5 6.0 %collective-permute-start.21 = (bf16[2304,128]{1,0:T(8,128)(2,1)S(1)}, bf16[2304,128]{1,0:T(8,128)(2,1)S(1)}, u32[]{:S(2)}, u32[]{:S(2)}) collective-permute-start(bf16[2304,128]{1,0:T(8,128)(2,1)S(1)} %collective-permute-done.19.refs_5_), channel_id=1, source_target_pairs={{2,0},{0,2},{6,4},{4,6},{10,8},{8,10},{14,12},{12,14},{18,16},{16,... | collective-permute-start | bytes 1769480 | tf_op jit(solution)/shard_map/ppermute | solution.py:323
  57.5 0.8 copy-start.7
  58.3 15.3 %collective-permute-start.9 = (bf16[2304,128]{1,0:T(8,128)(2,1)}, bf16[2304,128]{1,0:T(8,128)(2,1)S(1)}, u32[]{:S(2)}, u32[]{:S(2)}) collective-permute-start(bf16[2304,128]{1,0:T(8,128)(2,1)} %get-tuple-element.18), channel_id=1, source_target_pairs={{2,0},{0,2},{6,4},{4,6},{10,8},{8,10},{14,12},{12,14},{18,16},{16,... | collective-permute-start | bytes 1769480 | tf_op jit(solution)/shard_map/ppermute | solution.py:323
  58.9 1.0 %copy-start.2 = (bf16[2304,128]{1,0:T(8,128)(2,1)}, bf16[2304,128]{1,0:T(8,128)(2,1)S(1)}, u32[]{:S(2)}) copy-start(bf16[2304,128]{1,0:T(8,128)(2,1)S(1)} %collective-permute-done.10.refs_1_) | copy-start | bytes 1769476
  59.8 0.8 copy-start
  60.7 13.6 %collective-permute-start.12 = (bf16[576,128]{1,0:T(8,128)(2,1)}, bf16[576,128]{1,0:T(8,128)(2,1)}, u32[]{:S(2)}, u32[]{:S(2)}) collective-permute-start(bf16[576,128]{1,0:T(8,128)(2,1)} %get-tuple-element.21), channel_id=1, source_target_pairs={{4,0},{6,2},{0,4},{2,6},{12,8},{14,10},{8,12},{10,14},{20,16},{22,... | collective-permute-start | bytes 442376 | tf_op jit(solution)/shard_map/ppermute | solution.py:323
  62.2 0.8 copy-start.9
  63.0 13.5 %collective-permute-start.14 = (bf16[576,128]{1,0:T(8,128)(2,1)}, bf16[576,128]{1,0:T(8,128)(2,1)}, u32[]{:S(2)}, u32[]{:S(2)}) collective-permute-start(bf16[576,128]{1,0:T(8,128)(2,1)} %get-tuple-element.22), channel_id=1, source_target_pairs={{4,0},{6,2},{0,4},{2,6},{12,8},{14,10},{8,12},{10,14},{20,16},{22,... | collective-permute-start | bytes 442376 | tf_op jit(solution)/shard_map/ppermute | solution.py:323
  63.5 0.8 copy-start.11
  64.4 14.9 %collective-permute-start.16 = (bf16[576,128]{1,0:T(8,128)(2,1)}, bf16[576,128]{1,0:T(8,128)(2,1)}, u32[]{:S(2)}, u32[]{:S(2)}) collective-permute-start(bf16[576,128]{1,0:T(8,128)(2,1)} %get-tuple-element.23), channel_id=1, source_target_pairs={{4,0},{6,2},{0,4},{2,6},{12,8},{14,10},{8,12},{10,14},{20,16},{22,... | collective-permute-start | bytes 442376 | tf_op jit(solution)/shard_map/ppermute | solution.py:323
  65.9 1.1 %copy-start.1 = (bf16[2304,128]{1,0:T(8,128)(2,1)S(1)}, bf16[2304,128]{1,0:T(8,128)(2,1)}, u32[]{:S(2)}) copy-start(bf16[2304,128]{1,0:T(8,128)(2,1)} %copy-done) | copy-start | bytes 1769476
  66.9 1.1 %copy-start.3 = (bf16[2304,128]{1,0:T(8,128)(2,1)S(1)}, bf16[2304,128]{1,0:T(8,128)(2,1)}, u32[]{:S(2)}) copy-start(bf16[2304,128]{1,0:T(8,128)(2,1)} %copy-done.2) | copy-start | bytes 1769476
  68.0 1.1 %copy-start.6 = (bf16[2304,128]{1,0:T(8,128)(2,1)S(1)}, bf16[2304,128]{1,0:T(8,128)(2,1)}, u32[]{:S(2)}) copy-start(bf16[2304,128]{1,0:T(8,128)(2,1)} %copy-done.5) | copy-start | bytes 1769476
  69.1 1.1 %copy-start.8 = (bf16[2304,128]{1,0:T(8,128)(2,1)S(1)}, bf16[2304,128]{1,0:T(8,128)(2,1)}, u32[]{:S(2)}) copy-start(bf16[2304,128]{1,0:T(8,128)(2,1)} %copy-done.7) | copy-start | bytes 1769476
  70.2 1.1 %copy-start.10 = (bf16[2304,128]{1,0:T(8,128)(2,1)S(1)}, bf16[2304,128]{1,0:T(8,128)(2,1)}, u32[]{:S(2)}) copy-start(bf16[2304,128]{1,0:T(8,128)(2,1)} %copy-done.9) | copy-start | bytes 1769476
  71.2 1.1 %copy-start.12 = (bf16[2304,128]{1,0:T(8,128)(2,1)S(1)}, bf16[2304,128]{1,0:T(8,128)(2,1)}, u32[]{:S(2)}) copy-start(bf16[2304,128]{1,0:T(8,128)(2,1)} %copy-done.11) | copy-start | bytes 1769476
  73.7 16.4 %collective-permute-start.11 = (bf16[576,128]{1,0:T(8,128)(2,1)S(1)}, bf16[576,128]{1,0:T(8,128)(2,1)S(1)}, u32[]{:S(2)}, u32[]{:S(2)}) collective-permute-start(bf16[576,128]{1,0:T(8,128)(2,1)S(1)} %add_parts.5), channel_id=1, source_target_pairs={{4,0},{6,2},{0,4},{2,6},{12,8},{14,10},{8,12},{10,14},{20,16},{22,... | collective-permute-start | bytes 442376 | tf_op jit(solution)/shard_map/ppermute | solution.py:323
  75.2 14.8 %collective-permute-start.13 = (bf16[576,128]{1,0:T(8,128)(2,1)S(1)}, bf16[576,128]{1,0:T(8,128)(2,1)S(1)}, u32[]{:S(2)}, u32[]{:S(2)}) collective-permute-start(bf16[576,128]{1,0:T(8,128)(2,1)S(1)} %add_parts.7), channel_id=1, source_target_pairs={{8,0},{10,2},{12,4},{14,6},{0,8},{2,10},{4,12},{6,14},{24,16},{26,... | collective-permute-start | bytes 442376 | tf_op jit(solution)/shard_map/ppermute | solution.py:323
  77.5 13.0 %collective-permute-start.15 = (bf16[576,128]{1,0:T(8,128)(2,1)S(1)}, bf16[576,128]{1,0:T(8,128)(2,1)S(1)}, u32[]{:S(2)}, u32[]{:S(2)}) collective-permute-start(bf16[576,128]{1,0:T(8,128)(2,1)S(1)} %add_parts.8), channel_id=1, source_target_pairs={{16,0},{18,2},{20,4},{22,6},{24,8},{26,10},{28,12},{30,14},{0,16},... | collective-permute-start | bytes 442376 | tf_op jit(solution)/shard_map/ppermute | solution.py:323
  80.2 10.2 %collective-permute-start.17 = (bf16[576,128]{1,0:T(8,128)(2,1)S(1)}, bf16[576,128]{1,0:T(8,128)(2,1)S(1)}, u32[]{:S(2)}, u32[]{:S(2)}) collective-permute-start(bf16[576,128]{1,0:T(8,128)(2,1)S(1)} %add_parts.9), channel_id=1, source_target_pairs={{24,0},{26,2},{28,4},{30,6},{16,8},{18,10},{20,12},{22,14},{8,16},... | collective-permute-start | bytes 442376 | tf_op jit(solution)/shard_map/ppermute | solution.py:323
